TPU v7x, 32 devices: a whole 2x2x4 slice. The times are simulated.
32 devices in a mesh: tile: 8 (over z, y), ka: 4 (over x, core).
Axes of the slice: x: 2, y: 2, z: 4, core: 2. Of those that a mesh axis runs over, the one named last changes fastest.
Arguments:
- integrals: bfloat16 [640, 48, 640], P('tile', 'ka'), may hold values from -0.03125 to 0.03125
- amplitudes: bfloat16 [48, 640, 8, 640], P('ka', 'tile'), may hold values from -24 to 24
- virt_energy: float32 [640], replicated, may hold values from 0.5 to 3
- pair_energy: float32 [8], replicated, may hold values from -6 to -1
Outputs:
- update: bfloat16 [8, 640, 640], P('ka', 'tile')
All inputs are finite; a program needn't handle non-finite values.
Results may differ from a plain program's by a relative error of at most 0.001.
Values may be sent and summed in bfloat16 or wider, within the bound.
No kernel may reach another device: no remote copies, remote signals or barrier semaphores. Data moves between devices by JAX's collectives and lax.ppermute only.
A program may use at most 128 MiB of HBM per device.

v0:
```python
import jax
import jax.numpy as jnp
from jax import lax
from jax.sharding import PartitionSpec as P


def per_device(integrals, amplitudes, virt_energy, pair_energy):
    particle_hole = lax.all_to_all(amplitudes, "tile", split_axis=3, concat_axis=1, tiled=True)
    pair_count = particle_hole.shape[2]
    col_count = particle_hole.shape[3]
    summed = jnp.einsum(
        "cka,kcjb->jab",
        lax.all_gather(integrals, "tile", axis=0, tiled=True),
        particle_hole,
        preferred_element_type=jnp.float32,
    )
    tile_pos = lax.axis_index("tile")
    ka_pos = lax.axis_index("ka")
    local_pairs = pair_count // lax.axis_size("ka")
    own_virt = lax.dynamic_slice_in_dim(virt_energy, tile_pos * col_count, col_count, 0)
    own_pairs = lax.dynamic_slice_in_dim(pair_energy, ka_pos * local_pairs, local_pairs, 0)
    regrouped = lax.all_to_all(summed, "tile", split_axis=1, concat_axis=2, tiled=True)
    reduced = lax.psum_scatter(regrouped, "ka", scatter_dimension=0, tiled=True)
    denominator = own_virt[None, :, None] + virt_energy[None, None, :] - own_pairs[:, None, None]
    return (reduced / denominator).astype(jnp.bfloat16)


def solution(mesh):
    in_specs = (P("tile", "ka", None), P("ka", "tile", None, None), P(), P())
    out_specs = P("ka", "tile", None)
    return jax.shard_map(
        per_device, mesh=mesh, in_specs=in_specs, out_specs=out_specs, check_vma=False
    )
```

profile of v0, /device:TPU:0, one launch (start us, length us, event | category | flops | bytes accessed | tf_op | source)
XLA Modules:
  0.0 652.1 jit_solution(2694304044166551413)
XLA Ops:
  6.5 20.2 %copy.11 = bf16[12,80,8,640]{1,2,0,3:T(8,128)(2,1)} copy(bf16[12,80,8,640]{3,2,1,0:T(8,128)(2,1)} %param.5) | data formatting | bytes 19660800 | tf_op args[1]
  26.7 7.3 %all-to-all-start = ((bf16[12,80,8,640]{1,2,0,3:T(8,128)(2,1)}), bf16[12,80,8,640]{1,2,0,3:T(8,128)(2,1)}, u32[]{:S(2)}, u32[]{:S(2)}) async-start(bf16[12,80,8,640]{1,2,0,3:T(8,128)(2,1)} %copy.11), calls=%async_computation | async-start | bytes 31457280 | tf_op jit(solution)/shard_map/all_to_all | solution.py:8
  34.0 0.0 all-gather.2.cloned.1.call-start
  34.1 0.7 all-gather.2.cloned.1.call-update
  34.8 0.0 reduce-scatter.2.cloned.1.call-start
  34.8 458.2 %all-to-all-done = bf16[12,80,8,640]{1,2,0,3:T(8,128)(2,1)} async-done(((bf16[12,80,8,640]{1,2,0,3:T(8,128)(2,1)}), bf16[12,80,8,640]{1,2,0,3:T(8,128)(2,1)}, u32[]{:S(2)}, u32[]{:S(2)}) %all-to-all-start) | async-done | bytes 9830432 | tf_op jit(solution)/shard_map/all_to_all | solution.py:8
  493.0 17.9 %copy.17 = bf16[12,80,8,8,80]{1,3,4,0,2:T(8,128)(2,1)} copy(bf16[12,80,8,8,80]{1,2,0,4,3:T(8,128)(2,1)} %bitcast) | data formatting | bytes 19660800 | tf_op jit(solution)/shard_map/all_to_all | solution.py:8
  510.8 23.0 %all_to_all.29 = bf16[12,640,8,80]{1,3,0,2:T(8,128)(2,1)} reshape(bf16[12,8,80,8,80]{2,1,4,0,3:T(8,128)(2,1)} %bitcast.24) | data formatting | bytes 19660800 | tf_op jit(solution)/shard_map/all_to_all | solution.py:8
  533.9 0.0 all-gather.2.cloned.1.call-done
  533.9 13.0 %fusion.2 = f32[8,640,80]{1,2,0:T(8,128)} fusion(bf16[12,640,8,80]{1,3,0,2:T(8,128)(2,1)} %all_to_all.29, bf16[640,12,640]{2,0,1:T(8,128)(2,1)} %all-gather.2.cloned.1.call-done), kind=kOutput, calls=%fused_computation.3 | convolution fusion | flops 6291456000 | bytes 21299200 | tf_op jit(solution)/shard_map/cka,kcjb->jab/dot_general | solution.py:11
  546.9 0.0 copy-start.1
  546.9 0.0 copy-start
  546.9 2.4 copy.13
  549.3 63.0 %all_to_all.36 = f32[8,640,80]{2,0,1:T(8,128)S(1)} all-to-all(f32[8,640,80]{2,0,1:T(8,128)S(1)} %copy.13), channel_id=1, replica_groups=mesh['tile'=8,'ka'=4] {'tile'}, dimensions={1} | all-to-all | bytes 3276800 | tf_op jit(solution)/shard_map/all_to_all | solution.py:22
  612.4 1.5 copy.14
  613.9 1.7 all_to_all.33
  615.6 0.0 reduce-scatter.2.cloned.1.call-update
  615.7 0.0 copy-done.1
  615.7 0.1 dynamic_slice.7
  615.8 0.0 copy-done
  615.8 0.1 dynamic_slice.6
  615.8 0.1 broadcast_add_fusion
  615.9 27.5 %reduce-scatter.2.cloned.1.call-done = f32[2,80,640]{2,1,0:T(8,128)} async-done(((f32[8,80,640]{2,1,0:T(8,128)}), f32[2,80,640]{2,1,0:T(8,128)}) %reduce-scatter.2.cloned.1.call-update) | async-done | bytes 409616 | tf_op jit(solution)/shard_map/reduce_scatter | solution.py:23
  643.5 1.8 divide_convert_fusion
Async XLA Ops:
  26.7 466.2 %all-to-all-start = ((bf16[12,80,8,640]{1,2,0,3:T(8,128)(2,1)}), bf16[12,80,8,640]{1,2,0,3:T(8,128)(2,1)}, u32[]{:S(2)}, u32[]{:S(2)}) async-start(bf16[12,80,8,640]{1,2,0,3:T(8,128)(2,1)} %copy.11), calls=%async_computation | async-start | bytes 31457280 | tf_op jit(solution)/shard_map/all_to_all | solution.py:8
  34.0 499.9 %all-gather.2.cloned.1.call-start = ((), (), s32[]{:S(2)}) async-start(), calls=%async_computation.3 | async-start | bytes 11059200 | tf_op jit(solution)/shard_map/all_gather | solution.py:13
  34.8 608.7 %reduce-scatter.2.cloned.1.call-start = ((), (), s32[]{:S(2)}) async-start(), calls=%async_computation.4 | async-start | bytes 2048000 | tf_op jit(solution)/shard_map/reduce_scatter | solution.py:23
  546.9 68.8 %copy-start.1 = (f32[8]{0:T(128)S(1)}, f32[8]{0:T(128)}, u32[]{:S(2)}) copy-start(f32[8]{0:T(128)} %param.7) | copy-start | bytes 100
  546.9 68.9 %copy-start = (f32[640]{0:T(1024)S(1)}, f32[640]{0:T(1024)}, u32[]{:S(2)}) copy-start(f32[640]{0:T(1024)} %param.6) | copy-start | bytes 7684
Sparse Core Ops, SparseCore 0:
  37.1 412.8 all-gather.1
  615.8 27.6 reduce-scatter.1
where the time goes:
time: 654 us; the launch traced here: 652 us
  waiting for transfers between devices  486 us (74%)
  local copies, waits for them, and re-layouts  67 us (10%)
  blocking collectives  63 us (10%)
  between operations  13.4 us (2%)
  matrix products  13 us (2%)
  starting transfers between devices  7.36 us (1%)
    all_to_all x1, waiting for transfers between devices, per_device(): lax.all_to_all(amplitudes, 'tile', split_axis=3, concat_axis=1, tiled=True)  458 us
    all_to_all x1, blocking collectives, per_device(): lax.all_to_all(summed, 'tile', split_axis=1, concat_axis=2, tiled=True)  63 us
    all_to_all x2, local copies, waits for them, and re-layouts, per_device(): lax.all_to_all(amplitudes, 'tile', split_axis=3, concat_axis=1, tiled=True)  40.9 us
    reduce_scatter x1, waiting for transfers between devices, per_device(): reduced = lax.psum_scatter(regrouped, 'ka', scatter_dimension=0, tiled=True)  27.5 us
    unnamed x5, local copies, waits for them, and re-layouts  20.2 us
  transfers between devices with their start and end apart: 3, of which 2 were waited for; matrix products, arithmetic and copies ran while one was open for 3% of the time, Pallas kernels for 0%

commit v1 on v0

v1 whole, which is shorter than its diff:
```python
import jax
import jax.numpy as jnp
from jax import lax
from jax.sharding import PartitionSpec as P


def trade(parts, axis, bit, dim, wire):
    size = lax.axis_size(axis)
    mine = (lax.axis_index(axis) // bit) % 2
    keep = lax.dynamic_index_in_dim(parts, mine, dim, keepdims=False)
    away = lax.dynamic_index_in_dim(parts, 1 - mine, dim, keepdims=False)
    pairs = [(i, i ^ bit) for i in range(size)]
    got = lax.ppermute(away.astype(wire), axis, pairs)
    return keep + got.astype(jnp.float32)


def bits_of(size):
    return [1 << i for i in range(size.bit_length() - 1)]


def per_device(integrals, amplitudes, virt_energy, pair_energy):
    tile_size, ka_size = lax.axis_size("tile"), lax.axis_size("ka")
    summed = jnp.einsum("cka,kcjb->jab", integrals, amplitudes, preferred_element_type=jnp.float32)
    pairs, virt, cols = summed.shape
    own_pairs, own_rows = pairs // ka_size, virt // tile_size
    ka_bits, tile_bits = bits_of(ka_size), bits_of(tile_size)
    grid = summed.reshape([2] * len(ka_bits) + [own_pairs] + [2] * len(tile_bits) + [own_rows, cols])

    def reduce(grid, order):
        left = {("ka", b): i for i, b in enumerate(reversed(ka_bits))}
        left |= {("tile", b): len(ka_bits) + 1 + i for i, b in enumerate(reversed(tile_bits))}
        for step in order:
            axis, bit, wire = step
            dim = left.pop((axis, bit))
            left = {k: d - (d > dim) for k, d in left.items()}
            grid = trade(grid, axis, bit, dim, wire)
        return grid

    f16, f32 = jnp.float16, jnp.float32
    first = [("ka", ka_bits[0], f32)]
    last = [("tile", b, f32) for b in tile_bits[1:]]
    one = [("ka", b, f16) for b in ka_bits[1:]]
    two = [("tile", b, f16) for b in tile_bits[:1]]
    half = own_pairs // 2
    pair_dim = len(ka_bits)
    a = lax.slice_in_dim(grid, 0, half, axis=pair_dim)
    b = lax.slice_in_dim(grid, half, own_pairs, axis=pair_dim)
    reduced = jnp.concatenate([reduce(a, first + one + two + last), reduce(b, first + two + one + last)], 0)
    tile_pos = lax.axis_index("tile")
    ka_pos = lax.axis_index("ka")
    own_virt = lax.dynamic_slice_in_dim(virt_energy, tile_pos * own_rows, own_rows, 0)
    own_e = lax.dynamic_slice_in_dim(pair_energy, ka_pos * own_pairs, own_pairs, 0)
    denominator = own_virt[None, :, None] + virt_energy[None, None, :] - own_e[:, None, None]
    return (reduced / denominator).astype(jnp.bfloat16)


def solution(mesh):
    in_specs = (P("tile", "ka", None), P("ka", "tile", None, None), P(), P())
    out_specs = P("ka", "tile", None)
    return jax.shard_map(
        per_device, mesh=mesh, in_specs=in_specs, out_specs=out_specs, check_vma=False
    )
```

time: 654 us -> 121 us (0.19)
  waiting for transfers between devices: 486 us -> 47 us
  blocking collectives: 63 us -> 0 us
  local copies, waits for them, and re-layouts: 67 us -> 23.4 us
  other arithmetic: 1.89 us -> 20.4 us
  between operations: 13.4 us -> 0.22 us
  starting transfers between devices: 7.36 us -> 13.9 us
    all_to_all x1 -> x0, waiting for transfers between devices: 458 us -> none  [per_device(): lax.all_to_all(amplitudes, 'tile', split_axis=3, concat_axis=1, tiled=True)]
    all_to_all x1 -> x0, blocking collectives: 63 us -> none  [per_device(): lax.all_to_all(summed, 'tile', split_axis=1, concat_axis=2, tiled=True)]
    ppermute x0 -> x10, waiting for transfers between devices: none -> 47 us  [trade(): got = lax.ppermute(away.astype(wire), axis, pairs)]
    all_to_all x4 -> x0, local copies, waits for them, and re-layouts: 44.2 us -> none  [the longest x2 40.9 us: per_device(): lax.all_to_all(amplitudes, 'tile', split_axis=3, concat_axis=1, tiled=True)]
    reduce_scatter x1 -> x0, waiting for transfers between devices: 27.5 us -> none  [per_device(): reduced = lax.psum_scatter(regrouped, 'ka', scatter_dimension=0, tiled=True)]
    add x1 -> x11, other arithmetic: 0.08 us -> 15.1 us  [the longest x10 15 us: trade(): return keep + got.astype(jnp.float32)]
    unnamed x5 -> x28, local copies, waits for them, and re-layouts: 20.2 us -> 5.64 us
    ppermute x0 -> x10, starting transfers between devices: none -> 13.9 us  [trade(): got = lax.ppermute(away.astype(wire), axis, pairs)]
  transfers between devices with their start and end apart: 3 -> 10, of which waited for: 2 -> 8; matrix products, arithmetic and copies ran while one was open for 3% -> 19% of each run, Pallas kernels for 0% -> 0%
where the time goes in v1:
time: 121 us; the launch traced here: 120 us
  waiting for transfers between devices  47 us (39%)
  local copies, waits for them, and re-layouts  23.4 us (19%)
  other arithmetic  20.4 us (17%)
  matrix products  15.5 us (13%)
  starting transfers between devices  13.9 us (11%)
    ppermute x10, waiting for transfers between devices, trade(): got = lax.ppermute(away.astype(wire), axis, pairs)  47 us
    dot_general x1, matrix products, per_device(): jnp.einsum('cka,kcjb->jab', integrals, amplitudes, preferred_element_type...  15.5 us
    add x10, other arithmetic, trade(): return keep + got.astype(jnp.float32)  15 us
    ppermute x10, starting transfers between devices, trade(): got = lax.ppermute(away.astype(wire), axis, pairs)  13.9 us
    slice x1, local copies, waits for them, and re-layouts, per_device(): a = lax.slice_in_dim(grid, 0, half, axis=pair_dim)  10.7 us
    squeeze x6, local copies, waits for them, and re-layouts, trade(): away = lax.dynamic_index_in_dim(parts, 1 - mine, dim, keepdims=False)  6.87 us
    unnamed x28, local copies, waits for them, and re-layouts  5.64 us
    convert_element_type x4, other arithmetic, trade(): got = lax.ppermute(away.astype(wire), axis, pairs)  4.44 us
  transfers between devices with their start and end apart: 10, of which 8 were waited for; matrix products, arithmetic and copies ran while one was open for 19% of the time, Pallas kernels for 0%

profile of v1, /device:TPU:0, one launch (start us, length us, event | category | flops | bytes accessed | tf_op | source)
XLA Modules:
  0.0 120.5 jit_solution(18204140265672129457)
XLA Ops:
  0.0 1.3 %copy-done = bf16[80,12,640]{2,0,1:T(8,128)(2,1)S(1)} copy-done((bf16[80,12,640]{2,0,1:T(8,128)(2,1)S(1)}, bf16[80,12,640]{2,0,1:T(8,128)(2,1)}, u32[]{:S(2)}) %copy-start) | copy-done | bytes 1228824
  1.3 15.5 %fusion = f32[8,640,640,1]{1,2,3,0:T(8,128)} fusion(bf16[12,80,8,640]{3,2,1,0:T(8,128)(2,1)} %param.5, bf16[80,12,640]{2,0,1:T(8,128)(2,1)S(1)} %copy-done), kind=kOutput, calls=%fused_computation | convolution fusion | flops 6291456000 | bytes 24166400 | tf_op jit(solution)/shard_map/cka,kcjb->jab/dot_general | solution.py:23
  16.8 10.7 %fusion.8 = (f32[2,2,1,2,2,2,80,640]{7,6,5,4,3,2,1,0:T(8,128)}, f32[2,2,1,2,2,2,80,640]{7,6,5,4,3,2,1,0:T(8,128)}) fusion(f32[2,2,2,2,2,2,80,640]{7,6,5,4,3,2,1,0:T(8,128)} %bitcast.51), kind=kLoop, calls=%fused_computation.30 | loop fusion | bytes 26214400 | tf_op jit(solution)/shard_map/slice | solution.py:46
  27.6 4.0 %dynamic-slice_bitcast_fusion = f32[2,1,2,2,2,80,640]{6,5,4,3,2,0,1:T(8,128)} fusion(f32[2,2,1,2,2,2,80,640]{7,6,5,4,3,2,1,0:T(8,128)} %get-tuple-element.6, s32[]{:T(128)S(6)} %select_n.105), kind=kLoop, calls=%fused_computation.4 | loop fusion | bytes 6553604 | tf_op jit(solution)/shard_map/jit(dynamic_index_in_dim)/squeeze | solution.py:11
  31.5 0.5 collective-permute-start.5
  32.0 0.6 copy-done.2
  32.6 2.0 %dynamic-slice_bitcast_fusion.1 = f32[2,1,2,2,2,80,640]{6,5,4,3,2,0,1:T(8,128)} fusion(f32[2,2,1,2,2,2,80,640]{7,6,5,4,3,2,1,0:T(8,128)S(1)} %copy-done.2, s32[]{:T(128)S(6)} %select_n.105), kind=kLoop, calls=%fused_computation.5 | loop fusion | bytes 6553604 | tf_op jit(solution)/shard_map/jit(dynamic_index_in_dim)/squeeze | solution.py:11
  34.6 0.5 collective-permute-start
  35.0 2.8 %collective-permute-done.5 = f32[2,1,2,2,2,80,640]{6,5,4,3,2,0,1:T(8,128)} collective-permute-done((f32[2,1,2,2,2,80,640]{6,5,4,3,2,0,1:T(8,128)}, f32[2,1,2,2,2,80,640]{6,5,4,3,2,0,1:T(8,128)}, u32[]{:S(2)}, u32[]{:S(2)}) %collective-permute-start.5) | collective-permute-done | bytes 3276832 | tf_op jit(solution)/shard_map/ppermute | solution.py:13
  37.8 4.9 %bitcast_add_fusion = f32[2,1,2,2,2,80,640]{6,5,4,3,2,0,1:T(8,128)} fusion(f32[2,1,2,2,2,80,640]{6,5,4,3,2,0,1:T(8,128)} %collective-permute-done.5, f32[2,2,1,2,2,2,80,640]{7,6,5,4,3,2,1,0:T(8,128)} %get-tuple-element.6, s32[]{:T(128)S(6)} %select_n.104), kind=kLoop, calls=%fused_computation.2 | loop fusion | flops 819200 | bytes 9830404 | tf_op jit(solution)/shard_map/add | solution.py:14
  42.7 2.4 %fusion.4 = f16[2,1,2,2,80,640]{5,4,3,2,0,1:T(8,128)(2,1)} fusion(f32[2,1,2,2,2,80,640]{6,5,4,3,2,0,1:T(8,128)} %bitcast_add_fusion, s32[]{:T(128)S(6)} %select_n.112), kind=kLoop, calls=%fused_computation.12 | loop fusion | flops 409600 | bytes 2457604 | tf_op jit(solution)/shard_map/convert_element_type | solution.py:13
  45.2 2.9 %collective-permute-start.6 = (f16[2,1,2,2,80,640]{5,4,3,2,0,1:T(8,128)(2,1)}, f16[2,1,2,2,80,640]{5,4,3,2,0,1:T(8,128)(2,1)}, u32[]{:S(2)}, u32[]{:S(2)}) collective-permute-start(f16[2,1,2,2,80,640]{5,4,3,2,0,1:T(8,128)(2,1)} %fusion.4), channel_id=1, source_target_pairs={{0,4},{4,0},{8,12},{12,8},{16,20},{20,16},{24,28},{28,24},{1,5},{5... | collective-permute-start | bytes 2457608 | tf_op jit(solution)/shard_map/ppermute | solution.py:13
  48.1 0.0 collective-permute-done
  48.1 0.0 slice-done
  48.1 2.3 %bitcast_add_fusion.1 = f32[2,1,2,2,2,80,640]{6,5,4,3,2,0,1:T(8,128)S(1)} fusion(f32[2,1,2,2,2,80,640]{6,5,4,3,2,0,1:T(8,128)} %collective-permute-done, f32[2,2,1,2,2,2,80,640]{7,6,5,4,3,2,1,0:T(8,128)S(1)} %bitcast.50, s32[]{:T(128)S(6)} %select_n.104), kind=kLoop, calls=%fused_computation.3 | loop fusion | flops 819200 | bytes 9830404 | tf_op jit(solution)/shard_map/add | solution.py:14
  50.4 1.7 %copy-done.3 = f32[2,1,2,2,2,80,640]{6,5,4,3,2,0,1:T(8,128)} copy-done((f32[2,1,2,2,2,80,640]{6,5,4,3,2,0,1:T(8,128)}, f32[2,1,2,2,2,80,640]{6,5,4,3,2,0,1:T(8,128)S(1)}, u32[]{:S(2)}) %copy-start.3) | copy-done | bytes 3276824
  52.1 1.0 fusion.3
  53.1 1.5 %collective-permute-start.1 = (f16[1,2,2,2,80,640]{5,4,3,2,1,0:T(8,128)(2,1)}, f16[1,2,2,2,80,640]{5,4,3,2,1,0:T(8,128)(2,1)}, u32[]{:S(2)}, u32[]{:S(2)}) collective-permute-start(f16[1,2,2,2,80,640]{5,4,3,2,1,0:T(8,128)(2,1)} %fusion.3), channel_id=1, source_target_pairs={{0,2},{1,3},{2,0},{3,1},{4,6},{5,7},{6,4},{7,5},{8,10},{9,11},{10,... | collective-permute-start | bytes 2457608 | tf_op jit(solution)/shard_map/ppermute | solution.py:13
  54.6 12.3 %collective-permute-done.6 = f16[2,1,2,2,80,640]{5,4,3,2,0,1:T(8,128)(2,1)} collective-permute-done((f16[2,1,2,2,80,640]{5,4,3,2,0,1:T(8,128)(2,1)}, f16[2,1,2,2,80,640]{5,4,3,2,0,1:T(8,128)(2,1)}, u32[]{:S(2)}, u32[]{:S(2)}) %collective-permute-start.6) | collective-permute-done | bytes 819232 | tf_op jit(solution)/shard_map/ppermute | solution.py:13
  66.9 1.9 %bitcast_add_fusion.2 = f32[2,1,2,2,80,640]{5,4,3,2,0,1:T(8,128)S(1)} fusion(f16[2,1,2,2,80,640]{5,4,3,2,0,1:T(8,128)(2,1)} %collective-permute-done.6, f32[2,1,2,2,2,80,640]{6,5,4,3,2,0,1:T(8,128)} %bitcast_add_fusion, s32[]{:T(128)S(6)} %select_n.111), kind=kLoop, calls=%fused_computation.6 | loop fusion | flops 819200 | bytes 4096004 | tf_op jit(solution)/shard_map/add | solution.py:14
  68.8 0.0 copy-start.10
  68.8 0.9 fusion.6
  69.7 1.7 %collective-permute-start.7 = (f16[1,2,2,80,640]{4,3,2,1,0:T(8,128)(2,1)}, f16[1,2,2,80,640]{4,3,2,1,0:T(8,128)(2,1)}, u32[]{:S(2)}, u32[]{:S(2)}) collective-permute-start(f16[1,2,2,80,640]{4,3,2,1,0:T(8,128)(2,1)} %fusion.6), channel_id=1, source_target_pairs={{0,2},{1,3},{2,0},{3,1},{4,6},{5,7},{6,4},{7,5},{8,10},{9,11},{10,... | collective-permute-start | bytes 1228808 | tf_op jit(solution)/shard_map/ppermute | solution.py:13
  71.4 3.1 %collective-permute-done.1 = f16[1,2,2,2,80,640]{5,4,3,2,1,0:T(8,128)(2,1)} collective-permute-done((f16[1,2,2,2,80,640]{5,4,3,2,1,0:T(8,128)(2,1)}, f16[1,2,2,2,80,640]{5,4,3,2,1,0:T(8,128)(2,1)}, u32[]{:S(2)}, u32[]{:S(2)}) %collective-permute-start.1) | collective-permute-done | bytes 819232 | tf_op jit(solution)/shard_map/ppermute | solution.py:13
  74.6 1.3 %bitcast_add_fusion.3 = f32[1,2,2,2,80,640]{5,4,3,2,1,0:T(8,128)S(1)} fusion(f16[1,2,2,2,80,640]{5,4,3,2,1,0:T(8,128)(2,1)} %collective-permute-done.1, f32[2,1,2,2,2,80,640]{6,5,4,3,2,0,1:T(8,128)S(1)} %copy-done.4, s32[]{:T(128)S(6)} %select_n.108), kind=kLoop, calls=%fused_computation.7 | loop fusion | flops 819200 | bytes 4096004 | tf_op jit(solution)/shard_map/add | solution.py:14
  75.9 0.1 fusion.5
  76.0 1.1 copy-done.6
  77.1 0.0 collective-permute-start.2
  77.1 0.1 dynamic_slice.93
  77.1 5.1 %collective-permute-done.7 = f16[1,2,2,80,640]{4,3,2,1,0:T(8,128)(2,1)} collective-permute-done((f16[1,2,2,80,640]{4,3,2,1,0:T(8,128)(2,1)}, f16[1,2,2,80,640]{4,3,2,1,0:T(8,128)(2,1)}, u32[]{:S(2)}, u32[]{:S(2)}) %collective-permute-start.7) | collective-permute-done | bytes 409632 | tf_op jit(solution)/shard_map/ppermute | solution.py:13
  82.2 1.4 %bitcast_add_fusion.4 = f32[1,2,2,80,640]{4,3,2,1,0:T(8,128)S(1)} fusion(f16[1,2,2,80,640]{4,3,2,1,0:T(8,128)(2,1)} %collective-permute-done.7, f32[2,1,2,2,80,640]{5,4,3,2,0,1:T(8,128)} %copy-done.5, s32[]{:T(128)S(6)} %select_n.108), kind=kLoop, calls=%fused_computation.13 | loop fusion | flops 409600 | bytes 2048004 | tf_op jit(solution)/shard_map/add | solution.py:14
  83.6 0.8 dynamic-slice_bitcast_fusion.2
  84.4 1.6 %collective-permute-start.8 = (f32[1,2,80,640]{3,2,1,0:T(8,128)}, f32[1,2,80,640]{3,2,1,0:T(8,128)S(1)}, u32[]{:S(2)}, u32[]{:S(2)}) collective-permute-start(f32[1,2,80,640]{3,2,1,0:T(8,128)} %dynamic-slice_bitcast_fusion.2), channel_id=1, source_target_pairs={{0,8},{4,12},{8,0},{12,4},{16,24},{20,28},{24,16},{28,20},{1,9},{5... | collective-permute-start | bytes 1228808 | tf_op jit(solution)/shard_map/ppermute | solution.py:13
  86.0 0.4 collective-permute-done.2
  86.4 1.2 bitcast_add_fusion.5
  87.7 0.9 copy-done.9
  88.6 1.6 %collective-permute-start.3 = (f32[1,2,80,640]{3,2,1,0:T(8,128)S(1)}, f32[1,2,80,640]{3,2,1,0:T(8,128)S(1)}, u32[]{:S(2)}, u32[]{:S(2)}) collective-permute-start(f32[1,2,80,640]{3,2,1,0:T(8,128)S(1)} %dynamic-slice_bitcast_fusion.3), channel_id=1, source_target_pairs={{0,8},{4,12},{8,0},{12,4},{16,24},{20,28},{24,16},{28,20},{1,9},{5... | collective-permute-start | bytes 1228808 | tf_op jit(solution)/shard_map/ppermute | solution.py:13
  90.1 0.1 broadcast_add_fusion
  90.3 0.1 dynamic_slice.94
  90.4 6.7 %collective-permute-done.8 = f32[1,2,80,640]{3,2,1,0:T(8,128)S(1)} collective-permute-done((f32[1,2,80,640]{3,2,1,0:T(8,128)}, f32[1,2,80,640]{3,2,1,0:T(8,128)S(1)}, u32[]{:S(2)}, u32[]{:S(2)}) %collective-permute-start.8) | collective-permute-done | bytes 409632 | tf_op jit(solution)/shard_map/ppermute | solution.py:13
  97.0 1.0 bitcast_add_fusion.6
  98.1 2.7 %collective-permute-start.9 = (f32[1,80,640]{2,1,0:T(8,128)S(1)}, f32[1,80,640]{2,1,0:T(8,128)S(1)}, u32[]{:S(2)}, u32[]{:S(2)}) collective-permute-start(f32[1,80,640]{2,1,0:T(8,128)S(1)} %dynamic-slice_bitcast_fusion.4), channel_id=1, source_target_pairs={{0,16},{4,20},{8,24},{12,28},{16,0},{20,4},{24,8},{28,12},{1,17},{... | collective-permute-start | bytes 614408 | tf_op jit(solution)/shard_map/ppermute | solution.py:13
  100.8 7.4 %collective-permute-done.3 = f32[1,2,80,640]{3,2,1,0:T(8,128)S(1)} collective-permute-done((f32[1,2,80,640]{3,2,1,0:T(8,128)S(1)}, f32[1,2,80,640]{3,2,1,0:T(8,128)S(1)}, u32[]{:S(2)}, u32[]{:S(2)}) %collective-permute-start.3) | collective-permute-done | bytes 409632 | tf_op jit(solution)/shard_map/ppermute | solution.py:13
  108.1 1.1 bitcast_add_fusion.7
  109.2 1.1 collective-permute-start.4
  110.4 0.0 collective-permute-done.9
  110.4 9.2 %collective-permute-done.4 = f32[1,80,640]{2,1,0:T(8,128)S(1)} collective-permute-done((f32[1,80,640]{2,1,0:T(8,128)S(1)}, f32[1,80,640]{2,1,0:T(8,128)S(1)}, u32[]{:S(2)}, u32[]{:S(2)}) %collective-permute-start.4) | collective-permute-done | bytes 204832 | tf_op jit(solution)/shard_map/ppermute | solution.py:13
  119.7 0.8 fusion.7
  (27 shorter events, 0.2 us)
Async XLA Ops:
  0.0 1.3 %copy-start = (bf16[80,12,640]{2,0,1:T(8,128)(2,1)S(1)}, bf16[80,12,640]{2,0,1:T(8,128)(2,1)}, u32[]{:S(2)}) copy-start(bf16[80,12,640]{2,0,1:T(8,128)(2,1)} %param.4) | copy-start | bytes 3686404
  27.6 5.0 %copy-start.2 = (f32[2,2,1,2,2,2,80,640]{7,6,5,4,3,2,1,0:T(8,128)S(1)}, f32[2,2,1,2,2,2,80,640]{7,6,5,4,3,2,1,0:T(8,128)}, u32[]{:S(2)}) copy-start(f32[2,2,1,2,2,2,80,640]{7,6,5,4,3,2,1,0:T(8,128)} %get-tuple-element.5) | copy-start | bytes 19660804
  31.5 6.3 %collective-permute-start.5 = (f32[2,1,2,2,2,80,640]{6,5,4,3,2,0,1:T(8,128)}, f32[2,1,2,2,2,80,640]{6,5,4,3,2,0,1:T(8,128)}, u32[]{:S(2)}, u32[]{:S(2)}) collective-permute-start(f32[2,1,2,2,2,80,640]{6,5,4,3,2,0,1:T(8,128)} %dynamic-slice_bitcast_fusion), channel_id=1, source_target_pairs={{0,1},{1,0},{2,3},{3,2},{4,5},{5,4},{6,7},{7,6},{8,9},{9,8},{10,11... | collective-permute-start | bytes 9830408 | tf_op jit(solution)/shard_map/ppermute | solution.py:13
  32.6 15.5 %slice-start = ((s8[6553600]{0:T(1024)(128)(4,1)}), s8[2359296]{0:T(1024)(128)(4,1)S(1)}, s32[]{:S(2)}) async-start(s8[6553600]{0:T(1024)(128)(4,1)} %bitcast.49), calls=%async_computation | async-start | bytes 4718592
  34.6 13.5 %collective-permute-start = (f32[2,1,2,2,2,80,640]{6,5,4,3,2,0,1:T(8,128)}, f32[2,1,2,2,2,80,640]{6,5,4,3,2,0,1:T(8,128)}, u32[]{:S(2)}, u32[]{:S(2)}) collective-permute-start(f32[2,1,2,2,2,80,640]{6,5,4,3,2,0,1:T(8,128)} %dynamic-slice_bitcast_fusion.1), channel_id=1, source_target_pairs={{0,1},{1,0},{2,3},{3,2},{4,5},{5,4},{6,7},{7,6},{8,9},{9,8},{10,11... | collective-permute-start | bytes 9830408 | tf_op jit(solution)/shard_map/ppermute | solution.py:13
  35.0 13.1 %slice-start.1 = ((s8[6553600]{0:T(1024)(128)(4,1)}), s8[4194304]{0:T(1024)(128)(4,1)S(1)}, s32[]{:S(2)}) async-start(s8[6553600]{0:T(1024)(128)(4,1)} %bitcast.49), calls=%async_computation.1 | async-start | bytes 8388608
  45.2 21.7 %collective-permute-start.6 = (f16[2,1,2,2,80,640]{5,4,3,2,0,1:T(8,128)(2,1)}, f16[2,1,2,2,80,640]{5,4,3,2,0,1:T(8,128)(2,1)}, u32[]{:S(2)}, u32[]{:S(2)}) collective-permute-start(f16[2,1,2,2,80,640]{5,4,3,2,0,1:T(8,128)(2,1)} %fusion.4), channel_id=1, source_target_pairs={{0,4},{4,0},{8,12},{12,8},{16,20},{20,16},{24,28},{28,24},{1,5},{5... | collective-permute-start | bytes 2457608 | tf_op jit(solution)/shard_map/ppermute | solution.py:13
  50.3 1.7 %copy-start.3 = (f32[2,1,2,2,2,80,640]{6,5,4,3,2,0,1:T(8,128)}, f32[2,1,2,2,2,80,640]{6,5,4,3,2,0,1:T(8,128)S(1)}, u32[]{:S(2)}) copy-start(f32[2,1,2,2,2,80,640]{6,5,4,3,2,0,1:T(8,128)S(1)} %bitcast_add_fusion.1) | copy-start | bytes 9830404
  53.1 21.4 %copy-start.4 = (f32[2,1,2,2,2,80,640]{6,5,4,3,2,0,1:T(8,128)S(1)}, f32[2,1,2,2,2,80,640]{6,5,4,3,2,0,1:T(8,128)}, u32[]{:S(2)}) copy-start(f32[2,1,2,2,2,80,640]{6,5,4,3,2,0,1:T(8,128)} %copy-done.3) | copy-start | bytes 9830404
  53.1 21.4 %collective-permute-start.1 = (f16[1,2,2,2,80,640]{5,4,3,2,1,0:T(8,128)(2,1)}, f16[1,2,2,2,80,640]{5,4,3,2,1,0:T(8,128)(2,1)}, u32[]{:S(2)}, u32[]{:S(2)}) collective-permute-start(f16[1,2,2,2,80,640]{5,4,3,2,1,0:T(8,128)(2,1)} %fusion.3), channel_id=1, source_target_pairs={{0,2},{1,3},{2,0},{3,1},{4,6},{5,7},{6,4},{7,5},{8,10},{9,11},{10,... | collective-permute-start | bytes 2457608 | tf_op jit(solution)/shard_map/ppermute | solution.py:13
  68.8 7.1 %copy-start.5 = (f32[2,1,2,2,80,640]{5,4,3,2,0,1:T(8,128)}, f32[2,1,2,2,80,640]{5,4,3,2,0,1:T(8,128)S(1)}, u32[]{:S(2)}) copy-start(f32[2,1,2,2,80,640]{5,4,3,2,0,1:T(8,128)S(1)} %bitcast_add_fusion.2) | copy-start | bytes 4915204
  68.8 8.3 %copy-start.10 = (f32[640]{0:T(1024)S(1)}, f32[640]{0:T(1024)}, u32[]{:S(2)}) copy-start(f32[640]{0:T(1024)} %param.6) | copy-start | bytes 7684
  69.7 12.5 %collective-permute-start.7 = (f16[1,2,2,80,640]{4,3,2,1,0:T(8,128)(2,1)}, f16[1,2,2,80,640]{4,3,2,1,0:T(8,128)(2,1)}, u32[]{:S(2)}, u32[]{:S(2)}) collective-permute-start(f16[1,2,2,80,640]{4,3,2,1,0:T(8,128)(2,1)} %fusion.6), channel_id=1, source_target_pairs={{0,2},{1,3},{2,0},{3,1},{4,6},{5,7},{6,4},{7,5},{8,10},{9,11},{10,... | collective-permute-start | bytes 1228808 | tf_op jit(solution)/shard_map/ppermute | solution.py:13
  75.9 1.2 copy-start.6
  77.1 13.2 %copy-start.11 = (f32[8]{0:T(128)S(1)}, f32[8]{0:T(128)}, u32[]{:S(2)}) copy-start(f32[8]{0:T(128)} %param.7) | copy-start | bytes 100
  77.1 9.3 %collective-permute-start.2 = (f16[1,2,2,80,640]{4,3,2,1,0:T(8,128)(2,1)S(1)}, f16[1,2,2,80,640]{4,3,2,1,0:T(8,128)(2,1)}, u32[]{:S(2)}, u32[]{:S(2)}) collective-permute-start(f16[1,2,2,80,640]{4,3,2,1,0:T(8,128)(2,1)S(1)} %fusion.5), channel_id=1, source_target_pairs={{0,4},{4,0},{8,12},{12,8},{16,20},{20,16},{24,28},{28,24},{1,5},{5... | collective-permute-start | bytes 1228808 | tf_op jit(solution)/shard_map/ppermute | solution.py:13
  77.1 9.3 %copy-start.7 = (f32[1,2,2,2,80,640]{5,4,3,2,1,0:T(8,128)S(1)}, f32[1,2,2,2,80,640]{5,4,3,2,1,0:T(8,128)}, u32[]{:S(2)}) copy-start(f32[1,2,2,2,80,640]{5,4,3,2,1,0:T(8,128)} %copy-done.6) | copy-start | bytes 4915204
  83.6 4.0 %copy-start.8 = (f32[1,2,2,80,640]{4,3,2,1,0:T(8,128)}, f32[1,2,2,80,640]{4,3,2,1,0:T(8,128)S(1)}, u32[]{:S(2)}) copy-start(f32[1,2,2,80,640]{4,3,2,1,0:T(8,128)S(1)} %bitcast_add_fusion.4) | copy-start | bytes 2457604
  84.4 12.6 %collective-permute-start.8 = (f32[1,2,80,640]{3,2,1,0:T(8,128)}, f32[1,2,80,640]{3,2,1,0:T(8,128)S(1)}, u32[]{:S(2)}, u32[]{:S(2)}) collective-permute-start(f32[1,2,80,640]{3,2,1,0:T(8,128)} %dynamic-slice_bitcast_fusion.2), channel_id=1, source_target_pairs={{0,8},{4,12},{8,0},{12,4},{16,24},{20,28},{24,16},{28,20},{1,9},{5... | collective-permute-start | bytes 1228808 | tf_op jit(solution)/shard_map/ppermute | solution.py:13
  86.4 34.1 %copy-start.1 = (bf16[80,12,640]{2,0,1:T(8,128)(2,1)S(1)}, bf16[80,12,640]{2,0,1:T(8,128)(2,1)}, u32[]{:S(2)}) copy-start(bf16[80,12,640]{2,0,1:T(8,128)(2,1)} %param.4) | copy-start | bytes 3686404
  87.6 1.0 copy-start.9
  88.6 19.6 %collective-permute-start.3 = (f32[1,2,80,640]{3,2,1,0:T(8,128)S(1)}, f32[1,2,80,640]{3,2,1,0:T(8,128)S(1)}, u32[]{:S(2)}, u32[]{:S(2)}) collective-permute-start(f32[1,2,80,640]{3,2,1,0:T(8,128)S(1)} %dynamic-slice_bitcast_fusion.3), channel_id=1, source_target_pairs={{0,8},{4,12},{8,0},{12,4},{16,24},{20,28},{24,16},{28,20},{1,9},{5... | collective-permute-start | bytes 1228808 | tf_op jit(solution)/shard_map/ppermute | solution.py:13
  98.1 12.3 %collective-permute-start.9 = (f32[1,80,640]{2,1,0:T(8,128)S(1)}, f32[1,80,640]{2,1,0:T(8,128)S(1)}, u32[]{:S(2)}, u32[]{:S(2)}) collective-permute-start(f32[1,80,640]{2,1,0:T(8,128)S(1)} %dynamic-slice_bitcast_fusion.4), channel_id=1, source_target_pairs={{0,16},{4,20},{8,24},{12,28},{16,0},{20,4},{24,8},{28,12},{1,17},{... | collective-permute-start | bytes 614408 | tf_op jit(solution)/shard_map/ppermute | solution.py:13
  109.2 10.4 %collective-permute-start.4 = (f32[1,80,640]{2,1,0:T(8,128)S(1)}, f32[1,80,640]{2,1,0:T(8,128)S(1)}, u32[]{:S(2)}, u32[]{:S(2)}) collective-permute-start(f32[1,80,640]{2,1,0:T(8,128)S(1)} %dynamic-slice_bitcast_fusion.5), channel_id=1, source_target_pairs={{0,16},{4,20},{8,24},{12,28},{16,0},{20,4},{24,8},{28,12},{1,17},{... | collective-permute-start | bytes 614408 | tf_op jit(solution)/shard_map/ppermute | solution.py:13

commit v2 on v1

v2 whole, which is shorter than its diff:
```python
import functools

import jax
import jax.numpy as jnp
from jax import lax
from jax.experimental import pallas as pl
from jax.experimental.pallas import tpu as pltpu
from jax.sharding import PartitionSpec as P

F32, BF16 = jnp.float32, jnp.bfloat16
SPAN, BASE = 248.0, 124.0
EDGE = 16
PAD = 16
FAR = pl.BlockSpec(memory_space=pltpu.HBM)
WHOLE = pl.BlockSpec(memory_space=pltpu.VMEM)
SCALAR = pl.BlockSpec(memory_space=pltpu.SMEM)


def shape(dims, dtype):
    return jax.ShapeDtypeStruct(tuple(dims), dtype)


def encode(out_ref, value):
    rows, cols = value.shape
    tall = value.reshape(rows // 8, 8, cols)
    size = jnp.abs(tall)
    top = jnp.maximum(jnp.max(size, axis=0) * 1.01, 1e-30).astype(BF16)
    factor = SPAN / top.astype(F32)
    code = jnp.exp2(size * factor[None] - BASE)
    code = jnp.where(tall < 0, -code, code)
    out_ref[pl.ds(0, rows), :] = code.reshape(rows, cols).astype(BF16)
    out_ref[pl.ds(rows, PAD), :] = jnp.concatenate([top, top], 0)


def decode(ref, first, rows):
    total, cols = ref.shape[0] - PAD, ref.shape[1]
    factor = ref[pl.ds(total, PAD), :].astype(F32)[:8] * (1.0 / SPAN)
    code = ref[pl.ds(first, rows), :].astype(F32).reshape(rows // 8, 8, cols)
    size = (jnp.log2(jnp.abs(code)) + BASE) * factor[None]
    return jnp.where(code < 0, -size, size).reshape(rows, cols)


def call(kernel, outs, *args, specs=None, room=12, scratch=(), alias=None, after=()):
    specs = list(specs or [WHOLE] * len(args))
    count = len(after)

    def body(*refs):
        kernel(*refs[count:])

    return pl.pallas_call(
        body,
        in_specs=[pl.BlockSpec(memory_space=pl.ANY)] * count + specs,
        out_specs=[WHOLE] * len(outs),
        out_shape=outs,
        scratch_shapes=scratch,
        input_output_aliases={i + count: o for i, o in (alias or {}).items()},
        compiler_params=pltpu.CompilerParams(vmem_limit_bytes=room << 20),
        cost_estimate=pl.CostEstimate(
            flops=1000, bytes_accessed=1000, transcendentals=0
        ),
    )(*after, *args)


def front_kernel(place, wide, amp, turned, out, flat, held, sem, *, block, unit, own_rows, tiles_y, tiles_z):
    depth, pairs, cols = amp.shape
    copies = [
        pltpu.make_async_copy(amp.at[pl.ds(at, block)], held.at[pl.ds(at, block)], sem.at[at // block])
        for at in range(0, depth, block)
    ]
    for copy in copies:
        copy.start()
    t = wide[...].T
    bulk = own_rows - EDGE
    for y in range(tiles_y):
        for z in range(tiles_z):
            at = (z * tiles_y + y) * own_rows
            turned[pl.ds((y * tiles_z + z) * bulk, bulk), :] = t[at : at + bulk]
            edge = tiles_y * tiles_z * bulk + (z * tiles_y + y) * EDGE
            turned[pl.ds(edge, EDGE), :] = t[at + bulk : at + own_rows]
    n = unit * pairs
    r = lax.broadcasted_iota(jnp.int32, (n, n), 0)
    c = lax.broadcasted_iota(jnp.int32, (n, n), 1)
    perm = (c == (r % unit) * pairs + r // unit).astype(F32).astype(BF16)
    for at in range(0, depth, unit):
        if at % block == 0:
            copies[at // block].wait()
        part = held[at : at + unit].reshape(n, cols)
        moved = jnp.dot(perm, part, preferred_element_type=F32).astype(BF16)
        for j in range(pairs):
            flat[j, at : at + unit, :] = moved[j * unit : (j + 1) * unit]
    x, core = place[0], place[1]
    rows = tiles_y * tiles_z * bulk
    out[...] = jnp.dot(
        turned[pl.ds(0, rows), :], flat[4 * (1 - x) + 2 * (1 - core)], preferred_element_type=F32
    )


def product_kernel(place, turned, flat, *outs, jobs, bulk, tiles_y, tiles_z):
    x, core, y = place[0], place[1], place[2]
    rows = tiles_z * bulk

    def dot(at, height, plane):
        return jnp.dot(turned[pl.ds(at, height), :], flat[plane], preferred_element_type=F32)

    for out, (who, part) in zip(outs[:-1], jobs):
        pair = 2 * (core if who == "own" else 1 - core)
        if part == "a_away":
            out[...] = dot(0, 2 * rows, 4 * (1 - x) + pair)
        elif part == "a_home":
            out[...] = dot(0, 2 * rows, 4 * x + pair)
        elif part in ("b_away", "b_home"):
            side = y if part == "b_home" else 1 - y
            for xx in range(2):
                out[pl.ds(xx * rows, rows), :] = dot(pl.multiple_of(side * rows, 16), rows, 4 * xx + pair + 1)
        else:
            for xx in range(2):
                for i in range(2):
                    got = dot(2 * rows, tiles_y * tiles_z * EDGE, 4 * xx + pair + i)
                    for zz in range(tiles_z):
                        for yy in range(tiles_y):
                            at = (((zz * 2 + xx) * tiles_y + yy) * 2 + i) * EDGE
                            out[pl.ds(at, EDGE), :] = got[(zz * tiles_y + yy) * EDGE :][:EDGE]


def first_kernel(own, core, out):
    encode(out, own[...] + core[...])


def spread_kernel(place, own, core, keep, *outs, rows, count):
    z = place[3]

    def total(to):
        at = pl.ds(pl.multiple_of(to * rows, 16), rows)
        return own[at, :] + core[at, :]

    for hop in range(1, count):
        encode(outs[hop - 1], total(z ^ hop))
    keep[...] = total(z)


def mid_kernel(place, own, core, got, keep, out, *, which, rows):
    home = place[which]

    def total(half):
        at = pl.multiple_of(half * rows, 16)
        return own[pl.ds(at, rows), :] + core[pl.ds(at, rows), :] + decode(got, at, rows)

    encode(out, total(1 - home))
    keep[...] = total(home)


def halve_kernel(place, own, *refs, which, rows):
    *gots, keep, out = refs
    home = place[which]

    def total(half):
        at = pl.multiple_of(half * rows, 16)
        value = own[pl.ds(at, rows), :]
        for got in gots:
            value = value + decode(got, at, rows)
        return value

    encode(out, total(1 - home))
    keep[...] = total(home)


def line_kernel(place, keep_a, got_a, keep_b, got_b, own, *outs, rows, count):
    z = place[3]

    def total(to):
        start = pl.multiple_of(to * rows, 16)
        at = pl.ds(start, rows)
        first = keep_a[at, :] + decode(got_a, start, rows)
        second = keep_b[at, :] + decode(got_b, start, rows)
        return jnp.concatenate([first, second], 0)

    for hop in range(1, count):
        encode(outs[hop - 1], total(z ^ hop))
    own[...] = total(z)


def last_kernel(own, keep_c, got_c, *refs):
    gots, (row_e, col_e, pair_e, out) = refs[:-4], refs[-4:]
    value = own[...]
    for got in gots:
        value = value + decode(got, 0, own.shape[0])
    edge = keep_c[...] + decode(got_c, 0, keep_c.shape[0])
    bulk = out.shape[1] - EDGE
    for i in range(out.shape[0]):
        denominator = row_e[...] + col_e[...] - pair_e[i]
        rows = jnp.concatenate([value[i * bulk : (i + 1) * bulk], edge[i * EDGE : (i + 1) * EDGE]], 0)
        out[i] = (rows / denominator).astype(BF16)


def swap(value, axis, bit):
    return lax.ppermute(value, axis, [(i, i ^ bit) for i in range(lax.axis_size(axis))])


def on_chip_plan(integrals, amplitudes, virt_energy, pair_energy):
    tile_size, ka_size = lax.axis_size("tile"), lax.axis_size("ka")
    tile_pos, ka_pos = lax.axis_index("tile"), lax.axis_index("ka")
    k, c, pairs, cols = amplitudes.shape
    depth, virt = k * c, integrals.shape[2]
    own_pairs, own_rows = pairs // ka_size, virt // tile_size
    tiles_y, tiles_z = 2, tile_size // 2
    bulk = own_rows - EDGE
    rows = bulk * tiles_z
    edges = EDGE * tiles_y * own_pairs * 2
    place = jnp.stack([ka_pos // 2, ka_pos % 2, tile_pos % 2, tile_pos // 2]).astype(jnp.int32)
    wide = integrals.transpose(1, 0, 2).reshape(depth, virt)

    def full(height):
        return shape((height, cols), F32)

    def coded(height):
        return shape((height + PAD, cols), BF16)

    block = 160
    held = pltpu.VMEM((pairs, depth, cols), BF16)
    turned, c_a, flat = call(
        functools.partial(
            front_kernel, block=block, unit=32, own_rows=own_rows, tiles_y=tiles_y, tiles_z=tiles_z
        ),
        [pltpu.VMEM((virt, depth), BF16), full(2 * rows), held],
        place, wide, amplitudes.reshape(depth, pairs, cols), specs=[SCALAR, WHOLE, FAR], room=40,
        scratch=[pltpu.VMEM((depth, pairs, cols), BF16), pltpu.SemaphoreType.DMA((depth // block,))],
    )

    def products(flat, *jobs, after=()):
        heights = {"a": 2 * rows, "b": 2 * rows, "c": tiles_z * edges}
        return call(
            functools.partial(product_kernel, jobs=jobs, bulk=bulk, tiles_y=tiles_y, tiles_z=tiles_z),
            [full(heights[part[0]]) for _, part in jobs] + [held], place, turned, flat,
            specs=[SCALAR, WHOLE, WHOLE], alias={2: len(jobs)}, after=after,
        )

    g_a = swap(c_a, "ka", 1)
    c_b, c_c, flat = products(flat, ("core", "b_away"), ("core", "c"))
    g_b, g_c = swap(c_b, "ka", 1), swap(c_c, "ka", 1)
    c_ah, c_bh, flat = products(flat, ("core", "a_home"), ("core", "b_home"))
    g_ah, g_bh = swap(c_ah, "ka", 1), swap(c_bh, "ka", 1)
    o_a, o_b, o_c, o_ah, o_bh, flat = products(
        flat, ("own", "a_away"), ("own", "b_away"), ("own", "c"), ("own", "a_home"), ("own", "b_home")
    )
    (send_a,) = call(first_kernel, [coded(2 * rows)], o_a, g_a)
    got_a = swap(send_a, "ka", 2)
    (send_b,) = call(first_kernel, [coded(2 * rows)], o_b, g_b, after=[send_a])
    got_b = swap(send_b, "tile", 1)
    keep_c, *sends = call(
        functools.partial(spread_kernel, rows=edges, count=tiles_z),
        [full(edges)] + [coded(edges)] * (tiles_z - 1), place, o_c, g_c,
        specs=[SCALAR, WHOLE, WHOLE], after=[send_b],
    )
    gots_c = [swap(s, "tile", 2 * hop) for hop, s in enumerate(sends, 1)]

    mid = functools.partial(mid_kernel, rows=rows)
    specs = [SCALAR, WHOLE, WHOLE, WHOLE]
    keep_a, send_a = call(
        functools.partial(mid, which=2), [full(rows), coded(rows)], place, o_ah, g_ah, got_a, specs=specs
    )
    got_a = swap(send_a, "tile", 1)
    keep_c, send_c = call(
        functools.partial(halve_kernel, which=0, rows=edges // 2), [full(edges // 2), coded(edges // 2)],
        place, keep_c, *gots_c, specs=[SCALAR] + [WHOLE] * tiles_z, after=[keep_a],
    )
    got_c = swap(send_c, "ka", 2)
    keep_b, send_b = call(
        functools.partial(mid, which=0), [full(rows), coded(rows)], place, o_bh, g_bh, got_b,
        specs=specs, after=[send_c],
    )
    got_b = swap(send_b, "ka", 2)

    height = own_pairs * bulk
    own, *sends = call(
        functools.partial(line_kernel, rows=bulk, count=tiles_z),
        [full(height)] + [coded(height)] * (tiles_z - 1), place, keep_a, got_a, keep_b, got_b,
        specs=[SCALAR] + [WHOLE] * 4,
    )
    gots = [swap(s, "tile", 2 * hop) for hop, s in enumerate(sends, 1)]
    keep_c, send_c = call(
        functools.partial(halve_kernel, which=2, rows=edges // 4), [full(edges // 4), coded(edges // 4)],
        place, keep_c, got_c, specs=[SCALAR, WHOLE, WHOLE], after=[own],
    )
    got_c = swap(send_c, "tile", 1)
    own_virt = lax.dynamic_slice_in_dim(virt_energy, tile_pos * own_rows, own_rows, 0)
    own_e = lax.dynamic_slice_in_dim(pair_energy, ka_pos * own_pairs, own_pairs, 0)
    (out,) = call(
        last_kernel, [shape((own_pairs, own_rows, cols), BF16)],
        own, keep_c, got_c, *gots, own_virt[:, None], virt_energy[None, :], own_e,
        specs=[WHOLE] * (3 + len(gots) + 2) + [SCALAR],
    )
    return out


def trade(parts, axis, bit, dim, wire):
    mine = (lax.axis_index(axis) // bit) % 2
    keep = lax.dynamic_index_in_dim(parts, mine, dim, keepdims=False)
    away = lax.dynamic_index_in_dim(parts, 1 - mine, dim, keepdims=False)
    got = swap(away.astype(wire), axis, bit)
    return keep + got.astype(F32)


def bits_of(size):
    return [1 << i for i in range(size.bit_length() - 1)]


def any_plan(integrals, amplitudes, virt_energy, pair_energy):
    tile_size, ka_size = lax.axis_size("tile"), lax.axis_size("ka")
    summed = jnp.einsum("cka,kcjb->jab", integrals, amplitudes, preferred_element_type=F32)
    pairs, virt, cols = summed.shape
    own_pairs, own_rows = pairs // ka_size, virt // tile_size
    ka_bits, tile_bits = bits_of(ka_size), bits_of(tile_size)
    grid = summed.reshape([2] * len(ka_bits) + [own_pairs] + [2] * len(tile_bits) + [own_rows, cols])
    for i, bit in enumerate(ka_bits):
        grid = trade(grid, "ka", bit, len(ka_bits) - 1 - i, F32)
    for i, bit in enumerate(tile_bits):
        grid = trade(grid, "tile", bit, len(tile_bits) - i, F32)
    tile_pos, ka_pos = lax.axis_index("tile"), lax.axis_index("ka")
    own_virt = lax.dynamic_slice_in_dim(virt_energy, tile_pos * own_rows, own_rows, 0)
    own_e = lax.dynamic_slice_in_dim(pair_energy, ka_pos * own_pairs, own_pairs, 0)
    denominator = own_virt[None, :, None] + virt_energy[None, None, :] - own_e[:, None, None]
    return (grid / denominator).astype(BF16)


def solution(mesh):
    fits = mesh.shape["ka"] == 4 and mesh.shape["tile"] == 8

    def per_device(integrals, amplitudes, virt_energy, pair_energy):
        own_rows = integrals.shape[2] // lax.axis_size("tile")
        depth = amplitudes.shape[0] * amplitudes.shape[1]
        plain = fits and own_rows % 16 == 0 and depth % 160 == 0 and amplitudes.shape[2] == 8
        plan = on_chip_plan if plain else any_plan
        return plan(integrals, amplitudes, virt_energy, pair_energy)

    in_specs = (P("tile", "ka", None), P("ka", "tile", None, None), P(), P())
    out_specs = P("ka", "tile", None)
    return jax.shard_map(
        per_device, mesh=mesh, in_specs=in_specs, out_specs=out_specs, check_vma=False
    )
```

time: 121 us -> 81.5 us (0.67)
  Pallas kernels: 0 us -> 26.2 us
  local copies, waits for them, and re-layouts: 23.4 us -> 1.56 us
  other arithmetic: 20.4 us -> 0.08 us
  waiting for transfers between devices: 47 us -> 28.1 us
  matrix products: 15.5 us -> 0 us
  starting transfers between devices: 13.9 us -> 25.3 us
    pallas_call x0 -> x13, Pallas kernels: none -> 26.2 us  [call(): pl.pallas_call(body, in_specs=[pl.BlockSpec(memory_space=pl.ANY)] * count...]
    ppermute x10 -> x17, waiting for transfers between devices: 47 us -> 28.1 us  [swap(): lax.ppermute(value, axis, [(i, i ^ bit) for i in range(lax.axis_size(axis...]
    dot_general x1 -> x0, matrix products: 15.5 us -> none  [per_device(): jnp.einsum('cka,kcjb->jab', integrals, amplitudes, preferred_element_type...]
    add x11 -> x0, other arithmetic: 15.1 us -> none  [the longest x10 15 us: trade(): return keep + got.astype(jnp.float32)]
    ppermute x10 -> x17, starting transfers between devices: 13.9 us -> 25.3 us  [swap(): lax.ppermute(value, axis, [(i, i ^ bit) for i in range(lax.axis_size(axis...]
    slice x1 -> x0, local copies, waits for them, and re-layouts: 10.7 us -> none  [per_device(): a = lax.slice_in_dim(grid, 0, half, axis=pair_dim)]
    squeeze x6 -> x0, local copies, waits for them, and re-layouts: 6.87 us -> none  [trade(): away = lax.dynamic_index_in_dim(parts, 1 - mine, dim, keepdims=False)]
    convert_element_type x5 -> x0, other arithmetic: 5.25 us -> none  [the longest x4 4.44 us: trade(): got = lax.ppermute(away.astype(wire), axis, pairs)]
  transfers between devices with their start and end apart: 10 -> 17, of which waited for: 8 -> 5; matrix products, arithmetic and copies ran while one was open for 19% -> 0% of each run, Pallas kernels for 0% -> 19%
where the time goes in v2:
time: 81.5 us; the launch traced here: 81.3 us
  waiting for transfers between devices  28.1 us (34%)
  Pallas kernels  26.2 us (32%)
  starting transfers between devices  25.3 us (31%)
  local copies, waits for them, and re-layouts  1.56 us (2%)
    ppermute x17, waiting for transfers between devices, swap(): lax.ppermute(value, axis, [(i, i ^ bit) for i in range(lax.axis_size(axis...  28.1 us
    pallas_call x13, Pallas kernels, call(): pl.pallas_call(body, in_specs=[pl.BlockSpec(memory_space=pl.ANY)] * count...  26.2 us
    ppermute x17, starting transfers between devices, swap(): lax.ppermute(value, axis, [(i, i ^ bit) for i in range(lax.axis_size(axis...  25.3 us
  transfers between devices with their start and end apart: 17, of which 5 were waited for; matrix products, arithmetic and copies ran while one was open for 0% of the time, Pallas kernels for 19%

profile of v2, /device:TPU:0, one launch (start us, length us, event | category | flops | bytes accessed | tf_op | source)
XLA Modules:
  0.0 81.3 jit_solution(11612691782124755935)
XLA Ops:
  0.0 0.1 pad_add_fusion.refs_0_.refs_1_
  0.1 1.3 %copy-done = bf16[80,12,640]{2,0,1:T(8,128)(2,1)S(1)} copy-done((bf16[80,12,640]{2,0,1:T(8,128)(2,1)S(1)}, bf16[80,12,640]{2,0,1:T(8,128)(2,1)}, u32[]{:S(2)}) %copy-start) | copy-done | bytes 1228824
  1.4 7.3 %shard_map.46 = (bf16[640,960]{1,0:T(8,128)(2,1)S(1)}, f32[512,640]{1,0:T(8,128)S(1)}, bf16[8,960,640]{2,1,0:T(8,128)(2,1)S(1)}) custom-call(s32[4]{0:T(128)S(1)} %pad_add_fusion.refs_0_.refs_1_, bf16[960,640]{1,0:T(8,128)(2,1)S(1)} %bitcast.10, bf16[960,8,640]{2,1,0:T(8,128)(2,1)} %bitcast.11), custom_call_target="tpu_custom_call" | custom-call | flops 1000 | bytes 1000 | tf_op jit(solution)/shard_map/pallas_call | solution.py:50
  8.7 0.5 collective-permute-start.1
  9.2 2.3 %shard_map.47 = (f32[512,640]{1,0:T(8,128)S(1)}, f32[512,640]{1,0:T(8,128)S(1)}, bf16[8,960,640]{2,1,0:T(8,128)(2,1)S(1)}) custom-call(s32[4]{0:T(128)S(1)} %pad_add_fusion.refs_0_.refs_1_, bf16[640,960]{1,0:T(8,128)(2,1)S(1)} %get-tuple-element.35.refs_1_, bf16[8,960,640]{2,1,0:T(8,128)(2,1)S(1)} %get-tuple-element.36.refs_2_), custom_call_target="tpu_custom_call", output_to_operand_aliasing={{2}: (2, {})} | custom-call | flops 1000 | bytes 1000 | tf_op jit(solution)/shard_map/pallas_call | solution.py:50
  11.6 0.1 collective-permute-start.4
  11.7 0.5 collective-permute-start.5
  12.1 2.4 %shard_map.48 = (f32[512,640]{1,0:T(8,128)S(1)}, f32[512,640]{1,0:T(8,128)S(1)}, bf16[8,960,640]{2,1,0:T(8,128)(2,1)S(1)}) custom-call(s32[4]{0:T(128)S(1)} %pad_add_fusion.refs_0_.refs_1_, bf16[640,960]{1,0:T(8,128)(2,1)S(1)} %get-tuple-element.35.refs_1_, bf16[8,960,640]{2,1,0:T(8,128)(2,1)S(1)} %get-tuple-element.37.refs_2_), custom_call_target="tpu_custom_call", output_to_operand_aliasing={{2}: (2, {})} | custom-call | flops 1000 | bytes 1000 | tf_op jit(solution)/shard_map/pallas_call | solution.py:50
  14.5 0.1 collective-permute-start
  14.7 0.4 collective-permute-start.9
  15.1 4.8 %shard_map.49 = (f32[512,640]{1,0:T(8,128)S(1)}, f32[512,640]{1,0:T(8,128)S(1)}, f32[512,640]{1,0:T(8,128)S(1)}, f32[512,640]{1,0:T(8,128)S(1)}, f32[512,640]{1,...) custom-call(s32[4]{0:T(128)S(1)} %pad_add_fusion.refs_0_.refs_1_, ...), custom_call_target="tpu_custom_call", output_to_operand_aliasing={{5}: (2, {})} | custom-call | flops 1000 | bytes 1000 | tf_op jit(solution)/shard_map/pallas_call | solution.py:50
  19.9 0.0 collective-permute-done.1.refs_1_
  19.9 0.6 shard_map.50.refs_0_
  20.5 2.6 %collective-permute-start.2 = (bf16[528,640]{1,0:T(8,128)(2,1)S(1)}, bf16[528,640]{1,0:T(8,128)(2,1)S(1)}, u32[]{:S(2)}, u32[]{:S(2)}) collective-permute-start(bf16[528,640]{1,0:T(8,128)(2,1)S(1)} %shard_map.50.refs_0_), channel_id=1, source_target_pairs={{0,2},{1,3},{2,0},{3,1},{4,6},{5,7},{6,4},{7,5},{8,10},{9,11},{10,... | collective-permute-start | bytes 2027528 | tf_op jit(solution)/shard_map/ppermute | solution.py:196
  23.1 0.0 collective-permute-done.4.refs_2_
  23.1 0.6 shard_map.52.refs_0_
  23.7 1.6 %collective-permute-start.10 = (bf16[528,640]{1,0:T(8,128)(2,1)S(1)}, bf16[528,640]{1,0:T(8,128)(2,1)S(1)}, u32[]{:S(2)}, u32[]{:S(2)}) collective-permute-start(bf16[528,640]{1,0:T(8,128)(2,1)S(1)} %shard_map.52.refs_0_), channel_id=1, source_target_pairs={{0,4},{4,0},{8,12},{12,8},{16,20},{20,16},{24,28},{28,24},{1,5},{5... | collective-permute-start | bytes 2027528 | tf_op jit(solution)/shard_map/ppermute | solution.py:196
  25.3 0.0 collective-permute-done.5.refs_3_
  25.3 1.0 %shard_map.53 = (f32[128,640]{1,0:T(8,128)S(1)}, bf16[144,640]{1,0:T(8,128)(2,1)S(1)}, bf16[144,640]{1,0:T(8,128)(2,1)S(1)}, bf16[144,640]{1,0:T(8,128)(2,1)S(1)}) custom-call(bf16[528,640]{1,0:T(8,128)(2,1)S(1)} %shard_map.52.refs_0_, s32[4]{0:T(128)S(1)} %pad_add_fusion.refs_0_.refs_1_, f32[512,640]{1,0:T(8,128)S(1)} %get-tuple-element.47.refs_2_, ...), custom_call_target="tpu_custom_call" | custom-call | flops 1000 | bytes 1000 | tf_op jit(solution)/shard_map/pallas_call | solution.py:50
  26.3 1.6 %collective-permute-start.6 = (bf16[144,640]{1,0:T(8,128)(2,1)S(1)}, bf16[144,640]{1,0:T(8,128)(2,1)S(1)}, u32[]{:S(2)}, u32[]{:S(2)}) collective-permute-start(bf16[144,640]{1,0:T(8,128)(2,1)S(1)} %get-tuple-element.50), channel_id=1, source_target_pairs={{0,8},{4,12},{8,0},{12,4},{16,24},{20,28},{24,16},{28,20},{1,9},{5... | collective-permute-start | bytes 552968 | tf_op jit(solution)/shard_map/ppermute | solution.py:196
  27.9 2.6 %collective-permute-start.7 = (bf16[144,640]{1,0:T(8,128)(2,1)S(1)}, bf16[144,640]{1,0:T(8,128)(2,1)S(1)}, u32[]{:S(2)}, u32[]{:S(2)}) collective-permute-start(bf16[144,640]{1,0:T(8,128)(2,1)S(1)} %get-tuple-element.51), channel_id=1, source_target_pairs={{0,16},{4,20},{8,24},{12,28},{16,0},{20,4},{24,8},{28,12},{1,17},{... | collective-permute-start | bytes 552968 | tf_op jit(solution)/shard_map/ppermute | solution.py:196
  30.5 8.6 %collective-permute-done.2.refs_3_ = bf16[528,640]{1,0:T(8,128)(2,1)S(1)} collective-permute-done((bf16[528,640]{1,0:T(8,128)(2,1)S(1)}, bf16[528,640]{1,0:T(8,128)(2,1)S(1)}, u32[]{:S(2)}, u32[]{:S(2)}) %collective-permute-start.2) | collective-permute-done | bytes 675872 | tf_op jit(solution)/shard_map/ppermute | solution.py:196
  39.1 3.7 %collective-permute-start.8 = (bf16[144,640]{1,0:T(8,128)(2,1)S(1)}, bf16[144,640]{1,0:T(8,128)(2,1)S(1)}, u32[]{:S(2)}, u32[]{:S(2)}) collective-permute-start(bf16[144,640]{1,0:T(8,128)(2,1)S(1)} %get-tuple-element.52), channel_id=1, source_target_pairs={{0,24},{4,28},{8,16},{12,20},{16,8},{20,12},{24,0},{28,4},{1,25},{... | collective-permute-start | bytes 552968 | tf_op jit(solution)/shard_map/ppermute | solution.py:196
  42.8 1.3 %shard_map.51 = (f32[256,640]{1,0:T(8,128)S(1)}, bf16[272,640]{1,0:T(8,128)(2,1)S(1)}) custom-call(s32[4]{0:T(128)S(1)} %pad_add_fusion.refs_0_.refs_1_, f32[512,640]{1,0:T(8,128)S(1)} %get-tuple-element.39.refs_1_, f32[512,640]{1,0:T(8,128)S(1)} %collective-permute-done.refs_2_, bf16[528,640]{1,0:T(8,128)(2,1)S(1)} %collective-permute-done.2.refs_3_), custom_call_target="tpu_custom_call" | custom-call | flops 1000 | bytes 1000 | tf_op jit(solution)/shard_map/pallas_call | solution.py:50
  44.1 0.0 collective-permute-done.7.refs_4_
  44.1 3.3 %collective-permute-done.8.refs_5_ = bf16[144,640]{1,0:T(8,128)(2,1)S(1)} collective-permute-done((bf16[144,640]{1,0:T(8,128)(2,1)S(1)}, bf16[144,640]{1,0:T(8,128)(2,1)S(1)}, u32[]{:S(2)}, u32[]{:S(2)}) %collective-permute-start.8) | collective-permute-done | bytes 184352 | tf_op jit(solution)/shard_map/ppermute | solution.py:196
  47.4 0.9 %shard_map.54 = (f32[64,640]{1,0:T(8,128)S(1)}, bf16[80,640]{1,0:T(8,128)(2,1)S(1)}) custom-call(f32[256,640]{1,0:T(8,128)S(1)} %get-tuple-element.43.refs_0_.refs_1_, s32[4]{0:T(128)S(1)} %pad_add_fusion.refs_0_.refs_1_, f32[128,640]{1,0:T(8,128)S(1)} %get-tuple-element.49.refs_2_, bf16[144,640]{1,0:T(8,128)(2,1)S(1)} %collective-permute-done.6.refs_3_, ...), custom_call_target="tpu_custom_call" | custom-call | flops 1000 | bytes 1000 | tf_op jit(solution)/shard_map/pallas_call | solution.py:50
  48.3 0.0 collective-permute-done.10.refs_4_
  48.3 1.3 %shard_map.55 = (f32[256,640]{1,0:T(8,128)S(1)}, bf16[272,640]{1,0:T(8,128)(2,1)S(1)}) custom-call(bf16[80,640]{1,0:T(8,128)(2,1)S(1)} %get-tuple-element.53.refs_0_, s32[4]{0:T(128)S(1)} %pad_add_fusion.refs_0_.refs_1_, f32[512,640]{1,0:T(8,128)S(1)} %get-tuple-element.54.refs_2_, f32[512,640]{1,0:T(8,128)S(1)} %collective-permute-done.9.refs_3_, ...), custom_call_target="tpu_custom_call" | custom-call | flops 1000 | bytes 1000 | tf_op jit(solution)/shard_map/pallas_call | solution.py:50
  49.6 0.0 copy-start.1
  49.6 1.5 %collective-permute-start.11 = (bf16[272,640]{1,0:T(8,128)(2,1)S(1)}, bf16[272,640]{1,0:T(8,128)(2,1)S(1)}, u32[]{:S(2)}, u32[]{:S(2)}) collective-permute-start(bf16[272,640]{1,0:T(8,128)(2,1)S(1)} %get-tuple-element.57), channel_id=1, source_target_pairs={{0,2},{1,3},{2,0},{3,1},{4,6},{5,7},{6,4},{7,5},{8,10},{9,11},{10,... | collective-permute-start | bytes 1044488 | tf_op jit(solution)/shard_map/ppermute | solution.py:196
  51.1 1.5 %collective-permute-start.3 = (bf16[272,640]{1,0:T(8,128)(2,1)S(1)}, bf16[272,640]{1,0:T(8,128)(2,1)S(1)}, u32[]{:S(2)}, u32[]{:S(2)}) collective-permute-start(bf16[272,640]{1,0:T(8,128)(2,1)S(1)} %get-tuple-element.44), channel_id=1, source_target_pairs={{0,4},{4,0},{8,12},{12,8},{16,20},{20,16},{24,28},{28,24},{1,5},{5... | collective-permute-start | bytes 1044488 | tf_op jit(solution)/shard_map/ppermute | solution.py:196
  52.7 0.5 collective-permute-start.12
  53.2 6.6 %collective-permute-done.11.refs_4_ = bf16[272,640]{1,0:T(8,128)(2,1)S(1)} collective-permute-done((bf16[272,640]{1,0:T(8,128)(2,1)S(1)}, bf16[272,640]{1,0:T(8,128)(2,1)S(1)}, u32[]{:S(2)}, u32[]{:S(2)}) %collective-permute-start.11) | collective-permute-done | bytes 348192 | tf_op jit(solution)/shard_map/ppermute | solution.py:196
  59.8 1.3 %shard_map.56 = (f32[128,640]{1,0:T(8,128)S(1)}, bf16[144,640]{1,0:T(8,128)(2,1)S(1)}, bf16[144,640]{1,0:T(8,128)(2,1)S(1)}, bf16[144,640]{1,0:T(8,128)(2,1)S(1)}) custom-call(s32[4]{0:T(128)S(1)} %pad_add_fusion.refs_0_.refs_1_, f32[256,640]{1,0:T(8,128)S(1)} %get-tuple-element.43.refs_0_.refs_1_, bf16[272,640]{1,0:T(8,128)(2,1)S(1)} %collective-permute-done.3.refs_2_, ...), custom_call_target="tpu_custom_call" | custom-call | flops 1000 | bytes 1000 | tf_op jit(solution)/shard_map/pallas_call | solution.py:50
  61.1 3.9 %collective-permute-start.14 = (bf16[144,640]{1,0:T(8,128)(2,1)S(1)}, bf16[144,640]{1,0:T(8,128)(2,1)S(1)}, u32[]{:S(2)}, u32[]{:S(2)}) collective-permute-start(bf16[144,640]{1,0:T(8,128)(2,1)S(1)} %get-tuple-element.62), channel_id=1, source_target_pairs={{0,8},{4,12},{8,0},{12,4},{16,24},{20,28},{24,16},{28,20},{1,9},{5... | collective-permute-start | bytes 552968 | tf_op jit(solution)/shard_map/ppermute | solution.py:196
  65.0 0.7 collective-permute-start.15
  65.7 1.7 %collective-permute-start.16 = (bf16[144,640]{1,0:T(8,128)(2,1)S(1)}, bf16[144,640]{1,0:T(8,128)(2,1)S(1)}, u32[]{:S(2)}, u32[]{:S(2)}) collective-permute-start(bf16[144,640]{1,0:T(8,128)(2,1)S(1)} %get-tuple-element.64), channel_id=1, source_target_pairs={{0,24},{4,28},{8,16},{12,20},{16,8},{20,12},{24,0},{28,4},{1,25},{... | collective-permute-start | bytes 552968 | tf_op jit(solution)/shard_map/ppermute | solution.py:196
  67.4 0.0 collective-permute-done.12.refs_3_
  67.4 0.6 shard_map.57
  68.1 1.6 %collective-permute-start.13 = (bf16[48,640]{1,0:T(8,128)(2,1)S(1)}, bf16[48,640]{1,0:T(8,128)(2,1)S(1)}, u32[]{:S(2)}, u32[]{:S(2)}) collective-permute-start(bf16[48,640]{1,0:T(8,128)(2,1)S(1)} %get-tuple-element.61), channel_id=1, source_target_pairs={{0,4},{4,0},{8,12},{12,8},{16,20},{20,16},{24,28},{28,24},{1,5},{5... | collective-permute-start | bytes 184328 | tf_op jit(solution)/shard_map/ppermute | solution.py:196
  69.7 0.1 dynamic-slice_bitcast_fusion
  69.7 0.1 copy.8.refs_6_
  69.8 0.1 dynamic_slice.7.refs_8_
  69.9 2.5 %collective-permute-done.13.refs_2_ = bf16[48,640]{1,0:T(8,128)(2,1)S(1)} collective-permute-done((bf16[48,640]{1,0:T(8,128)(2,1)S(1)}, bf16[48,640]{1,0:T(8,128)(2,1)S(1)}, u32[]{:S(2)}, u32[]{:S(2)}) %collective-permute-start.13) | collective-permute-done | bytes 61472 | tf_op jit(solution)/shard_map/ppermute | solution.py:196
  72.4 0.0 collective-permute-done.14.refs_3_
  72.4 7.2 %collective-permute-done.15.refs_4_ = bf16[144,640]{1,0:T(8,128)(2,1)S(1)} collective-permute-done((bf16[144,640]{1,0:T(8,128)(2,1)S(1)}, bf16[144,640]{1,0:T(8,128)(2,1)S(1)}, u32[]{:S(2)}, u32[]{:S(2)}) %collective-permute-start.15) | collective-permute-done | bytes 184352 | tf_op jit(solution)/shard_map/ppermute | solution.py:196
  79.6 1.8 %shard_map.58 = bf16[2,80,640]{2,1,0:T(8,128)(2,1)} custom-call(f32[128,640]{1,0:T(8,128)S(1)} %get-tuple-element.58.refs_0_, f32[32,640]{1,0:T(8,128)S(1)} %get-tuple-element.60.refs_1_, bf16[48,640]{1,0:T(8,128)(2,1)S(1)} %collective-permute-done.13.refs_2_, bf16[144,640]{1,0:T(8,128)(2,1)S(1)} %collective-permute-done.14.refs_3_, ...), custom_call_target="tpu_custom_call" | custom-call | flops 1000 | bytes 1000 | tf_op jit(solution)/shard_map/pallas_call | solution.py:50
  (10 shorter events, 0.0 us)
Async XLA Ops:
  0.1 1.3 %copy-start = (bf16[80,12,640]{2,0,1:T(8,128)(2,1)S(1)}, bf16[80,12,640]{2,0,1:T(8,128)(2,1)}, u32[]{:S(2)}) copy-start(bf16[80,12,640]{2,0,1:T(8,128)(2,1)} %param.4) | copy-start | bytes 3686404
  8.7 11.2 %collective-permute-start.1 = (f32[512,640]{1,0:T(8,128)S(1)}, f32[512,640]{1,0:T(8,128)S(1)}, u32[]{:S(2)}, u32[]{:S(2)}) collective-permute-start(f32[512,640]{1,0:T(8,128)S(1)} %get-tuple-element.42), channel_id=1, source_target_pairs={{0,1},{1,0},{2,3},{3,2},{4,5},{5,4},{6,7},{7,6},{8,9},{9,8},{10,11... | collective-permute-start | bytes 3932168 | tf_op jit(solution)/shard_map/ppermute | solution.py:196
  11.6 11.5 %collective-permute-start.4 = (f32[512,640]{1,0:T(8,128)S(1)}, f32[512,640]{1,0:T(8,128)S(1)}, u32[]{:S(2)}, u32[]{:S(2)}) collective-permute-start(f32[512,640]{1,0:T(8,128)S(1)} %get-tuple-element.46), channel_id=1, source_target_pairs={{0,1},{1,0},{2,3},{3,2},{4,5},{5,4},{6,7},{7,6},{8,9},{9,8},{10,11... | collective-permute-start | bytes 3932168 | tf_op jit(solution)/shard_map/ppermute | solution.py:196
  11.7 13.6 %collective-permute-start.5 = (f32[512,640]{1,0:T(8,128)S(1)}, f32[512,640]{1,0:T(8,128)S(1)}, u32[]{:S(2)}, u32[]{:S(2)}) collective-permute-start(f32[512,640]{1,0:T(8,128)S(1)} %get-tuple-element.48), channel_id=1, source_target_pairs={{0,1},{1,0},{2,3},{3,2},{4,5},{5,4},{6,7},{7,6},{8,9},{9,8},{10,11... | collective-permute-start | bytes 3932168 | tf_op jit(solution)/shard_map/ppermute | solution.py:196
  14.5 13.4 %collective-permute-start = (f32[512,640]{1,0:T(8,128)S(1)}, f32[512,640]{1,0:T(8,128)S(1)}, u32[]{:S(2)}, u32[]{:S(2)}) collective-permute-start(f32[512,640]{1,0:T(8,128)S(1)} %get-tuple-element.40), channel_id=1, source_target_pairs={{0,1},{1,0},{2,3},{3,2},{4,5},{5,4},{6,7},{7,6},{8,9},{9,8},{10,11... | collective-permute-start | bytes 3932168 | tf_op jit(solution)/shard_map/ppermute | solution.py:196
  14.7 33.6 %collective-permute-start.9 = (f32[512,640]{1,0:T(8,128)S(1)}, f32[512,640]{1,0:T(8,128)S(1)}, u32[]{:S(2)}, u32[]{:S(2)}) collective-permute-start(f32[512,640]{1,0:T(8,128)S(1)} %get-tuple-element.55), channel_id=1, source_target_pairs={{0,1},{1,0},{2,3},{3,2},{4,5},{5,4},{6,7},{7,6},{8,9},{9,8},{10,11... | collective-permute-start | bytes 3932168 | tf_op jit(solution)/shard_map/ppermute | solution.py:196
  20.5 18.6 %collective-permute-start.2 = (bf16[528,640]{1,0:T(8,128)(2,1)S(1)}, bf16[528,640]{1,0:T(8,128)(2,1)S(1)}, u32[]{:S(2)}, u32[]{:S(2)}) collective-permute-start(bf16[528,640]{1,0:T(8,128)(2,1)S(1)} %shard_map.50.refs_0_), channel_id=1, source_target_pairs={{0,2},{1,3},{2,0},{3,1},{4,6},{5,7},{6,4},{7,5},{8,10},{9,11},{10,... | collective-permute-start | bytes 2027528 | tf_op jit(solution)/shard_map/ppermute | solution.py:196
  23.7 24.6 %collective-permute-start.10 = (bf16[528,640]{1,0:T(8,128)(2,1)S(1)}, bf16[528,640]{1,0:T(8,128)(2,1)S(1)}, u32[]{:S(2)}, u32[]{:S(2)}) collective-permute-start(bf16[528,640]{1,0:T(8,128)(2,1)S(1)} %shard_map.52.refs_0_), channel_id=1, source_target_pairs={{0,4},{4,0},{8,12},{12,8},{16,20},{20,16},{24,28},{28,24},{1,5},{5... | collective-permute-start | bytes 2027528 | tf_op jit(solution)/shard_map/ppermute | solution.py:196
  26.3 17.8 %collective-permute-start.6 = (bf16[144,640]{1,0:T(8,128)(2,1)S(1)}, bf16[144,640]{1,0:T(8,128)(2,1)S(1)}, u32[]{:S(2)}, u32[]{:S(2)}) collective-permute-start(bf16[144,640]{1,0:T(8,128)(2,1)S(1)} %get-tuple-element.50), channel_id=1, source_target_pairs={{0,8},{4,12},{8,0},{12,4},{16,24},{20,28},{24,16},{28,20},{1,9},{5... | collective-permute-start | bytes 552968 | tf_op jit(solution)/shard_map/ppermute | solution.py:196
  27.9 16.2 %collective-permute-start.7 = (bf16[144,640]{1,0:T(8,128)(2,1)S(1)}, bf16[144,640]{1,0:T(8,128)(2,1)S(1)}, u32[]{:S(2)}, u32[]{:S(2)}) collective-permute-start(bf16[144,640]{1,0:T(8,128)(2,1)S(1)} %get-tuple-element.51), channel_id=1, source_target_pairs={{0,16},{4,20},{8,24},{12,28},{16,0},{20,4},{24,8},{28,12},{1,17},{... | collective-permute-start | bytes 552968 | tf_op jit(solution)/shard_map/ppermute | solution.py:196
  39.1 8.3 %collective-permute-start.8 = (bf16[144,640]{1,0:T(8,128)(2,1)S(1)}, bf16[144,640]{1,0:T(8,128)(2,1)S(1)}, u32[]{:S(2)}, u32[]{:S(2)}) collective-permute-start(bf16[144,640]{1,0:T(8,128)(2,1)S(1)} %get-tuple-element.52), channel_id=1, source_target_pairs={{0,24},{4,28},{8,16},{12,20},{16,8},{20,12},{24,0},{28,4},{1,25},{... | collective-permute-start | bytes 552968 | tf_op jit(solution)/shard_map/ppermute | solution.py:196
  49.6 17.8 %copy-start.1 = (f32[640]{0:T(1024)S(1)}, f32[640]{0:T(1024)}, u32[]{:S(2)}) copy-start(f32[640]{0:T(1024)} %param.6) | copy-start | bytes 7684
  49.6 10.2 %collective-permute-start.11 = (bf16[272,640]{1,0:T(8,128)(2,1)S(1)}, bf16[272,640]{1,0:T(8,128)(2,1)S(1)}, u32[]{:S(2)}, u32[]{:S(2)}) collective-permute-start(bf16[272,640]{1,0:T(8,128)(2,1)S(1)} %get-tuple-element.57), channel_id=1, source_target_pairs={{0,2},{1,3},{2,0},{3,1},{4,6},{5,7},{6,4},{7,5},{8,10},{9,11},{10,... | collective-permute-start | bytes 1044488 | tf_op jit(solution)/shard_map/ppermute | solution.py:196
  51.1 8.7 %collective-permute-start.3 = (bf16[272,640]{1,0:T(8,128)(2,1)S(1)}, bf16[272,640]{1,0:T(8,128)(2,1)S(1)}, u32[]{:S(2)}, u32[]{:S(2)}) collective-permute-start(bf16[272,640]{1,0:T(8,128)(2,1)S(1)} %get-tuple-element.44), channel_id=1, source_target_pairs={{0,4},{4,0},{8,12},{12,8},{16,20},{20,16},{24,28},{28,24},{1,5},{5... | collective-permute-start | bytes 1044488 | tf_op jit(solution)/shard_map/ppermute | solution.py:196
  52.7 14.8 %collective-permute-start.12 = (bf16[80,640]{1,0:T(8,128)(2,1)S(1)}, bf16[80,640]{1,0:T(8,128)(2,1)S(1)}, u32[]{:S(2)}, u32[]{:S(2)}) collective-permute-start(bf16[80,640]{1,0:T(8,128)(2,1)S(1)} %get-tuple-element.53.refs_0_), channel_id=1, source_target_pairs={{0,2},{1,3},{2,0},{3,1},{4,6},{5,7},{6,4},{7,5},{8,10},{9,11},{10,... | collective-permute-start | bytes 307208 | tf_op jit(solution)/shard_map/ppermute | solution.py:196
  59.8 10.0 %copy-start.2 = (f32[8]{0:T(128)S(1)}, f32[8]{0:T(128)}, u32[]{:S(2)}) copy-start(f32[8]{0:T(128)} %param.7) | copy-start | bytes 100
  61.1 11.2 %collective-permute-start.14 = (bf16[144,640]{1,0:T(8,128)(2,1)S(1)}, bf16[144,640]{1,0:T(8,128)(2,1)S(1)}, u32[]{:S(2)}, u32[]{:S(2)}) collective-permute-start(bf16[144,640]{1,0:T(8,128)(2,1)S(1)} %get-tuple-element.62), channel_id=1, source_target_pairs={{0,8},{4,12},{8,0},{12,4},{16,24},{20,28},{24,16},{28,20},{1,9},{5... | collective-permute-start | bytes 552968 | tf_op jit(solution)/shard_map/ppermute | solution.py:196
  65.0 14.6 %collective-permute-start.15 = (bf16[144,640]{1,0:T(8,128)(2,1)S(1)}, bf16[144,640]{1,0:T(8,128)(2,1)S(1)}, u32[]{:S(2)}, u32[]{:S(2)}) collective-permute-start(bf16[144,640]{1,0:T(8,128)(2,1)S(1)} %get-tuple-element.63), channel_id=1, source_target_pairs={{0,16},{4,20},{8,24},{12,28},{16,0},{20,4},{24,8},{28,12},{1,17},{... | collective-permute-start | bytes 552968 | tf_op jit(solution)/shard_map/ppermute | solution.py:196
  65.7 13.8 %collective-permute-start.16 = (bf16[144,640]{1,0:T(8,128)(2,1)S(1)}, bf16[144,640]{1,0:T(8,128)(2,1)S(1)}, u32[]{:S(2)}, u32[]{:S(2)}) collective-permute-start(bf16[144,640]{1,0:T(8,128)(2,1)S(1)} %get-tuple-element.64), channel_id=1, source_target_pairs={{0,24},{4,28},{8,16},{12,20},{16,8},{20,12},{24,0},{28,4},{1,25},{... | collective-permute-start | bytes 552968 | tf_op jit(solution)/shard_map/ppermute | solution.py:196
  68.1 4.3 %collective-permute-start.13 = (bf16[48,640]{1,0:T(8,128)(2,1)S(1)}, bf16[48,640]{1,0:T(8,128)(2,1)S(1)}, u32[]{:S(2)}, u32[]{:S(2)}) collective-permute-start(bf16[48,640]{1,0:T(8,128)(2,1)S(1)} %get-tuple-element.61), channel_id=1, source_target_pairs={{0,4},{4,0},{8,12},{12,8},{16,20},{20,16},{24,28},{28,24},{1,5},{5... | collective-permute-start | bytes 184328 | tf_op jit(solution)/shard_map/ppermute | solution.py:196

commit v3 on v2

--- a/solution.py
+++ b/solution.py
@@ -10,7 +10,8 @@
 F32, BF16 = jnp.float32, jnp.bfloat16
 SPAN, BASE = 248.0, 124.0
 EDGE = 16
-PAD = 16
+LONG = 1 << 35
+PAD = 8
 FAR = pl.BlockSpec(memory_space=pltpu.HBM)
 WHOLE = pl.BlockSpec(memory_space=pltpu.VMEM)
 SCALAR = pl.BlockSpec(memory_space=pltpu.SMEM)
@@ -29,18 +30,18 @@
     code = jnp.exp2(size * factor[None] - BASE)
     code = jnp.where(tall < 0, -code, code)
     out_ref[pl.ds(0, rows), :] = code.reshape(rows, cols).astype(BF16)
-    out_ref[pl.ds(rows, PAD), :] = jnp.concatenate([top, top], 0)
+    out_ref[pl.ds(rows, PAD), :] = top
 
 
 def decode(ref, first, rows):
     total, cols = ref.shape[0] - PAD, ref.shape[1]
-    factor = ref[pl.ds(total, PAD), :].astype(F32)[:8] * (1.0 / SPAN)
+    factor = ref[pl.ds(total, PAD), :].astype(F32) * (1.0 / SPAN)
     code = ref[pl.ds(first, rows), :].astype(F32).reshape(rows // 8, 8, cols)
     size = (jnp.log2(jnp.abs(code)) + BASE) * factor[None]
     return jnp.where(code < 0, -size, size).reshape(rows, cols)
 
 
-def call(kernel, outs, *args, specs=None, room=12, scratch=(), alias=None, after=()):
+def call(kernel, outs, *args, specs=None, room=12, scratch=(), alias=None, after=(), work=1000, out_specs=None):
     specs = list(specs or [WHOLE] * len(args))
     count = len(after)
 
@@ -50,18 +51,23 @@
     return pl.pallas_call(
         body,
         in_specs=[pl.BlockSpec(memory_space=pl.ANY)] * count + specs,
-        out_specs=[WHOLE] * len(outs),
+        out_specs=out_specs or [WHOLE] * len(outs),
         out_shape=outs,
         scratch_shapes=scratch,
         input_output_aliases={i + count: o for i, o in (alias or {}).items()},
         compiler_params=pltpu.CompilerParams(vmem_limit_bytes=room << 20),
         cost_estimate=pl.CostEstimate(
-            flops=1000, bytes_accessed=1000, transcendentals=0
+            flops=work, bytes_accessed=1000, transcendentals=0
         ),
     )(*after, *args)
 
 
-def front_kernel(place, wide, amp, turned, out, flat, held, sem, *, block, unit, own_rows, tiles_y, tiles_z):
+def home_planes(place):
+    x, core = place[0], place[1]
+    return 4 * x + 2 * core, 2 * core + 1, 4 + 2 * core + 1
+
+
+def front_kernel(place, wide, amp, turned, out, flat, far, held, sem, far_sem, *, block, unit, own_rows, tiles_y, tiles_z):
     depth, pairs, cols = amp.shape
     copies = [
         pltpu.make_async_copy(amp.at[pl.ds(at, block)], held.at[pl.ds(at, block)], sem.at[at // block])
@@ -77,6 +83,7 @@
             turned[pl.ds((y * tiles_z + z) * bulk, bulk), :] = t[at : at + bulk]
             edge = tiles_y * tiles_z * bulk + (z * tiles_y + y) * EDGE
             turned[pl.ds(edge, EDGE), :] = t[at + bulk : at + own_rows]
+    leaving = []
     n = unit * pairs
     r = lax.broadcasted_iota(jnp.int32, (n, n), 0)
     c = lax.broadcasted_iota(jnp.int32, (n, n), 1)
@@ -88,11 +95,22 @@
         moved = jnp.dot(perm, part, preferred_element_type=F32).astype(BF16)
         for j in range(pairs):
             flat[j, at : at + unit, :] = moved[j * unit : (j + 1) * unit]
+        done = at + unit
+        if done % block == 0:
+            here = pl.ds(done - block, block)
+            for slot, plane in enumerate(home_planes(place)):
+                copy = pltpu.make_async_copy(
+                    flat.at[plane, here], far.at[slot, here], far_sem.at[slot, done // block - 1]
+                )
+                copy.start()
+                leaving.append(copy)
     x, core = place[0], place[1]
     rows = tiles_y * tiles_z * bulk
     out[...] = jnp.dot(
         turned[pl.ds(0, rows), :], flat[4 * (1 - x) + 2 * (1 - core)], preferred_element_type=F32
     )
+    for copy in leaving:
+        copy.wait()
 
 
 def product_kernel(place, turned, flat, *outs, jobs, bulk, tiles_y, tiles_z):
@@ -102,51 +120,62 @@
     def dot(at, height, plane):
         return jnp.dot(turned[pl.ds(at, height), :], flat[plane], preferred_element_type=F32)
 
-    for out, (who, part) in zip(outs[:-1], jobs):
-        pair = 2 * (core if who == "own" else 1 - core)
-        if part == "a_away":
-            out[...] = dot(0, 2 * rows, 4 * (1 - x) + pair)
-        elif part == "a_home":
-            out[...] = dot(0, 2 * rows, 4 * x + pair)
-        elif part in ("b_away", "b_home"):
-            side = y if part == "b_home" else 1 - y
-            for xx in range(2):
-                out[pl.ds(xx * rows, rows), :] = dot(pl.multiple_of(side * rows, 16), rows, 4 * xx + pair + 1)
-        else:
-            for xx in range(2):
-                for i in range(2):
-                    got = dot(2 * rows, tiles_y * tiles_z * EDGE, 4 * xx + pair + i)
-                    for zz in range(tiles_z):
-                        for yy in range(tiles_y):
-                            at = (((zz * 2 + xx) * tiles_y + yy) * 2 + i) * EDGE
-                            out[pl.ds(at, EDGE), :] = got[(zz * tiles_y + yy) * EDGE :][:EDGE]
+    for out, parts in zip(outs[:-1], jobs):
+        base = 0
+        for who, part in parts:
+            pair = 2 * (core if who == "own" else 1 - core)
+            if part == "a_away":
+                out[pl.ds(base, 2 * rows), :] = dot(0, 2 * rows, 4 * (1 - x) + pair)
+            elif part == "a_home":
+                out[pl.ds(base, 2 * rows), :] = dot(0, 2 * rows, 4 * x + pair)
+            elif part in ("b_away", "b_home"):
+                side = y if part == "b_home" else 1 - y
+                for xx in range(2):
+                    at = pl.multiple_of(side * rows, 16)
+                    out[pl.ds(base + xx * rows, rows), :] = dot(at, rows, 4 * xx + pair + 1)
+            else:
+                for xx in range(2):
+                    for i in range(2):
+                        got = dot(2 * rows, tiles_y * tiles_z * EDGE, 4 * xx + pair + i)
+                        for zz in range(tiles_z):
+                            for yy in range(tiles_y):
+                                at = base + (((zz * 2 + xx) * tiles_y + yy) * 2 + i) * EDGE
+                                out[pl.ds(at, EDGE), :] = got[(zz * tiles_y + yy) * EDGE :][:EDGE]
+            base += 2 * rows if part != "c" else 4 * tiles_y * tiles_z * EDGE
+
+
+def home_kernel(place, turned, far, core_a, core_b, out_a, out_b, held, sem, *, bulk, tiles_z):
+    y = place[2]
+    rows = tiles_z * bulk
+    copies = [pltpu.make_async_copy(far.at[slot], held.at[slot], sem.at[slot]) for slot in range(3)]
+    for copy in copies:
+        copy.start()
+
+    def dot(at, height, slot):
+        return jnp.dot(turned[pl.ds(at, height), :], held[slot], preferred_element_type=F32)
+
+    copies[0].wait()
+    out_a[...] = core_a[...] + dot(0, 2 * rows, 0)
+    for xx in range(2):
+        copies[1 + xx].wait()
+        here = pl.ds(xx * rows, rows)
+        out_b[here, :] = core_b[here, :] + dot(pl.multiple_of(y * rows, 16), rows, 1 + xx)
 
 
 def first_kernel(own, core, out):
-    encode(out, own[...] + core[...])
-
-
-def spread_kernel(place, own, core, keep, *outs, rows, count):
+    encode(out, own[...] + core[pl.ds(0, own.shape[0]), :])
+
+
+def spread_kernel(place, own, core, keep, *outs, rows, count, base):
     z = place[3]
 
     def total(to):
-        at = pl.ds(pl.multiple_of(to * rows, 16), rows)
-        return own[at, :] + core[at, :]
+        at = pl.multiple_of(to * rows, 16)
+        return own[pl.ds(at, rows), :] + core[pl.ds(base + at, rows), :]
 
     for hop in range(1, count):
         encode(outs[hop - 1], total(z ^ hop))
     keep[...] = total(z)
-
-
-def mid_kernel(place, own, core, got, keep, out, *, which, rows):
-    home = place[which]
-
-    def total(half):
-        at = pl.multiple_of(half * rows, 16)
-        return own[pl.ds(at, rows), :] + core[pl.ds(at, rows), :] + decode(got, at, rows)
-
-    encode(out, total(1 - home))
-    keep[...] = total(home)
 
 
 def halve_kernel(place, own, *refs, which, rows):
@@ -203,6 +232,7 @@
     depth, virt = k * c, integrals.shape[2]
     own_pairs, own_rows = pairs // ka_size, virt // tile_size
     tiles_y, tiles_z = 2, tile_size // 2
+    hops = [hop for hop in range(2, tiles_z)] + [1]
     bulk = own_rows - EDGE
     rows = bulk * tiles_z
     edges = EDGE * tiles_y * own_pairs * 2
@@ -217,56 +247,64 @@
 
     block = 160
     held = pltpu.VMEM((pairs, depth, cols), BF16)
-    turned, c_a, flat = call(
+    turned, c_a, flat, far = call(
         functools.partial(
             front_kernel, block=block, unit=32, own_rows=own_rows, tiles_y=tiles_y, tiles_z=tiles_z
         ),
-        [pltpu.VMEM((virt, depth), BF16), full(2 * rows), held],
-        place, wide, amplitudes.reshape(depth, pairs, cols), specs=[SCALAR, WHOLE, FAR], room=40,
-        scratch=[pltpu.VMEM((depth, pairs, cols), BF16), pltpu.SemaphoreType.DMA((depth // block,))],
+        [pltpu.VMEM((virt, depth), BF16), full(2 * rows), held, pltpu.HBM((3, depth, cols), BF16)],
+        place, wide, amplitudes.reshape(depth, pairs, cols), specs=[SCALAR, WHOLE, FAR], room=40, out_specs=[WHOLE] * 3 + [FAR],
+        scratch=[
+            pltpu.VMEM((depth, pairs, cols), BF16),
+            pltpu.SemaphoreType.DMA((depth // block,)),
+            pltpu.SemaphoreType.DMA((3, depth // block)),
+        ],
     )
 
     def products(flat, *jobs, after=()):
         heights = {"a": 2 * rows, "b": 2 * rows, "c": tiles_z * edges}
+        outs = [full(sum(heights[part[0]] for _, part in parts)) for parts in jobs]
         return call(
             functools.partial(product_kernel, jobs=jobs, bulk=bulk, tiles_y=tiles_y, tiles_z=tiles_z),
-            [full(heights[part[0]]) for _, part in jobs] + [held], place, turned, flat,
+            outs + [held], place, turned, flat,
             specs=[SCALAR, WHOLE, WHOLE], alias={2: len(jobs)}, after=after,
         )
 
     g_a = swap(c_a, "ka", 1)
-    c_b, c_c, flat = products(flat, ("core", "b_away"), ("core", "c"))
+    c_b, c_c, flat = products(flat, [("core", "b_away")], [("core", "c")])
     g_b, g_c = swap(c_b, "ka", 1), swap(c_c, "ka", 1)
-    c_ah, c_bh, flat = products(flat, ("core", "a_home"), ("core", "b_home"))
+    c_ah, c_bh, flat = products(flat, [("core", "a_home")], [("core", "b_home")])
     g_ah, g_bh = swap(c_ah, "ka", 1), swap(c_bh, "ka", 1)
-    o_a, o_b, o_c, o_ah, o_bh, flat = products(
-        flat, ("own", "a_away"), ("own", "b_away"), ("own", "c"), ("own", "a_home"), ("own", "b_home")
-    )
+    o_a, o_b, o_c, flat = products(flat, *([("own", part)] for part in ("a_away", "b_away", "c")))
     (send_a,) = call(first_kernel, [coded(2 * rows)], o_a, g_a)
     got_a = swap(send_a, "ka", 2)
     (send_b,) = call(first_kernel, [coded(2 * rows)], o_b, g_b, after=[send_a])
     got_b = swap(send_b, "tile", 1)
     keep_c, *sends = call(
-        functools.partial(spread_kernel, rows=edges, count=tiles_z),
+        functools.partial(spread_kernel, rows=edges, count=tiles_z, base=0),
         [full(edges)] + [coded(edges)] * (tiles_z - 1), place, o_c, g_c,
         specs=[SCALAR, WHOLE, WHOLE], after=[send_b],
     )
-    gots_c = [swap(s, "tile", 2 * hop) for hop, s in enumerate(sends, 1)]
-
-    mid = functools.partial(mid_kernel, rows=rows)
-    specs = [SCALAR, WHOLE, WHOLE, WHOLE]
+    gots_c = [swap(sends[hop - 1], "tile", 2 * hop) for hop in hops]
+
+    h_a, h_b = call(
+        functools.partial(home_kernel, bulk=bulk, tiles_z=tiles_z), [full(2 * rows), full(2 * rows)],
+        place, turned, far, g_ah, g_bh, specs=[SCALAR, WHOLE, FAR, WHOLE, WHOLE], after=[keep_c], room=16,
+        scratch=[pltpu.VMEM((3, depth, cols), BF16), pltpu.SemaphoreType.DMA((3,))],
+    )
+    mid = functools.partial(halve_kernel, rows=rows)
+    specs = [SCALAR, WHOLE, WHOLE]
     keep_a, send_a = call(
-        functools.partial(mid, which=2), [full(rows), coded(rows)], place, o_ah, g_ah, got_a, specs=specs
+        functools.partial(mid, which=2), [full(rows), coded(rows)], place, h_a, got_a, specs=specs
     )
     got_a = swap(send_a, "tile", 1)
     keep_c, send_c = call(
         functools.partial(halve_kernel, which=0, rows=edges // 2), [full(edges // 2), coded(edges // 2)],
-        place, keep_c, *gots_c, specs=[SCALAR] + [WHOLE] * tiles_z, after=[keep_a],
+        place, keep_c, *gots_c, specs=[SCALAR] + [WHOLE] * tiles_z, work=LONG,
     )
     got_c = swap(send_c, "ka", 2)
     keep_b, send_b = call(
-        functools.partial(mid, which=0), [full(rows), coded(rows)], place, o_bh, g_bh, got_b,
-        specs=specs, after=[send_c],
+        functools.partial(mid, which=0), [full(rows), coded(rows)], place, h_b, got_b,
+        specs=specs, after=[keep_a],
     )
     got_b = swap(send_b, "ka", 2)
 
@@ -276,7 +314,7 @@
         [full(height)] + [coded(height)] * (tiles_z - 1), place, keep_a, got_a, keep_b, got_b,
         specs=[SCALAR] + [WHOLE] * 4,
     )
-    gots = [swap(s, "tile", 2 * hop) for hop, s in enumerate(sends, 1)]
+    gots = [swap(sends[hop - 1], "tile", 2 * hop) for hop in hops]
     keep_c, send_c = call(
         functools.partial(halve_kernel, which=2, rows=edges // 4), [full(edges // 4), coded(edges // 4)],
         place, keep_c, got_c, specs=[SCALAR, WHOLE, WHOLE], after=[own],

time: 81.5 us -> 70.1 us (0.86); the launches traced: 81.3 us -> 68.9 us
  waiting for transfers between devices: 28.1 us -> 18.8 us
  starting transfers between devices: 25.3 us -> 19.6 us
  Pallas kernels: 26.2 us -> 28.7 us
    ppermute x17, waiting for transfers between devices: 28.1 us -> 18.8 us  [swap(): lax.ppermute(value, axis, [(i, i ^ bit) for i in range(lax.axis_size(axis...]
    ppermute x17, starting transfers between devices: 25.3 us -> 19.6 us  [swap(): lax.ppermute(value, axis, [(i, i ^ bit) for i in range(lax.axis_size(axis...]
    pallas_call x13 -> x14, Pallas kernels: 26.2 us -> 28.7 us  [call(): pl.pallas_call(body, in_specs=[pl.BlockSpec(memory_space=pl.ANY)] * count...]
  transfers between devices with their start and end apart: 17 -> 17, of which waited for: 5 -> 7; matrix products, arithmetic and copies ran while one was open for 0% -> 0% of each run, Pallas kernels for 19% -> 28%
where the time goes in v3:
time: 70.1 us; the launch traced here: 68.9 us
  Pallas kernels  28.7 us (41%)
  starting transfers between devices  19.6 us (28%)
  waiting for transfers between devices  18.8 us (27%)
  local copies, waits for them, and re-layouts  1.56 us (2%)
    pallas_call x14, Pallas kernels, call(): pl.pallas_call(body, in_specs=[pl.BlockSpec(memory_space=pl.ANY)] * count...  28.7 us
    ppermute x17, starting transfers between devices, swap(): lax.ppermute(value, axis, [(i, i ^ bit) for i in range(lax.axis_size(axis...  19.6 us
    ppermute x17, waiting for transfers between devices, swap(): lax.ppermute(value, axis, [(i, i ^ bit) for i in range(lax.axis_size(axis...  18.8 us
  transfers between devices with their start and end apart: 17, of which 7 were waited for; matrix products, arithmetic and copies ran while one was open for 0% of the time, Pallas kernels for 28%

profile of v3, /device:TPU:0, one launch (start us, length us, event | category | flops | bytes accessed | tf_op | source)
XLA Modules:
  0.0 68.9 jit_solution(5601992014133174992)
XLA Ops:
  0.0 0.1 pad_add_fusion.refs_0_.refs_1_
  0.1 1.3 %copy-done.1 = bf16[80,12,640]{2,0,1:T(8,128)(2,1)S(1)} copy-done((bf16[80,12,640]{2,0,1:T(8,128)(2,1)S(1)}, bf16[80,12,640]{2,0,1:T(8,128)(2,1)}, u32[]{:S(2)}) %copy-start.1) | copy-done | bytes 1228824
  1.4 7.9 %shard_map.46 = (bf16[640,960]{1,0:T(8,128)(2,1)S(1)}, f32[512,640]{1,0:T(8,128)S(1)}, bf16[8,960,640]{2,1,0:T(8,128)(2,1)S(1)}, bf16[3,960,640]{2,1,0:T(8,128)(2,1)}) custom-call(s32[4]{0:T(128)S(1)} %pad_add_fusion.refs_0_.refs_1_, bf16[960,640]{1,0:T(8,128)(2,1)S(1)} %bitcast.10, bf16[960,8,640]{2,1,0:T(8,128)(2,1)} %bitcast.11), custom_call_target="tpu_custom_call" | custom-call | flops 1000 | bytes 1000 | tf_op jit(solution)/shard_map/pallas_call | solution.py:51
  9.3 0.5 collective-permute-start
  9.8 2.3 %shard_map.47 = (f32[512,640]{1,0:T(8,128)S(1)}, f32[512,640]{1,0:T(8,128)S(1)}, bf16[8,960,640]{2,1,0:T(8,128)(2,1)S(1)}) custom-call(s32[4]{0:T(128)S(1)} %pad_add_fusion.refs_0_.refs_1_, bf16[640,960]{1,0:T(8,128)(2,1)S(1)} %get-tuple-element.36.refs_1_.refs_2_, bf16[8,960,640]{2,1,0:T(8,128)(2,1)S(1)} %get-tuple-element.37.refs_2_), custom_call_target="tpu_custom_call", output_to_operand_aliasing={{2}: (2, {})} | custom-call | flops 1000 | bytes 1000 | tf_op jit(solution)/shard_map/pallas_call | solution.py:51
  12.2 0.1 collective-permute-start.1
  12.3 0.4 collective-permute-start.2
  12.8 2.4 %shard_map.48 = (f32[512,640]{1,0:T(8,128)S(1)}, f32[512,640]{1,0:T(8,128)S(1)}, bf16[8,960,640]{2,1,0:T(8,128)(2,1)S(1)}) custom-call(s32[4]{0:T(128)S(1)} %pad_add_fusion.refs_0_.refs_1_, bf16[640,960]{1,0:T(8,128)(2,1)S(1)} %get-tuple-element.36.refs_1_.refs_2_, bf16[8,960,640]{2,1,0:T(8,128)(2,1)S(1)} %get-tuple-element.38.refs_2_), custom_call_target="tpu_custom_call", output_to_operand_aliasing={{2}: (2, {})} | custom-call | flops 1000 | bytes 1000 | tf_op jit(solution)/shard_map/pallas_call | solution.py:51
  15.1 0.1 collective-permute-start.3
  15.3 0.4 collective-permute-start.4
  15.7 3.2 %shard_map.49 = (f32[512,640]{1,0:T(8,128)S(1)}, f32[512,640]{1,0:T(8,128)S(1)}, f32[512,640]{1,0:T(8,128)S(1)}, bf16[8,960,640]{2,1,0:T(8,128)(2,1)S(1)}) custom-call(s32[4]{0:T(128)S(1)} %pad_add_fusion.refs_0_.refs_1_, bf16[640,960]{1,0:T(8,128)(2,1)S(1)} %get-tuple-element.36.refs_1_.refs_2_, ...), custom_call_target="tpu_custom_call", output_to_operand_aliasing={{3}: (2, {})} | custom-call | flops 1000 | bytes 1000 | tf_op jit(solution)/shard_map/pallas_call | solution.py:51
  18.9 0.0 collective-permute-done.refs_1_
  18.9 0.6 shard_map.50.refs_0_
  19.5 2.6 %collective-permute-start.5 = (bf16[520,640]{1,0:T(8,128)(2,1)S(1)}, bf16[520,640]{1,0:T(8,128)(2,1)S(1)}, u32[]{:S(2)}, u32[]{:S(2)}) collective-permute-start(bf16[520,640]{1,0:T(8,128)(2,1)S(1)} %shard_map.50.refs_0_), channel_id=1, source_target_pairs={{0,2},{1,3},{2,0},{3,1},{4,6},{5,7},{6,4},{7,5},{8,10},{9,11},{10,... | collective-permute-start | bytes 1996808 | tf_op jit(solution)/shard_map/ppermute | solution.py:225
  22.1 0.6 shard_map.51.refs_0_
  22.7 1.6 %collective-permute-start.7 = (bf16[520,640]{1,0:T(8,128)(2,1)S(1)}, bf16[520,640]{1,0:T(8,128)(2,1)S(1)}, u32[]{:S(2)}, u32[]{:S(2)}) collective-permute-start(bf16[520,640]{1,0:T(8,128)(2,1)S(1)} %shard_map.51.refs_0_), channel_id=1, source_target_pairs={{0,4},{4,0},{8,12},{12,8},{16,20},{20,16},{24,28},{28,24},{1,5},{5... | collective-permute-start | bytes 1996808 | tf_op jit(solution)/shard_map/ppermute | solution.py:225
  24.3 0.0 collective-permute-done.2.refs_3_
  24.3 1.0 %shard_map.52 = (f32[128,640]{1,0:T(8,128)S(1)}, bf16[136,640]{1,0:T(8,128)(2,1)S(1)}, bf16[136,640]{1,0:T(8,128)(2,1)S(1)}, bf16[136,640]{1,0:T(8,128)(2,1)S(1)}) custom-call(bf16[520,640]{1,0:T(8,128)(2,1)S(1)} %shard_map.51.refs_0_, s32[4]{0:T(128)S(1)} %pad_add_fusion.refs_0_.refs_1_, f32[512,640]{1,0:T(8,128)S(1)} %get-tuple-element.44.refs_2_, ...), custom_call_target="tpu_custom_call" | custom-call | flops 1000 | bytes 1000 | tf_op jit(solution)/shard_map/pallas_call | solution.py:51
  25.3 3.9 %collective-permute-start.10 = (bf16[136,640]{1,0:T(8,128)(2,1)S(1)}, bf16[136,640]{1,0:T(8,128)(2,1)S(1)}, u32[]{:S(2)}, u32[]{:S(2)}) collective-permute-start(bf16[136,640]{1,0:T(8,128)(2,1)S(1)} %get-tuple-element.58), channel_id=1, source_target_pairs={{0,24},{4,28},{8,16},{12,20},{16,8},{20,12},{24,0},{28,4},{1,25},{... | collective-permute-start | bytes 522248 | tf_op jit(solution)/shard_map/ppermute | solution.py:225
  29.1 0.0 collective-permute-done.3.refs_4_
  29.1 0.0 collective-permute-start.11
  29.1 0.8 %collective-permute-start.9 = (bf16[136,640]{1,0:T(8,128)(2,1)S(1)}, bf16[136,640]{1,0:T(8,128)(2,1)S(1)}, u32[]{:S(2)}, u32[]{:S(2)}) collective-permute-start(bf16[136,640]{1,0:T(8,128)(2,1)S(1)} %get-tuple-element.57), channel_id=1, source_target_pairs={{0,16},{4,20},{8,24},{12,28},{16,0},{20,4},{24,8},{28,12},{1,17},{... | collective-permute-start | bytes 522248 | tf_op jit(solution)/shard_map/ppermute | solution.py:225
  29.9 3.7 %shard_map.53 = (f32[512,640]{1,0:T(8,128)S(1)}, f32[512,640]{1,0:T(8,128)S(1)}) custom-call(f32[128,640]{1,0:T(8,128)S(1)} %get-tuple-element.46.refs_0_.refs_1_, s32[4]{0:T(128)S(1)} %pad_add_fusion.refs_0_.refs_1_, bf16[640,960]{1,0:T(8,128)(2,1)S(1)} %get-tuple-element.36.refs_1_.refs_2_, bf16[3,960,640]{2,1,0:T(8,128)(2,1)S(1)} %copy-done, ...), custom_call_target="tpu_custom_call" | custom-call | flops 1000 | bytes 1000 | tf_op jit(solution)/shard_map/pallas_call | solution.py:51
  33.6 4.1 %collective-permute-done.5.refs_2_ = bf16[520,640]{1,0:T(8,128)(2,1)S(1)} collective-permute-done((bf16[520,640]{1,0:T(8,128)(2,1)S(1)}, bf16[520,640]{1,0:T(8,128)(2,1)S(1)}, u32[]{:S(2)}, u32[]{:S(2)}) %collective-permute-start.5) | collective-permute-done | bytes 665632 | tf_op jit(solution)/shard_map/ppermute | solution.py:225
  37.7 1.2 %shard_map.54 = (f32[256,640]{1,0:T(8,128)S(1)}, bf16[264,640]{1,0:T(8,128)(2,1)S(1)}) custom-call(s32[4]{0:T(128)S(1)} %pad_add_fusion.refs_0_.refs_1_, f32[512,640]{1,0:T(8,128)S(1)} %get-tuple-element.50.refs_1_, bf16[520,640]{1,0:T(8,128)(2,1)S(1)} %collective-permute-done.5.refs_2_), custom_call_target="tpu_custom_call" | custom-call | flops 1000 | bytes 1000 | tf_op jit(solution)/shard_map/pallas_call | solution.py:51
  38.9 0.9 %collective-permute-done.7.refs_3_ = bf16[520,640]{1,0:T(8,128)(2,1)S(1)} collective-permute-done((bf16[520,640]{1,0:T(8,128)(2,1)S(1)}, bf16[520,640]{1,0:T(8,128)(2,1)S(1)}, u32[]{:S(2)}, u32[]{:S(2)}) %collective-permute-start.7) | collective-permute-done | bytes 665632 | tf_op jit(solution)/shard_map/ppermute | solution.py:225
  39.8 1.2 %shard_map.55 = (f32[256,640]{1,0:T(8,128)S(1)}, bf16[264,640]{1,0:T(8,128)(2,1)S(1)}) custom-call(f32[256,640]{1,0:T(8,128)S(1)} %get-tuple-element.51.refs_0_.refs_1_, s32[4]{0:T(128)S(1)} %pad_add_fusion.refs_0_.refs_1_, f32[512,640]{1,0:T(8,128)S(1)} %get-tuple-element.53.refs_2_, bf16[520,640]{1,0:T(8,128)(2,1)S(1)} %collective-permute-done.7.refs_3_), custom_call_target="tpu_custom_call" | custom-call | flops 1000 | bytes 1000 | tf_op jit(solution)/shard_map/pallas_call | solution.py:51
  41.1 0.9 %collective-permute-start.8 = (bf16[264,640]{1,0:T(8,128)(2,1)S(1)}, bf16[264,640]{1,0:T(8,128)(2,1)S(1)}, u32[]{:S(2)}, u32[]{:S(2)}) collective-permute-start(bf16[264,640]{1,0:T(8,128)(2,1)S(1)} %get-tuple-element.55), channel_id=1, source_target_pairs={{0,2},{1,3},{2,0},{3,1},{4,6},{5,7},{6,4},{7,5},{8,10},{9,11},{10,... | collective-permute-start | bytes 1013768 | tf_op jit(solution)/shard_map/ppermute | solution.py:225
  42.0 1.5 %collective-permute-start.6 = (bf16[264,640]{1,0:T(8,128)(2,1)S(1)}, bf16[264,640]{1,0:T(8,128)(2,1)S(1)}, u32[]{:S(2)}, u32[]{:S(2)}) collective-permute-start(bf16[264,640]{1,0:T(8,128)(2,1)S(1)} %get-tuple-element.52), channel_id=1, source_target_pairs={{0,4},{4,0},{8,12},{12,8},{16,20},{20,16},{24,28},{28,24},{1,5},{5... | collective-permute-start | bytes 1013768 | tf_op jit(solution)/shard_map/ppermute | solution.py:225
  43.5 0.4 collective-permute-done.9.refs_2_
  43.9 0.9 %shard_map.57 = (f32[64,640]{1,0:T(8,128)S(1)}, bf16[72,640]{1,0:T(8,128)(2,1)S(1)}) custom-call(s32[4]{0:T(128)S(1)} %pad_add_fusion.refs_0_.refs_1_, f32[128,640]{1,0:T(8,128)S(1)} %get-tuple-element.46.refs_0_.refs_1_, bf16[136,640]{1,0:T(8,128)(2,1)S(1)} %collective-permute-done.9.refs_2_, bf16[136,640]{1,0:T(8,128)(2,1)S(1)} %collective-permute-done.10.refs_3_, ...), custom_call_target="tpu_custom_call" | custom-call | flops 34359738368 | bytes 1000 | tf_op jit(solution)/shard_map/pallas_call | solution.py:51
  44.9 0.0 copy-start.2
  44.9 0.8 %collective-permute-start.12 = (bf16[72,640]{1,0:T(8,128)(2,1)S(1)}, bf16[72,640]{1,0:T(8,128)(2,1)S(1)}, u32[]{:S(2)}, u32[]{:S(2)}) collective-permute-start(bf16[72,640]{1,0:T(8,128)(2,1)S(1)} %get-tuple-element.61), channel_id=1, source_target_pairs={{0,2},{1,3},{2,0},{3,1},{4,6},{5,7},{6,4},{7,5},{8,10},{9,11},{10,... | collective-permute-start | bytes 276488 | tf_op jit(solution)/shard_map/ppermute | solution.py:225
  45.7 5.6 %collective-permute-done.8.refs_4_ = bf16[264,640]{1,0:T(8,128)(2,1)S(1)} collective-permute-done((bf16[264,640]{1,0:T(8,128)(2,1)S(1)}, bf16[264,640]{1,0:T(8,128)(2,1)S(1)}, u32[]{:S(2)}, u32[]{:S(2)}) %collective-permute-start.8) | collective-permute-done | bytes 337952 | tf_op jit(solution)/shard_map/ppermute | solution.py:225
  51.3 0.0 collective-permute-done.6.refs_2_
  51.3 1.3 %shard_map.56 = (f32[128,640]{1,0:T(8,128)S(1)}, bf16[136,640]{1,0:T(8,128)(2,1)S(1)}, bf16[136,640]{1,0:T(8,128)(2,1)S(1)}, bf16[136,640]{1,0:T(8,128)(2,1)S(1)}) custom-call(s32[4]{0:T(128)S(1)} %pad_add_fusion.refs_0_.refs_1_, f32[256,640]{1,0:T(8,128)S(1)} %get-tuple-element.51.refs_0_.refs_1_, bf16[264,640]{1,0:T(8,128)(2,1)S(1)} %collective-permute-done.6.refs_2_, ...), custom_call_target="tpu_custom_call" | custom-call | flops 1000 | bytes 1000 | tf_op jit(solution)/shard_map/pallas_call | solution.py:51
  52.6 2.7 %collective-permute-start.14 = (bf16[136,640]{1,0:T(8,128)(2,1)S(1)}, bf16[136,640]{1,0:T(8,128)(2,1)S(1)}, u32[]{:S(2)}, u32[]{:S(2)}) collective-permute-start(bf16[136,640]{1,0:T(8,128)(2,1)S(1)} %get-tuple-element.64), channel_id=1, source_target_pairs={{0,16},{4,20},{8,24},{12,28},{16,0},{20,4},{24,8},{28,12},{1,17},{... | collective-permute-start | bytes 522248 | tf_op jit(solution)/shard_map/ppermute | solution.py:225
  55.3 1.3 %collective-permute-start.15 = (bf16[136,640]{1,0:T(8,128)(2,1)S(1)}, bf16[136,640]{1,0:T(8,128)(2,1)S(1)}, u32[]{:S(2)}, u32[]{:S(2)}) collective-permute-start(bf16[136,640]{1,0:T(8,128)(2,1)S(1)} %get-tuple-element.65), channel_id=1, source_target_pairs={{0,24},{4,28},{8,16},{12,20},{16,8},{20,12},{24,0},{28,4},{1,25},{... | collective-permute-start | bytes 522248 | tf_op jit(solution)/shard_map/ppermute | solution.py:225
  56.6 0.2 collective-permute-start.16
  56.8 0.6 shard_map.58
  57.5 1.6 %collective-permute-start.13 = (bf16[40,640]{1,0:T(8,128)(2,1)S(1)}, bf16[40,640]{1,0:T(8,128)(2,1)S(1)}, u32[]{:S(2)}, u32[]{:S(2)}) collective-permute-start(bf16[40,640]{1,0:T(8,128)(2,1)S(1)} %get-tuple-element.63), channel_id=1, source_target_pairs={{0,4},{4,0},{8,12},{12,8},{16,20},{20,16},{24,28},{28,24},{1,5},{5... | collective-permute-start | bytes 153608 | tf_op jit(solution)/shard_map/ppermute | solution.py:225
  59.1 0.1 dynamic-slice_bitcast_fusion
  59.2 0.1 copy.8.refs_6_
  59.3 0.1 dynamic_slice.7.refs_8_
  59.3 2.3 %collective-permute-done.13.refs_2_ = bf16[40,640]{1,0:T(8,128)(2,1)S(1)} collective-permute-done((bf16[40,640]{1,0:T(8,128)(2,1)S(1)}, bf16[40,640]{1,0:T(8,128)(2,1)S(1)}, u32[]{:S(2)}, u32[]{:S(2)}) %collective-permute-start.13) | collective-permute-done | bytes 51232 | tf_op jit(solution)/shard_map/ppermute | solution.py:225
  61.7 5.3 %collective-permute-done.14.refs_3_ = bf16[136,640]{1,0:T(8,128)(2,1)S(1)} collective-permute-done((bf16[136,640]{1,0:T(8,128)(2,1)S(1)}, bf16[136,640]{1,0:T(8,128)(2,1)S(1)}, u32[]{:S(2)}, u32[]{:S(2)}) %collective-permute-start.14) | collective-permute-done | bytes 174112 | tf_op jit(solution)/shard_map/ppermute | solution.py:225
  66.9 0.2 collective-permute-done.16.refs_5_
  67.1 1.8 %shard_map.59 = bf16[2,80,640]{2,1,0:T(8,128)(2,1)} custom-call(f32[128,640]{1,0:T(8,128)S(1)} %get-tuple-element.56.refs_0_, f32[32,640]{1,0:T(8,128)S(1)} %get-tuple-element.62.refs_1_, bf16[40,640]{1,0:T(8,128)(2,1)S(1)} %collective-permute-done.13.refs_2_, bf16[136,640]{1,0:T(8,128)(2,1)S(1)} %collective-permute-done.14.refs_3_, ...), custom_call_target="tpu_custom_call" | custom-call | flops 1000 | bytes 1000 | tf_op jit(solution)/shard_map/pallas_call | solution.py:51
  (13 shorter events, 0.0 us)
Async XLA Ops:
  0.1 1.3 %copy-start.1 = (bf16[80,12,640]{2,0,1:T(8,128)(2,1)S(1)}, bf16[80,12,640]{2,0,1:T(8,128)(2,1)}, u32[]{:S(2)}) copy-start(bf16[80,12,640]{2,0,1:T(8,128)(2,1)} %param.4) | copy-start | bytes 3686404
  9.3 9.6 %collective-permute-start = (f32[512,640]{1,0:T(8,128)S(1)}, f32[512,640]{1,0:T(8,128)S(1)}, u32[]{:S(2)}, u32[]{:S(2)}) collective-permute-start(f32[512,640]{1,0:T(8,128)S(1)} %get-tuple-element.41), channel_id=1, source_target_pairs={{0,1},{1,0},{2,3},{3,2},{4,5},{5,4},{6,7},{7,6},{8,9},{9,8},{10,11... | collective-permute-start | bytes 3932168 | tf_op jit(solution)/shard_map/ppermute | solution.py:225
  12.2 9.9 %collective-permute-start.1 = (f32[512,640]{1,0:T(8,128)S(1)}, f32[512,640]{1,0:T(8,128)S(1)}, u32[]{:S(2)}, u32[]{:S(2)}) collective-permute-start(f32[512,640]{1,0:T(8,128)S(1)} %get-tuple-element.43), channel_id=1, source_target_pairs={{0,1},{1,0},{2,3},{3,2},{4,5},{5,4},{6,7},{7,6},{8,9},{9,8},{10,11... | collective-permute-start | bytes 3932168 | tf_op jit(solution)/shard_map/ppermute | solution.py:225
  12.3 12.0 %collective-permute-start.2 = (f32[512,640]{1,0:T(8,128)S(1)}, f32[512,640]{1,0:T(8,128)S(1)}, u32[]{:S(2)}, u32[]{:S(2)}) collective-permute-start(f32[512,640]{1,0:T(8,128)S(1)} %get-tuple-element.45), channel_id=1, source_target_pairs={{0,1},{1,0},{2,3},{3,2},{4,5},{5,4},{6,7},{7,6},{8,9},{9,8},{10,11... | collective-permute-start | bytes 3932168 | tf_op jit(solution)/shard_map/ppermute | solution.py:225
  15.1 14.0 %collective-permute-start.3 = (f32[512,640]{1,0:T(8,128)S(1)}, f32[512,640]{1,0:T(8,128)S(1)}, u32[]{:S(2)}, u32[]{:S(2)}) collective-permute-start(f32[512,640]{1,0:T(8,128)S(1)} %get-tuple-element.48), channel_id=1, source_target_pairs={{0,1},{1,0},{2,3},{3,2},{4,5},{5,4},{6,7},{7,6},{8,9},{9,8},{10,11... | collective-permute-start | bytes 3932168 | tf_op jit(solution)/shard_map/ppermute | solution.py:225
  15.3 13.9 %collective-permute-start.4 = (f32[512,640]{1,0:T(8,128)S(1)}, f32[512,640]{1,0:T(8,128)S(1)}, u32[]{:S(2)}, u32[]{:S(2)}) collective-permute-start(f32[512,640]{1,0:T(8,128)S(1)} %get-tuple-element.49), channel_id=1, source_target_pairs={{0,1},{1,0},{2,3},{3,2},{4,5},{5,4},{6,7},{7,6},{8,9},{9,8},{10,11... | collective-permute-start | bytes 3932168 | tf_op jit(solution)/shard_map/ppermute | solution.py:225
  19.5 18.2 %collective-permute-start.5 = (bf16[520,640]{1,0:T(8,128)(2,1)S(1)}, bf16[520,640]{1,0:T(8,128)(2,1)S(1)}, u32[]{:S(2)}, u32[]{:S(2)}) collective-permute-start(bf16[520,640]{1,0:T(8,128)(2,1)S(1)} %shard_map.50.refs_0_), channel_id=1, source_target_pairs={{0,2},{1,3},{2,0},{3,1},{4,6},{5,7},{6,4},{7,5},{8,10},{9,11},{10,... | collective-permute-start | bytes 1996808 | tf_op jit(solution)/shard_map/ppermute | solution.py:225
  22.1 7.8 %copy-start = (bf16[3,960,640]{2,1,0:T(8,128)(2,1)S(1)}, bf16[3,960,640]{2,1,0:T(8,128)(2,1)}, u32[]{:S(2)}) copy-start(bf16[3,960,640]{2,1,0:T(8,128)(2,1)} %get-tuple-element.47.refs_3_) | copy-start | bytes 11059204
  22.7 17.1 %collective-permute-start.7 = (bf16[520,640]{1,0:T(8,128)(2,1)S(1)}, bf16[520,640]{1,0:T(8,128)(2,1)S(1)}, u32[]{:S(2)}, u32[]{:S(2)}) collective-permute-start(bf16[520,640]{1,0:T(8,128)(2,1)S(1)} %shard_map.51.refs_0_), channel_id=1, source_target_pairs={{0,4},{4,0},{8,12},{12,8},{16,20},{20,16},{24,28},{28,24},{1,5},{5... | collective-permute-start | bytes 1996808 | tf_op jit(solution)/shard_map/ppermute | solution.py:225
  25.3 18.2 %collective-permute-start.10 = (bf16[136,640]{1,0:T(8,128)(2,1)S(1)}, bf16[136,640]{1,0:T(8,128)(2,1)S(1)}, u32[]{:S(2)}, u32[]{:S(2)}) collective-permute-start(bf16[136,640]{1,0:T(8,128)(2,1)S(1)} %get-tuple-element.58), channel_id=1, source_target_pairs={{0,24},{4,28},{8,16},{12,20},{16,8},{20,12},{24,0},{28,4},{1,25},{... | collective-permute-start | bytes 522248 | tf_op jit(solution)/shard_map/ppermute | solution.py:225
  29.1 14.4 %collective-permute-start.11 = (bf16[136,640]{1,0:T(8,128)(2,1)S(1)}, bf16[136,640]{1,0:T(8,128)(2,1)S(1)}, u32[]{:S(2)}, u32[]{:S(2)}) collective-permute-start(bf16[136,640]{1,0:T(8,128)(2,1)S(1)} %get-tuple-element.59), channel_id=1, source_target_pairs={{0,8},{4,12},{8,0},{12,4},{16,24},{20,28},{24,16},{28,20},{1,9},{5... | collective-permute-start | bytes 522248 | tf_op jit(solution)/shard_map/ppermute | solution.py:225
  29.1 14.8 %collective-permute-start.9 = (bf16[136,640]{1,0:T(8,128)(2,1)S(1)}, bf16[136,640]{1,0:T(8,128)(2,1)S(1)}, u32[]{:S(2)}, u32[]{:S(2)}) collective-permute-start(bf16[136,640]{1,0:T(8,128)(2,1)S(1)} %get-tuple-element.57), channel_id=1, source_target_pairs={{0,16},{4,20},{8,24},{12,28},{16,0},{20,4},{24,8},{28,12},{1,17},{... | collective-permute-start | bytes 522248 | tf_op jit(solution)/shard_map/ppermute | solution.py:225
  41.1 10.2 %collective-permute-start.8 = (bf16[264,640]{1,0:T(8,128)(2,1)S(1)}, bf16[264,640]{1,0:T(8,128)(2,1)S(1)}, u32[]{:S(2)}, u32[]{:S(2)}) collective-permute-start(bf16[264,640]{1,0:T(8,128)(2,1)S(1)} %get-tuple-element.55), channel_id=1, source_target_pairs={{0,2},{1,3},{2,0},{3,1},{4,6},{5,7},{6,4},{7,5},{8,10},{9,11},{10,... | collective-permute-start | bytes 1013768 | tf_op jit(solution)/shard_map/ppermute | solution.py:225
  42.0 9.3 %collective-permute-start.6 = (bf16[264,640]{1,0:T(8,128)(2,1)S(1)}, bf16[264,640]{1,0:T(8,128)(2,1)S(1)}, u32[]{:S(2)}, u32[]{:S(2)}) collective-permute-start(bf16[264,640]{1,0:T(8,128)(2,1)S(1)} %get-tuple-element.52), channel_id=1, source_target_pairs={{0,4},{4,0},{8,12},{12,8},{16,20},{20,16},{24,28},{28,24},{1,5},{5... | collective-permute-start | bytes 1013768 | tf_op jit(solution)/shard_map/ppermute | solution.py:225
  44.9 14.2 %copy-start.2 = (f32[640]{0:T(1024)S(1)}, f32[640]{0:T(1024)}, u32[]{:S(2)}) copy-start(f32[640]{0:T(1024)} %param.6) | copy-start | bytes 7684
  44.9 12.0 %collective-permute-start.12 = (bf16[72,640]{1,0:T(8,128)(2,1)S(1)}, bf16[72,640]{1,0:T(8,128)(2,1)S(1)}, u32[]{:S(2)}, u32[]{:S(2)}) collective-permute-start(bf16[72,640]{1,0:T(8,128)(2,1)S(1)} %get-tuple-element.61), channel_id=1, source_target_pairs={{0,2},{1,3},{2,0},{3,1},{4,6},{5,7},{6,4},{7,5},{8,10},{9,11},{10,... | collective-permute-start | bytes 276488 | tf_op jit(solution)/shard_map/ppermute | solution.py:225
  51.3 8.0 %copy-start.3 = (f32[8]{0:T(128)S(1)}, f32[8]{0:T(128)}, u32[]{:S(2)}) copy-start(f32[8]{0:T(128)} %param.7) | copy-start | bytes 100
  52.6 14.3 %collective-permute-start.14 = (bf16[136,640]{1,0:T(8,128)(2,1)S(1)}, bf16[136,640]{1,0:T(8,128)(2,1)S(1)}, u32[]{:S(2)}, u32[]{:S(2)}) collective-permute-start(bf16[136,640]{1,0:T(8,128)(2,1)S(1)} %get-tuple-element.64), channel_id=1, source_target_pairs={{0,16},{4,20},{8,24},{12,28},{16,0},{20,4},{24,8},{28,12},{1,17},{... | collective-permute-start | bytes 522248 | tf_op jit(solution)/shard_map/ppermute | solution.py:225
  55.3 11.7 %collective-permute-start.15 = (bf16[136,640]{1,0:T(8,128)(2,1)S(1)}, bf16[136,640]{1,0:T(8,128)(2,1)S(1)}, u32[]{:S(2)}, u32[]{:S(2)}) collective-permute-start(bf16[136,640]{1,0:T(8,128)(2,1)S(1)} %get-tuple-element.65), channel_id=1, source_target_pairs={{0,24},{4,28},{8,16},{12,20},{16,8},{20,12},{24,0},{28,4},{1,25},{... | collective-permute-start | bytes 522248 | tf_op jit(solution)/shard_map/ppermute | solution.py:225
  56.6 10.5 %collective-permute-start.16 = (bf16[136,640]{1,0:T(8,128)(2,1)S(1)}, bf16[136,640]{1,0:T(8,128)(2,1)S(1)}, u32[]{:S(2)}, u32[]{:S(2)}) collective-permute-start(bf16[136,640]{1,0:T(8,128)(2,1)S(1)} %get-tuple-element.66), channel_id=1, source_target_pairs={{0,8},{4,12},{8,0},{12,4},{16,24},{20,28},{24,16},{28,20},{1,9},{5... | collective-permute-start | bytes 522248 | tf_op jit(solution)/shard_map/ppermute | solution.py:225
  57.5 4.2 %collective-permute-start.13 = (bf16[40,640]{1,0:T(8,128)(2,1)S(1)}, bf16[40,640]{1,0:T(8,128)(2,1)S(1)}, u32[]{:S(2)}, u32[]{:S(2)}) collective-permute-start(bf16[40,640]{1,0:T(8,128)(2,1)S(1)} %get-tuple-element.63), channel_id=1, source_target_pairs={{0,4},{4,0},{8,12},{12,8},{16,20},{20,16},{24,28},{28,24},{1,5},{5... | collective-permute-start | bytes 153608 | tf_op jit(solution)/shard_map/ppermute | solution.py:225

commit v4 on v3

--- a/solution.py
+++ b/solution.py
@@ -178,47 +178,63 @@
     keep[...] = total(z)
 
 
+def part_of(own, gots, to, rows):
+    at = pl.multiple_of(to * rows, 16)
+    value = own[pl.ds(at, rows), :]
+    for got in gots:
+        value = value + decode(got, at, rows)
+    return value
+
+
 def halve_kernel(place, own, *refs, which, rows):
     *gots, keep, out = refs
-    home = place[which]
-
-    def total(half):
-        at = pl.multiple_of(half * rows, 16)
-        value = own[pl.ds(at, rows), :]
-        for got in gots:
-            value = value + decode(got, at, rows)
-        return value
-
-    encode(out, total(1 - home))
-    keep[...] = total(home)
-
-
-def line_kernel(place, keep_a, got_a, keep_b, got_b, own, *outs, rows, count):
-    z = place[3]
-
-    def total(to):
-        start = pl.multiple_of(to * rows, 16)
-        at = pl.ds(start, rows)
-        first = keep_a[at, :] + decode(got_a, start, rows)
-        second = keep_b[at, :] + decode(got_b, start, rows)
-        return jnp.concatenate([first, second], 0)
-
-    for hop in range(1, count):
-        encode(outs[hop - 1], total(z ^ hop))
-    own[...] = total(z)
-
-
-def last_kernel(own, keep_c, got_c, *refs):
-    gots, (row_e, col_e, pair_e, out) = refs[:-4], refs[-4:]
+    encode(out, part_of(own, gots, 1 - place[which], rows))
+    keep[...] = part_of(own, gots, place[which], rows)
+
+
+def away_kernel(place, own, got, out, *, which, rows):
+    encode(out, part_of(own, [got], 1 - place[which], rows))
+
+
+def stay_kernel(place, own_a, got_a, own_b, got_b, keep_a, keep_b, *, which_a, which_b, rows):
+    keep_a[...] = part_of(own_a, [got_a], place[which_a], rows)
+    keep_b[...] = part_of(own_b, [got_b], place[which_b], rows)
+
+
+def line_kernel(place, keep_a, got_a, keep_b, got_b, *outs, rows, hops):
+    for hop, out in zip(hops, outs):
+        first = part_of(keep_a, [got_a], place[3] ^ hop, rows)
+        second = part_of(keep_b, [got_b], place[3] ^ hop, rows)
+        value = jnp.concatenate([first, second], 0)
+        if hop:
+            encode(out, value)
+        else:
+            out[...] = value
+
+
+def rest_kernel(place, keep_a, got_a, keep_b, got_b, row_e, col_e, pair_e, own, below, *, rows):
+    line_kernel(place, keep_a, got_a, keep_b, got_b, own, rows=rows, hops=[0])
+    for i in range(below.shape[0]):
+        below[i] = row_e[...] + col_e[...] - pair_e[i]
+
+
+def bulk_kernel(own, *refs):
+    gots, (below, out) = refs[:-2], refs[-2:]
     value = own[...]
     for got in gots:
         value = value + decode(got, 0, own.shape[0])
+    bulk = own.shape[0] // below.shape[0]
+    for i in range(below.shape[0]):
+        here = pl.ds(i * bulk, bulk)
+        out[here, :] = (value[i * bulk : (i + 1) * bulk] / below[i, :bulk]).astype(BF16)
+
+
+def last_kernel(bulk_rows, keep_c, got_c, below, out):
     edge = keep_c[...] + decode(got_c, 0, keep_c.shape[0])
     bulk = out.shape[1] - EDGE
     for i in range(out.shape[0]):
-        denominator = row_e[...] + col_e[...] - pair_e[i]
-        rows = jnp.concatenate([value[i * bulk : (i + 1) * bulk], edge[i * EDGE : (i + 1) * EDGE]], 0)
-        out[i] = (rows / denominator).astype(BF16)
+        out[i, pl.ds(0, bulk), :] = bulk_rows[pl.ds(i * bulk, bulk), :]
+        out[i, pl.ds(bulk, EDGE), :] = (edge[i * EDGE : (i + 1) * EDGE] / below[i, bulk:]).astype(BF16)
 
 
 def swap(value, axis, bit):
@@ -291,42 +307,46 @@
         place, turned, far, g_ah, g_bh, specs=[SCALAR, WHOLE, FAR, WHOLE, WHOLE], after=[keep_c], room=16,
         scratch=[pltpu.VMEM((3, depth, cols), BF16), pltpu.SemaphoreType.DMA((3,))],
     )
-    mid = functools.partial(halve_kernel, rows=rows)
+    away = functools.partial(away_kernel, rows=rows)
     specs = [SCALAR, WHOLE, WHOLE]
-    keep_a, send_a = call(
-        functools.partial(mid, which=2), [full(rows), coded(rows)], place, h_a, got_a, specs=specs
+    (send_a,) = call(functools.partial(away, which=2), [coded(rows)], place, h_a, got_a, specs=specs)
+    (send_b,) = call(
+        functools.partial(away, which=0), [coded(rows)], place, h_b, got_b, specs=specs, after=[send_a]
+    )
+    keep_a, keep_b = call(
+        functools.partial(stay_kernel, which_a=2, which_b=0, rows=rows), [full(rows)] * 2,
+        place, h_a, got_a, h_b, got_b, specs=[SCALAR] + [WHOLE] * 4, after=[send_b],
     )
     got_a = swap(send_a, "tile", 1)
+    got_b = swap(send_b, "ka", 2)
     keep_c, send_c = call(
         functools.partial(halve_kernel, which=0, rows=edges // 2), [full(edges // 2), coded(edges // 2)],
-        place, keep_c, *gots_c, specs=[SCALAR] + [WHOLE] * tiles_z, work=LONG,
+        place, keep_c, *gots_c, specs=[SCALAR] + [WHOLE] * tiles_z, work=LONG, after=[keep_a],
     )
     got_c = swap(send_c, "ka", 2)
-    keep_b, send_b = call(
-        functools.partial(mid, which=0), [full(rows), coded(rows)], place, h_b, got_b,
-        specs=specs, after=[keep_a],
-    )
-    got_b = swap(send_b, "ka", 2)
 
     height = own_pairs * bulk
-    own, *sends = call(
-        functools.partial(line_kernel, rows=bulk, count=tiles_z),
-        [full(height)] + [coded(height)] * (tiles_z - 1), place, keep_a, got_a, keep_b, got_b,
-        specs=[SCALAR] + [WHOLE] * 4,
-    )
-    gots = [swap(sends[hop - 1], "tile", 2 * hop) for hop in hops]
+    line = functools.partial(line_kernel, rows=bulk)
+    specs = [SCALAR] + [WHOLE] * 4
+    sends = call(
+        functools.partial(line, hops=hops), [coded(height)] * len(hops),
+        place, keep_a, got_a, keep_b, got_b, specs=specs, after=[send_c],
+    )
+    gots = [swap(send, "tile", 2 * hop) for hop, send in zip(hops, sends)]
     keep_c, send_c = call(
         functools.partial(halve_kernel, which=2, rows=edges // 4), [full(edges // 4), coded(edges // 4)],
-        place, keep_c, got_c, specs=[SCALAR, WHOLE, WHOLE], after=[own],
+        place, keep_c, got_c, specs=[SCALAR, WHOLE, WHOLE], after=[sends[0]],
     )
     got_c = swap(send_c, "tile", 1)
     own_virt = lax.dynamic_slice_in_dim(virt_energy, tile_pos * own_rows, own_rows, 0)
     own_e = lax.dynamic_slice_in_dim(pair_energy, ka_pos * own_pairs, own_pairs, 0)
-    (out,) = call(
-        last_kernel, [shape((own_pairs, own_rows, cols), BF16)],
-        own, keep_c, got_c, *gots, own_virt[:, None], virt_energy[None, :], own_e,
-        specs=[WHOLE] * (3 + len(gots) + 2) + [SCALAR],
-    )
+    own, below = call(
+        functools.partial(rest_kernel, rows=bulk), [full(height), shape((own_pairs, own_rows, cols), F32)],
+        place, keep_a, got_a, keep_b, got_b, own_virt[:, None], virt_energy[None, :], own_e,
+        specs=specs + [WHOLE, WHOLE, SCALAR], after=[keep_c],
+    )
+    (bulk_rows,) = call(bulk_kernel, [shape((height, cols), BF16)], own, *gots, below)
+    (out,) = call(last_kernel, [shape((own_pairs, own_rows, cols), BF16)], bulk_rows, keep_c, got_c, below)
     return out
 
 

time: 70.1 us -> 69.1 us (0.986)
  waiting for transfers between devices: 18.8 us -> 17.4 us
    ppermute x17, waiting for transfers between devices: 18.8 us -> 17.4 us  [swap(): lax.ppermute(value, axis, [(i, i ^ bit) for i in range(lax.axis_size(axis...]
    pallas_call x14 -> x17, Pallas kernels: 28.7 us -> 29.3 us  [call(): pl.pallas_call(body, in_specs=[pl.BlockSpec(memory_space=pl.ANY)] * count...]
  transfers between devices with their start and end apart: 17 -> 17, of which waited for: 7 -> 3; matrix products, arithmetic and copies ran while one was open for 0% -> 0% of each run, Pallas kernels for 28% -> 30%
where the time goes in v4:
time: 69.1 us; the launch traced here: 67.9 us
  Pallas kernels  29.3 us (42%)
  starting transfers between devices  19.4 us (28%)
  waiting for transfers between devices  17.4 us (25%)
  local copies, waits for them, and re-layouts  1.56 us (2%)
    pallas_call x17, Pallas kernels, call(): pl.pallas_call(body, in_specs=[pl.BlockSpec(memory_space=pl.ANY)] * count...  29.3 us
    ppermute x17, starting transfers between devices, swap(): lax.ppermute(value, axis, [(i, i ^ bit) for i in range(lax.axis_size(axis...  19.4 us
    ppermute x17, waiting for transfers between devices, swap(): lax.ppermute(value, axis, [(i, i ^ bit) for i in range(lax.axis_size(axis...  17.4 us
  transfers between devices with their start and end apart: 17, of which 3 were waited for; matrix products, arithmetic and copies ran while one was open for 0% of the time, Pallas kernels for 30%

profile of v4, /device:TPU:0, one launch (start us, length us, event | category | flops | bytes accessed | tf_op | source)
XLA Modules:
  0.0 67.9 jit_solution(3107396426380033432)
XLA Ops:
  0.0 0.1 pad_add_fusion.refs_0_.refs_1_
  0.1 1.3 %copy-done.1 = bf16[80,12,640]{2,0,1:T(8,128)(2,1)S(1)} copy-done((bf16[80,12,640]{2,0,1:T(8,128)(2,1)S(1)}, bf16[80,12,640]{2,0,1:T(8,128)(2,1)}, u32[]{:S(2)}) %copy-start.1) | copy-done | bytes 1228824
  1.4 7.9 %shard_map.46 = (bf16[640,960]{1,0:T(8,128)(2,1)S(1)}, f32[512,640]{1,0:T(8,128)S(1)}, bf16[8,960,640]{2,1,0:T(8,128)(2,1)S(1)}, bf16[3,960,640]{2,1,0:T(8,128)(2,1)}) custom-call(s32[4]{0:T(128)S(1)} %pad_add_fusion.refs_0_.refs_1_, bf16[960,640]{1,0:T(8,128)(2,1)S(1)} %bitcast.10, bf16[960,8,640]{2,1,0:T(8,128)(2,1)} %bitcast.11), custom_call_target="tpu_custom_call" | custom-call | flops 1000 | bytes 1000 | tf_op jit(solution)/shard_map/pallas_call | solution.py:51
  9.3 0.5 collective-permute-start
  9.8 2.3 %shard_map.47 = (f32[512,640]{1,0:T(8,128)S(1)}, f32[512,640]{1,0:T(8,128)S(1)}, bf16[8,960,640]{2,1,0:T(8,128)(2,1)S(1)}) custom-call(s32[4]{0:T(128)S(1)} %pad_add_fusion.refs_0_.refs_1_, bf16[640,960]{1,0:T(8,128)(2,1)S(1)} %get-tuple-element.35.refs_1_.refs_2_, bf16[8,960,640]{2,1,0:T(8,128)(2,1)S(1)} %get-tuple-element.36.refs_2_), custom_call_target="tpu_custom_call", output_to_operand_aliasing={{2}: (2, {})} | custom-call | flops 1000 | bytes 1000 | tf_op jit(solution)/shard_map/pallas_call | solution.py:51
  12.2 0.1 collective-permute-start.1
  12.3 0.4 collective-permute-start.2
  12.8 2.4 %shard_map.48 = (f32[512,640]{1,0:T(8,128)S(1)}, f32[512,640]{1,0:T(8,128)S(1)}, bf16[8,960,640]{2,1,0:T(8,128)(2,1)S(1)}) custom-call(s32[4]{0:T(128)S(1)} %pad_add_fusion.refs_0_.refs_1_, bf16[640,960]{1,0:T(8,128)(2,1)S(1)} %get-tuple-element.35.refs_1_.refs_2_, bf16[8,960,640]{2,1,0:T(8,128)(2,1)S(1)} %get-tuple-element.37.refs_2_), custom_call_target="tpu_custom_call", output_to_operand_aliasing={{2}: (2, {})} | custom-call | flops 1000 | bytes 1000 | tf_op jit(solution)/shard_map/pallas_call | solution.py:51
  15.1 0.1 collective-permute-start.3
  15.3 0.4 collective-permute-start.4
  15.7 3.2 %shard_map.49 = (f32[512,640]{1,0:T(8,128)S(1)}, f32[512,640]{1,0:T(8,128)S(1)}, f32[512,640]{1,0:T(8,128)S(1)}, bf16[8,960,640]{2,1,0:T(8,128)(2,1)S(1)}) custom-call(s32[4]{0:T(128)S(1)} %pad_add_fusion.refs_0_.refs_1_, bf16[640,960]{1,0:T(8,128)(2,1)S(1)} %get-tuple-element.35.refs_1_.refs_2_, ...), custom_call_target="tpu_custom_call", output_to_operand_aliasing={{3}: (2, {})} | custom-call | flops 1000 | bytes 1000 | tf_op jit(solution)/shard_map/pallas_call | solution.py:51
  18.9 0.6 shard_map.50.refs_0_
  19.5 2.6 %collective-permute-start.5 = (bf16[520,640]{1,0:T(8,128)(2,1)S(1)}, bf16[520,640]{1,0:T(8,128)(2,1)S(1)}, u32[]{:S(2)}, u32[]{:S(2)}) collective-permute-start(bf16[520,640]{1,0:T(8,128)(2,1)S(1)} %shard_map.50.refs_0_), channel_id=1, source_target_pairs={{0,2},{1,3},{2,0},{3,1},{4,6},{5,7},{6,4},{7,5},{8,10},{9,11},{10,... | collective-permute-start | bytes 1996808 | tf_op jit(solution)/shard_map/ppermute | solution.py:241
  22.1 0.0 collective-permute-done.1.refs_2_
  22.1 0.6 shard_map.51.refs_0_
  22.7 1.6 %collective-permute-start.6 = (bf16[520,640]{1,0:T(8,128)(2,1)S(1)}, bf16[520,640]{1,0:T(8,128)(2,1)S(1)}, u32[]{:S(2)}, u32[]{:S(2)}) collective-permute-start(bf16[520,640]{1,0:T(8,128)(2,1)S(1)} %shard_map.51.refs_0_), channel_id=1, source_target_pairs={{0,4},{4,0},{8,12},{12,8},{16,20},{20,16},{24,28},{28,24},{1,5},{5... | collective-permute-start | bytes 1996808 | tf_op jit(solution)/shard_map/ppermute | solution.py:241
  24.3 0.0 collective-permute-done.2.refs_3_
  24.3 1.0 %shard_map.52 = (f32[128,640]{1,0:T(8,128)S(1)}, bf16[136,640]{1,0:T(8,128)(2,1)S(1)}, bf16[136,640]{1,0:T(8,128)(2,1)S(1)}, bf16[136,640]{1,0:T(8,128)(2,1)S(1)}) custom-call(bf16[520,640]{1,0:T(8,128)(2,1)S(1)} %shard_map.51.refs_0_, s32[4]{0:T(128)S(1)} %pad_add_fusion.refs_0_.refs_1_, f32[512,640]{1,0:T(8,128)S(1)} %get-tuple-element.43.refs_2_, ...), custom_call_target="tpu_custom_call" | custom-call | flops 1000 | bytes 1000 | tf_op jit(solution)/shard_map/pallas_call | solution.py:51
  25.3 2.8 %collective-permute-start.7 = (bf16[136,640]{1,0:T(8,128)(2,1)S(1)}, bf16[136,640]{1,0:T(8,128)(2,1)S(1)}, u32[]{:S(2)}, u32[]{:S(2)}) collective-permute-start(bf16[136,640]{1,0:T(8,128)(2,1)S(1)} %get-tuple-element.52), channel_id=1, source_target_pairs={{0,16},{4,20},{8,24},{12,28},{16,0},{20,4},{24,8},{28,12},{1,17},{... | collective-permute-start | bytes 522248 | tf_op jit(solution)/shard_map/ppermute | solution.py:241
  28.2 0.0 collective-permute-done.3.refs_4_
  28.2 1.3 %collective-permute-start.8 = (bf16[136,640]{1,0:T(8,128)(2,1)S(1)}, bf16[136,640]{1,0:T(8,128)(2,1)S(1)}, u32[]{:S(2)}, u32[]{:S(2)}) collective-permute-start(bf16[136,640]{1,0:T(8,128)(2,1)S(1)} %get-tuple-element.53), channel_id=1, source_target_pairs={{0,24},{4,28},{8,16},{12,20},{16,8},{20,12},{24,0},{28,4},{1,25},{... | collective-permute-start | bytes 522248 | tf_op jit(solution)/shard_map/ppermute | solution.py:241
  29.5 0.0 collective-permute-done.4.refs_5_
  29.5 0.3 collective-permute-start.9
  29.8 3.7 %shard_map.53 = (f32[512,640]{1,0:T(8,128)S(1)}, f32[512,640]{1,0:T(8,128)S(1)}) custom-call(f32[128,640]{1,0:T(8,128)S(1)} %get-tuple-element.45.refs_0_.refs_2_, s32[4]{0:T(128)S(1)} %pad_add_fusion.refs_0_.refs_1_, bf16[640,960]{1,0:T(8,128)(2,1)S(1)} %get-tuple-element.35.refs_1_.refs_2_, bf16[3,960,640]{2,1,0:T(8,128)(2,1)S(1)} %copy-done, ...), custom_call_target="tpu_custom_call" | custom-call | flops 1000 | bytes 1000 | tf_op jit(solution)/shard_map/pallas_call | solution.py:51
  33.5 4.2 %collective-permute-done.5.refs_2_.refs_3_ = bf16[520,640]{1,0:T(8,128)(2,1)S(1)} collective-permute-done((bf16[520,640]{1,0:T(8,128)(2,1)S(1)}, bf16[520,640]{1,0:T(8,128)(2,1)S(1)}, u32[]{:S(2)}, u32[]{:S(2)}) %collective-permute-start.5) | collective-permute-done | bytes 665632 | tf_op jit(solution)/shard_map/ppermute | solution.py:241
  37.7 1.1 %shard_map.54.refs_0_ = bf16[264,640]{1,0:T(8,128)(2,1)S(1)} custom-call(s32[4]{0:T(128)S(1)} %pad_add_fusion.refs_0_.refs_1_, f32[512,640]{1,0:T(8,128)S(1)} %get-tuple-element.49.refs_1_.refs_2_, bf16[520,640]{1,0:T(8,128)(2,1)S(1)} %collective-permute-done.5.refs_2_.refs_3_), custom_call_target="tpu_custom_call" | custom-call | flops 1000 | bytes 1000 | tf_op jit(solution)/shard_map/pallas_call | solution.py:51
  38.7 1.8 %collective-permute-start.10 = (bf16[264,640]{1,0:T(8,128)(2,1)S(1)}, bf16[264,640]{1,0:T(8,128)(2,1)S(1)}, u32[]{:S(2)}, u32[]{:S(2)}) collective-permute-start(bf16[264,640]{1,0:T(8,128)(2,1)S(1)} %shard_map.54.refs_0_), channel_id=1, source_target_pairs={{0,4},{4,0},{8,12},{12,8},{16,20},{20,16},{24,28},{28,24},{1,5},{5... | collective-permute-start | bytes 1013768 | tf_op jit(solution)/shard_map/ppermute | solution.py:241
  40.6 1.1 %shard_map.55.refs_0_ = bf16[264,640]{1,0:T(8,128)(2,1)S(1)} custom-call(bf16[264,640]{1,0:T(8,128)(2,1)S(1)} %shard_map.54.refs_0_, s32[4]{0:T(128)S(1)} %pad_add_fusion.refs_0_.refs_1_, f32[512,640]{1,0:T(8,128)S(1)} %get-tuple-element.50.refs_2_.refs_4_, bf16[520,640]{1,0:T(8,128)(2,1)S(1)} %collective-permute-done.6.refs_3_.refs_5_), custom_call_target="tpu_custom_call" | custom-call | flops 1000 | bytes 1000 | tf_op jit(solution)/shard_map/pallas_call | solution.py:51
  41.6 1.6 %collective-permute-start.11 = (bf16[264,640]{1,0:T(8,128)(2,1)S(1)}, bf16[264,640]{1,0:T(8,128)(2,1)S(1)}, u32[]{:S(2)}, u32[]{:S(2)}) collective-permute-start(bf16[264,640]{1,0:T(8,128)(2,1)S(1)} %shard_map.55.refs_0_), channel_id=1, source_target_pairs={{0,2},{1,3},{2,0},{3,1},{4,6},{5,7},{6,4},{7,5},{8,10},{9,11},{10,... | collective-permute-start | bytes 1013768 | tf_op jit(solution)/shard_map/ppermute | solution.py:241
  43.2 0.9 %shard_map.56 = (f32[256,640]{1,0:T(8,128)S(1)}, f32[256,640]{1,0:T(8,128)S(1)}) custom-call(bf16[264,640]{1,0:T(8,128)(2,1)S(1)} %shard_map.55.refs_0_, s32[4]{0:T(128)S(1)} %pad_add_fusion.refs_0_.refs_1_, f32[512,640]{1,0:T(8,128)S(1)} %get-tuple-element.49.refs_1_.refs_2_, bf16[520,640]{1,0:T(8,128)(2,1)S(1)} %collective-permute-done.5.refs_2_.refs_3_, ...), custom_call_target="tpu_custom_call" | custom-call | flops 1000 | bytes 1000 | tf_op jit(solution)/shard_map/pallas_call | solution.py:51
  44.2 0.9 %shard_map.57 = (f32[64,640]{1,0:T(8,128)S(1)}, bf16[72,640]{1,0:T(8,128)(2,1)S(1)}) custom-call(f32[256,640]{1,0:T(8,128)S(1)} %get-tuple-element.51.refs_0_.refs_2_, s32[4]{0:T(128)S(1)} %pad_add_fusion.refs_0_.refs_1_, f32[128,640]{1,0:T(8,128)S(1)} %get-tuple-element.45.refs_0_.refs_2_, bf16[136,640]{1,0:T(8,128)(2,1)S(1)} %collective-permute-done.7.refs_3_, ...), custom_call_target="tpu_custom_call" | custom-call | flops 34359738368 | bytes 1000 | tf_op jit(solution)/shard_map/pallas_call | solution.py:51
  45.1 0.0 copy-start.2
  45.1 0.0 copy-start.3
  45.1 0.6 collective-permute-start.12
  45.7 6.2 %collective-permute-done.11.refs_5_ = bf16[264,640]{1,0:T(8,128)(2,1)S(1)} collective-permute-done((bf16[264,640]{1,0:T(8,128)(2,1)S(1)}, bf16[264,640]{1,0:T(8,128)(2,1)S(1)}, u32[]{:S(2)}, u32[]{:S(2)}) %collective-permute-start.11) | collective-permute-done | bytes 337952 | tf_op jit(solution)/shard_map/ppermute | solution.py:241
  51.9 1.2 %shard_map.58 = (bf16[136,640]{1,0:T(8,128)(2,1)S(1)}, bf16[136,640]{1,0:T(8,128)(2,1)S(1)}, bf16[136,640]{1,0:T(8,128)(2,1)S(1)}) custom-call(bf16[72,640]{1,0:T(8,128)(2,1)S(1)} %get-tuple-element.55.refs_0_, s32[4]{0:T(128)S(1)} %pad_add_fusion.refs_0_.refs_1_, f32[256,640]{1,0:T(8,128)S(1)} %get-tuple-element.51.refs_0_.refs_2_, ...), custom_call_target="tpu_custom_call" | custom-call | flops 1000 | bytes 1000 | tf_op jit(solution)/shard_map/pallas_call | solution.py:51
  53.1 2.6 %collective-permute-start.13 = (bf16[136,640]{1,0:T(8,128)(2,1)S(1)}, bf16[136,640]{1,0:T(8,128)(2,1)S(1)}, u32[]{:S(2)}, u32[]{:S(2)}) collective-permute-start(bf16[136,640]{1,0:T(8,128)(2,1)S(1)} %get-tuple-element.57.refs_0_), channel_id=1, source_target_pairs={{0,16},{4,20},{8,24},{12,28},{16,0},{20,4},{24,8},{28,12},{1,17},{... | collective-permute-start | bytes 522248 | tf_op jit(solution)/shard_map/ppermute | solution.py:241
  55.8 1.4 %collective-permute-start.14 = (bf16[136,640]{1,0:T(8,128)(2,1)S(1)}, bf16[136,640]{1,0:T(8,128)(2,1)S(1)}, u32[]{:S(2)}, u32[]{:S(2)}) collective-permute-start(bf16[136,640]{1,0:T(8,128)(2,1)S(1)} %get-tuple-element.61), channel_id=1, source_target_pairs={{0,24},{4,28},{8,16},{12,20},{16,8},{20,12},{24,0},{28,4},{1,25},{... | collective-permute-start | bytes 522248 | tf_op jit(solution)/shard_map/ppermute | solution.py:241
  57.1 0.2 collective-permute-start.15
  57.4 0.6 shard_map.59
  58.0 0.8 %collective-permute-start.16 = (bf16[40,640]{1,0:T(8,128)(2,1)S(1)}, bf16[40,640]{1,0:T(8,128)(2,1)S(1)}, u32[]{:S(2)}, u32[]{:S(2)}) collective-permute-start(bf16[40,640]{1,0:T(8,128)(2,1)S(1)} %get-tuple-element.64), channel_id=1, source_target_pairs={{0,4},{4,0},{8,12},{12,8},{16,20},{20,16},{24,28},{28,24},{1,5},{5... | collective-permute-start | bytes 153608 | tf_op jit(solution)/shard_map/ppermute | solution.py:241
  58.8 0.1 dynamic-slice_bitcast_fusion
  58.9 0.1 copy.8.refs_6_
  59.0 0.1 dynamic_slice.7.refs_8_
  59.1 0.7 %shard_map.60 = (f32[128,640]{1,0:T(8,128)S(1)}, f32[2,80,640]{2,1,0:T(8,128)S(1)}) custom-call(f32[32,640]{1,0:T(8,128)S(1)} %get-tuple-element.59.refs_0_.refs_1_, s32[4]{0:T(128)S(1)} %pad_add_fusion.refs_0_.refs_1_, f32[256,640]{1,0:T(8,128)S(1)} %get-tuple-element.51.refs_0_.refs_2_, bf16[264,640]{1,0:T(8,128)(2,1)S(1)} %collective-permute-done.10.refs_3_, ...), custom_call_target="tpu_custom_call" | custom-call | flops 1000 | bytes 1000 | tf_op jit(solution)/shard_map/pallas_call | solution.py:51
  59.8 7.0 %collective-permute-done.13.refs_1_ = bf16[136,640]{1,0:T(8,128)(2,1)S(1)} collective-permute-done((bf16[136,640]{1,0:T(8,128)(2,1)S(1)}, bf16[136,640]{1,0:T(8,128)(2,1)S(1)}, u32[]{:S(2)}, u32[]{:S(2)}) %collective-permute-start.13) | collective-permute-done | bytes 174112 | tf_op jit(solution)/shard_map/ppermute | solution.py:241
  66.8 0.3 shard_map.61.refs_0_
  67.1 0.7 %shard_map.62 = bf16[2,80,640]{2,1,0:T(8,128)(2,1)} custom-call(bf16[128,640]{1,0:T(8,128)(2,1)S(1)} %shard_map.61.refs_0_, f32[32,640]{1,0:T(8,128)S(1)} %get-tuple-element.59.refs_0_.refs_1_, bf16[40,640]{1,0:T(8,128)(2,1)S(1)} %collective-permute-done.16.refs_2_, f32[2,80,640]{2,1,0:T(8,128)S(1)} %get-tuple-element.63.refs_4_.refs_3_), custom_call_target="tpu_custom_call" | custom-call | flops 1000 | bytes 1000 | tf_op jit(solution)/shard_map/pallas_call | solution.py:51
  (16 shorter events, 0.0 us)
Async XLA Ops:
  0.1 1.3 %copy-start.1 = (bf16[80,12,640]{2,0,1:T(8,128)(2,1)S(1)}, bf16[80,12,640]{2,0,1:T(8,128)(2,1)}, u32[]{:S(2)}) copy-start(bf16[80,12,640]{2,0,1:T(8,128)(2,1)} %param.4) | copy-start | bytes 3686404
  9.3 9.6 %collective-permute-start = (f32[512,640]{1,0:T(8,128)S(1)}, f32[512,640]{1,0:T(8,128)S(1)}, u32[]{:S(2)}, u32[]{:S(2)}) collective-permute-start(f32[512,640]{1,0:T(8,128)S(1)} %get-tuple-element.40), channel_id=1, source_target_pairs={{0,1},{1,0},{2,3},{3,2},{4,5},{5,4},{6,7},{7,6},{8,9},{9,8},{10,11... | collective-permute-start | bytes 3932168 | tf_op jit(solution)/shard_map/ppermute | solution.py:241
  12.2 9.9 %collective-permute-start.1 = (f32[512,640]{1,0:T(8,128)S(1)}, f32[512,640]{1,0:T(8,128)S(1)}, u32[]{:S(2)}, u32[]{:S(2)}) collective-permute-start(f32[512,640]{1,0:T(8,128)S(1)} %get-tuple-element.42), channel_id=1, source_target_pairs={{0,1},{1,0},{2,3},{3,2},{4,5},{5,4},{6,7},{7,6},{8,9},{9,8},{10,11... | collective-permute-start | bytes 3932168 | tf_op jit(solution)/shard_map/ppermute | solution.py:241
  12.3 12.0 %collective-permute-start.2 = (f32[512,640]{1,0:T(8,128)S(1)}, f32[512,640]{1,0:T(8,128)S(1)}, u32[]{:S(2)}, u32[]{:S(2)}) collective-permute-start(f32[512,640]{1,0:T(8,128)S(1)} %get-tuple-element.44), channel_id=1, source_target_pairs={{0,1},{1,0},{2,3},{3,2},{4,5},{5,4},{6,7},{7,6},{8,9},{9,8},{10,11... | collective-permute-start | bytes 3932168 | tf_op jit(solution)/shard_map/ppermute | solution.py:241
  15.1 13.1 %collective-permute-start.3 = (f32[512,640]{1,0:T(8,128)S(1)}, f32[512,640]{1,0:T(8,128)S(1)}, u32[]{:S(2)}, u32[]{:S(2)}) collective-permute-start(f32[512,640]{1,0:T(8,128)S(1)} %get-tuple-element.47), channel_id=1, source_target_pairs={{0,1},{1,0},{2,3},{3,2},{4,5},{5,4},{6,7},{7,6},{8,9},{9,8},{10,11... | collective-permute-start | bytes 3932168 | tf_op jit(solution)/shard_map/ppermute | solution.py:241
  15.3 14.3 %collective-permute-start.4 = (f32[512,640]{1,0:T(8,128)S(1)}, f32[512,640]{1,0:T(8,128)S(1)}, u32[]{:S(2)}, u32[]{:S(2)}) collective-permute-start(f32[512,640]{1,0:T(8,128)S(1)} %get-tuple-element.48), channel_id=1, source_target_pairs={{0,1},{1,0},{2,3},{3,2},{4,5},{5,4},{6,7},{7,6},{8,9},{9,8},{10,11... | collective-permute-start | bytes 3932168 | tf_op jit(solution)/shard_map/ppermute | solution.py:241
  19.5 18.2 %collective-permute-start.5 = (bf16[520,640]{1,0:T(8,128)(2,1)S(1)}, bf16[520,640]{1,0:T(8,128)(2,1)S(1)}, u32[]{:S(2)}, u32[]{:S(2)}) collective-permute-start(bf16[520,640]{1,0:T(8,128)(2,1)S(1)} %shard_map.50.refs_0_), channel_id=1, source_target_pairs={{0,2},{1,3},{2,0},{3,1},{4,6},{5,7},{6,4},{7,5},{8,10},{9,11},{10,... | collective-permute-start | bytes 1996808 | tf_op jit(solution)/shard_map/ppermute | solution.py:241
  22.1 7.7 %copy-start = (bf16[3,960,640]{2,1,0:T(8,128)(2,1)S(1)}, bf16[3,960,640]{2,1,0:T(8,128)(2,1)}, u32[]{:S(2)}) copy-start(bf16[3,960,640]{2,1,0:T(8,128)(2,1)} %get-tuple-element.46.refs_3_) | copy-start | bytes 11059204
  22.7 17.8 %collective-permute-start.6 = (bf16[520,640]{1,0:T(8,128)(2,1)S(1)}, bf16[520,640]{1,0:T(8,128)(2,1)S(1)}, u32[]{:S(2)}, u32[]{:S(2)}) collective-permute-start(bf16[520,640]{1,0:T(8,128)(2,1)S(1)} %shard_map.51.refs_0_), channel_id=1, source_target_pairs={{0,4},{4,0},{8,12},{12,8},{16,20},{20,16},{24,28},{28,24},{1,5},{5... | collective-permute-start | bytes 1996808 | tf_op jit(solution)/shard_map/ppermute | solution.py:241
  25.3 18.8 %collective-permute-start.7 = (bf16[136,640]{1,0:T(8,128)(2,1)S(1)}, bf16[136,640]{1,0:T(8,128)(2,1)S(1)}, u32[]{:S(2)}, u32[]{:S(2)}) collective-permute-start(bf16[136,640]{1,0:T(8,128)(2,1)S(1)} %get-tuple-element.52), channel_id=1, source_target_pairs={{0,16},{4,20},{8,24},{12,28},{16,0},{20,4},{24,8},{28,12},{1,17},{... | collective-permute-start | bytes 522248 | tf_op jit(solution)/shard_map/ppermute | solution.py:241
  28.2 16.0 %collective-permute-start.8 = (bf16[136,640]{1,0:T(8,128)(2,1)S(1)}, bf16[136,640]{1,0:T(8,128)(2,1)S(1)}, u32[]{:S(2)}, u32[]{:S(2)}) collective-permute-start(bf16[136,640]{1,0:T(8,128)(2,1)S(1)} %get-tuple-element.53), channel_id=1, source_target_pairs={{0,24},{4,28},{8,16},{12,20},{16,8},{20,12},{24,0},{28,4},{1,25},{... | collective-permute-start | bytes 522248 | tf_op jit(solution)/shard_map/ppermute | solution.py:241
  29.5 14.6 %collective-permute-start.9 = (bf16[136,640]{1,0:T(8,128)(2,1)S(1)}, bf16[136,640]{1,0:T(8,128)(2,1)S(1)}, u32[]{:S(2)}, u32[]{:S(2)}) collective-permute-start(bf16[136,640]{1,0:T(8,128)(2,1)S(1)} %get-tuple-element.54), channel_id=1, source_target_pairs={{0,8},{4,12},{8,0},{12,4},{16,24},{20,28},{24,16},{28,20},{1,9},{5... | collective-permute-start | bytes 522248 | tf_op jit(solution)/shard_map/ppermute | solution.py:241
  38.7 13.2 %collective-permute-start.10 = (bf16[264,640]{1,0:T(8,128)(2,1)S(1)}, bf16[264,640]{1,0:T(8,128)(2,1)S(1)}, u32[]{:S(2)}, u32[]{:S(2)}) collective-permute-start(bf16[264,640]{1,0:T(8,128)(2,1)S(1)} %shard_map.54.refs_0_), channel_id=1, source_target_pairs={{0,4},{4,0},{8,12},{12,8},{16,20},{20,16},{24,28},{28,24},{1,5},{5... | collective-permute-start | bytes 1013768 | tf_op jit(solution)/shard_map/ppermute | solution.py:241
  41.6 10.3 %collective-permute-start.11 = (bf16[264,640]{1,0:T(8,128)(2,1)S(1)}, bf16[264,640]{1,0:T(8,128)(2,1)S(1)}, u32[]{:S(2)}, u32[]{:S(2)}) collective-permute-start(bf16[264,640]{1,0:T(8,128)(2,1)S(1)} %shard_map.55.refs_0_), channel_id=1, source_target_pairs={{0,2},{1,3},{2,0},{3,1},{4,6},{5,7},{6,4},{7,5},{8,10},{9,11},{10,... | collective-permute-start | bytes 1013768 | tf_op jit(solution)/shard_map/ppermute | solution.py:241
  45.1 13.7 %copy-start.2 = (f32[640]{0:T(1024)S(1)}, f32[640]{0:T(1024)}, u32[]{:S(2)}) copy-start(f32[640]{0:T(1024)} %param.6) | copy-start | bytes 7684
  45.1 13.9 %copy-start.3 = (f32[8]{0:T(128)S(1)}, f32[8]{0:T(128)}, u32[]{:S(2)}) copy-start(f32[8]{0:T(128)} %param.7) | copy-start | bytes 100
  45.1 12.3 %collective-permute-start.12 = (bf16[72,640]{1,0:T(8,128)(2,1)S(1)}, bf16[72,640]{1,0:T(8,128)(2,1)S(1)}, u32[]{:S(2)}, u32[]{:S(2)}) collective-permute-start(bf16[72,640]{1,0:T(8,128)(2,1)S(1)} %get-tuple-element.55.refs_0_), channel_id=1, source_target_pairs={{0,2},{1,3},{2,0},{3,1},{4,6},{5,7},{6,4},{7,5},{8,10},{9,11},{10,... | collective-permute-start | bytes 276488 | tf_op jit(solution)/shard_map/ppermute | solution.py:241
  53.1 13.7 %collective-permute-start.13 = (bf16[136,640]{1,0:T(8,128)(2,1)S(1)}, bf16[136,640]{1,0:T(8,128)(2,1)S(1)}, u32[]{:S(2)}, u32[]{:S(2)}) collective-permute-start(bf16[136,640]{1,0:T(8,128)(2,1)S(1)} %get-tuple-element.57.refs_0_), channel_id=1, source_target_pairs={{0,16},{4,20},{8,24},{12,28},{16,0},{20,4},{24,8},{28,12},{1,17},{... | collective-permute-start | bytes 522248 | tf_op jit(solution)/shard_map/ppermute | solution.py:241
  55.8 11.0 %collective-permute-start.14 = (bf16[136,640]{1,0:T(8,128)(2,1)S(1)}, bf16[136,640]{1,0:T(8,128)(2,1)S(1)}, u32[]{:S(2)}, u32[]{:S(2)}) collective-permute-start(bf16[136,640]{1,0:T(8,128)(2,1)S(1)} %get-tuple-element.61), channel_id=1, source_target_pairs={{0,24},{4,28},{8,16},{12,20},{16,8},{20,12},{24,0},{28,4},{1,25},{... | collective-permute-start | bytes 522248 | tf_op jit(solution)/shard_map/ppermute | solution.py:241
  57.1 9.7 %collective-permute-start.15 = (bf16[136,640]{1,0:T(8,128)(2,1)S(1)}, bf16[136,640]{1,0:T(8,128)(2,1)S(1)}, u32[]{:S(2)}, u32[]{:S(2)}) collective-permute-start(bf16[136,640]{1,0:T(8,128)(2,1)S(1)} %get-tuple-element.62), channel_id=1, source_target_pairs={{0,8},{4,12},{8,0},{12,4},{16,24},{20,28},{24,16},{28,20},{1,9},{5... | collective-permute-start | bytes 522248 | tf_op jit(solution)/shard_map/ppermute | solution.py:241
  58.0 9.1 %collective-permute-start.16 = (bf16[40,640]{1,0:T(8,128)(2,1)S(1)}, bf16[40,640]{1,0:T(8,128)(2,1)S(1)}, u32[]{:S(2)}, u32[]{:S(2)}) collective-permute-start(bf16[40,640]{1,0:T(8,128)(2,1)S(1)} %get-tuple-element.64), channel_id=1, source_target_pairs={{0,4},{4,0},{8,12},{12,8},{16,20},{20,16},{24,28},{28,24},{1,5},{5... | collective-permute-start | bytes 153608 | tf_op jit(solution)/shard_map/ppermute | solution.py:241

commit v5 on v4

--- a/solution.py
+++ b/solution.py
@@ -62,27 +62,38 @@
     )(*after, *args)
 
 
+def plane(flat, group, side, rows=slice(None)):
+    cols = flat.shape[2] // 2
+    return flat.at[group, rows, pl.ds(pl.multiple_of(side * cols, 128), cols)]
+
+
 def home_planes(place):
     x, core = place[0], place[1]
-    return 4 * x + 2 * core, 2 * core + 1, 4 + 2 * core + 1
-
-
-def front_kernel(place, wide, amp, turned, out, flat, far, held, sem, far_sem, *, block, unit, own_rows, tiles_y, tiles_z):
+    return (2 * core, x), (2 * core + 1, 0), (2 * core + 1, 1)
+
+
+def front_kernel(place, wide, amp, turned, out, flat, far, held, sem, far_sem, *, block, far_block, unit, own_rows, tiles_y, tiles_z):
     depth, pairs, cols = amp.shape
+    virt = wide.shape[1]
     copies = [
         pltpu.make_async_copy(amp.at[pl.ds(at, block)], held.at[pl.ds(at, block)], sem.at[at // block])
         for at in range(0, depth, block)
     ]
     for copy in copies:
         copy.start()
-    t = wide[...].T
     bulk = own_rows - EDGE
-    for y in range(tiles_y):
-        for z in range(tiles_z):
-            at = (z * tiles_y + y) * own_rows
-            turned[pl.ds((y * tiles_z + z) * bulk, bulk), :] = t[at : at + bulk]
-            edge = tiles_y * tiles_z * bulk + (z * tiles_y + y) * EDGE
-            turned[pl.ds(edge, EDGE), :] = t[at + bulk : at + own_rows]
+
+    def turn(first, count):
+        t = wide[:, first : first + count].T
+        for at in range(0, count, EDGE):
+            tile, row = divmod(first + at, own_rows)
+            z, y = divmod(tile, tiles_y)
+            if row < bulk:
+                to = (y * tiles_z + z) * bulk + row
+            else:
+                to = tiles_y * tiles_z * bulk + (z * tiles_y + y) * EDGE
+            turned[to : to + EDGE, :] = t[at : at + EDGE]
+
     leaving = []
     n = unit * pairs
     r = lax.broadcasted_iota(jnp.int32, (n, n), 0)
@@ -94,20 +105,22 @@
         part = held[at : at + unit].reshape(n, cols)
         moved = jnp.dot(perm, part, preferred_element_type=F32).astype(BF16)
         for j in range(pairs):
-            flat[j, at : at + unit, :] = moved[j * unit : (j + 1) * unit]
+            flat[j % 4, at : at + unit, pl.ds(j // 4 * cols, cols)] = moved[j * unit : (j + 1) * unit]
+        if at // unit % 4 == 2 and at // unit // 4 < virt // 128:
+            turn(at // unit // 4 * 128, 128)
         done = at + unit
-        if done % block == 0:
-            here = pl.ds(done - block, block)
-            for slot, plane in enumerate(home_planes(place)):
+        if done % far_block == 0:
+            here = pl.ds(done - far_block, far_block)
+            for slot, (group, side) in enumerate(home_planes(place)):
                 copy = pltpu.make_async_copy(
-                    flat.at[plane, here], far.at[slot, here], far_sem.at[slot, done // block - 1]
+                    plane(flat, group, side, here), far.at[slot, here], far_sem.at[slot, done // far_block - 1]
                 )
                 copy.start()
                 leaving.append(copy)
     x, core = place[0], place[1]
     rows = tiles_y * tiles_z * bulk
     out[...] = jnp.dot(
-        turned[pl.ds(0, rows), :], flat[4 * (1 - x) + 2 * (1 - core)], preferred_element_type=F32
+        turned[pl.ds(0, rows), :], plane(flat, 2 * (1 - core), 1 - x)[...], preferred_element_type=F32
     )
     for copy in leaving:
         copy.wait()
@@ -117,29 +130,33 @@
     x, core, y = place[0], place[1], place[2]
     rows = tiles_z * bulk
 
-    def dot(at, height, plane):
-        return jnp.dot(turned[pl.ds(at, height), :], flat[plane], preferred_element_type=F32)
+    cols = flat.shape[2] // 2
+
+    def dot(at, height, group, side=None):
+        rhs = flat.at[group] if side is None else plane(flat, group, side)
+        return jnp.dot(turned[pl.ds(at, height), :], rhs[...], preferred_element_type=F32)
 
     for out, parts in zip(outs[:-1], jobs):
         base = 0
         for who, part in parts:
             pair = 2 * (core if who == "own" else 1 - core)
             if part == "a_away":
-                out[pl.ds(base, 2 * rows), :] = dot(0, 2 * rows, 4 * (1 - x) + pair)
+                out[pl.ds(base, 2 * rows), :] = dot(0, 2 * rows, pair, 1 - x)
             elif part == "a_home":
-                out[pl.ds(base, 2 * rows), :] = dot(0, 2 * rows, 4 * x + pair)
+                out[pl.ds(base, 2 * rows), :] = dot(0, 2 * rows, pair, x)
             elif part in ("b_away", "b_home"):
                 side = y if part == "b_home" else 1 - y
+                got = dot(pl.multiple_of(side * rows, 16), rows, pair + 1)
                 for xx in range(2):
-                    at = pl.multiple_of(side * rows, 16)
-                    out[pl.ds(base + xx * rows, rows), :] = dot(at, rows, 4 * xx + pair + 1)
+                    out[pl.ds(base + xx * rows, rows), :] = got[:, xx * cols :][:, :cols]
             else:
-                for xx in range(2):
-                    for i in range(2):
-                        got = dot(2 * rows, tiles_y * tiles_z * EDGE, 4 * xx + pair + i)
+                for i in range(2):
+                    wide = dot(2 * rows, tiles_y * tiles_z * EDGE, pair + i)
+                    for xx in range(2):
+                        got = wide[:, xx * cols :][:, :cols]
                         for zz in range(tiles_z):
                             for yy in range(tiles_y):
-                                at = base + (((zz * 2 + xx) * tiles_y + yy) * 2 + i) * EDGE
+                                at = base + (((zz * tiles_y + yy) * 2 + xx) * 2 + i) * EDGE
                                 out[pl.ds(at, EDGE), :] = got[(zz * tiles_y + yy) * EDGE :][:EDGE]
             base += 2 * rows if part != "c" else 4 * tiles_y * tiles_z * EDGE
 
@@ -261,18 +278,18 @@
     def coded(height):
         return shape((height + PAD, cols), BF16)
 
-    block = 160
-    held = pltpu.VMEM((pairs, depth, cols), BF16)
+    block, far_block = 320, 320
+    held = pltpu.VMEM((pairs // 2, depth, 2 * cols), BF16)
     turned, c_a, flat, far = call(
         functools.partial(
-            front_kernel, block=block, unit=32, own_rows=own_rows, tiles_y=tiles_y, tiles_z=tiles_z
+            front_kernel, block=block, far_block=far_block, unit=32, own_rows=own_rows, tiles_y=tiles_y, tiles_z=tiles_z
         ),
         [pltpu.VMEM((virt, depth), BF16), full(2 * rows), held, pltpu.HBM((3, depth, cols), BF16)],
         place, wide, amplitudes.reshape(depth, pairs, cols), specs=[SCALAR, WHOLE, FAR], room=40, out_specs=[WHOLE] * 3 + [FAR],
         scratch=[
             pltpu.VMEM((depth, pairs, cols), BF16),
             pltpu.SemaphoreType.DMA((depth // block,)),
-            pltpu.SemaphoreType.DMA((3, depth // block)),
+            pltpu.SemaphoreType.DMA((3, depth // far_block)),
         ],
     )
 
@@ -320,10 +337,10 @@
     got_a = swap(send_a, "tile", 1)
     got_b = swap(send_b, "ka", 2)
     keep_c, send_c = call(
-        functools.partial(halve_kernel, which=0, rows=edges // 2), [full(edges // 2), coded(edges // 2)],
+        functools.partial(halve_kernel, which=2, rows=edges // 2), [full(edges // 2), coded(edges // 2)],
         place, keep_c, *gots_c, specs=[SCALAR] + [WHOLE] * tiles_z, work=LONG, after=[keep_a],
     )
-    got_c = swap(send_c, "ka", 2)
+    got_c = swap(send_c, "tile", 1)
 
     height = own_pairs * bulk
     line = functools.partial(line_kernel, rows=bulk)
@@ -334,10 +351,10 @@
     )
     gots = [swap(send, "tile", 2 * hop) for hop, send in zip(hops, sends)]
     keep_c, send_c = call(
-        functools.partial(halve_kernel, which=2, rows=edges // 4), [full(edges // 4), coded(edges // 4)],
+        functools.partial(halve_kernel, which=0, rows=edges // 4), [full(edges // 4), coded(edges // 4)],
         place, keep_c, got_c, specs=[SCALAR, WHOLE, WHOLE], after=[sends[0]],
     )
-    got_c = swap(send_c, "tile", 1)
+    got_c = swap(send_c, "ka", 2)
     own_virt = lax.dynamic_slice_in_dim(virt_energy, tile_pos * own_rows, own_rows, 0)
     own_e = lax.dynamic_slice_in_dim(pair_energy, ka_pos * own_pairs, own_pairs, 0)
     own, below = call(
@@ -386,7 +403,8 @@
     def per_device(integrals, amplitudes, virt_energy, pair_energy):
         own_rows = integrals.shape[2] // lax.axis_size("tile")
         depth = amplitudes.shape[0] * amplitudes.shape[1]
-        plain = fits and own_rows % 16 == 0 and depth % 160 == 0 and amplitudes.shape[2] == 8
+        plain = fits and own_rows % 16 == 0 and depth % 960 == 0 and amplitudes.shape[2] == 8
+        plain = plain and integrals.shape[2] % 128 == 0 and depth // 128 >= integrals.shape[2] // 128
         plan = on_chip_plan if plain else any_plan
         return plan(integrals, amplitudes, virt_energy, pair_energy)
 

time: 69.1 us -> 68.2 us (0.987)
  waiting for transfers between devices: 17.4 us -> 16.6 us
  Pallas kernels: 29.3 us -> 28.6 us
    ppermute x17, waiting for transfers between devices: 17.4 us -> 16.6 us  [swap(): lax.ppermute(value, axis, [(i, i ^ bit) for i in range(lax.axis_size(axis...]
  transfers between devices with their start and end apart: 17 -> 17, of which waited for: 3 -> 4; matrix products, arithmetic and copies ran while one was open for 0% -> 0% of each run, Pallas kernels for 30% -> 30%
where the time goes in v5:
time: 68.2 us; the launch traced here: 67 us
  Pallas kernels  28.6 us (42%)
  starting transfers between devices  19.9 us (29%)
  waiting for transfers between devices  16.6 us (24%)
  local copies, waits for them, and re-layouts  1.56 us (2%)
    pallas_call x17, Pallas kernels, call(): pl.pallas_call(body, in_specs=[pl.BlockSpec(memory_space=pl.ANY)] * count...  28.6 us
    ppermute x17, starting transfers between devices, swap(): lax.ppermute(value, axis, [(i, i ^ bit) for i in range(lax.axis_size(axis...  19.9 us
    ppermute x17, waiting for transfers between devices, swap(): lax.ppermute(value, axis, [(i, i ^ bit) for i in range(lax.axis_size(axis...  16.6 us
  transfers between devices with their start and end apart: 17, of which 4 were waited for; matrix products, arithmetic and copies ran while one was open for 0% of the time, Pallas kernels for 30%

profile of v5, /device:TPU:0, one launch (start us, length us, event | category | flops | bytes accessed | tf_op | source)
XLA Modules:
  0.0 67.0 jit_solution(16625996474201737847)
XLA Ops:
  0.0 0.1 pad_add_fusion.refs_0_.refs_1_
  0.1 1.3 %copy-done.1 = bf16[80,12,640]{2,0,1:T(8,128)(2,1)S(1)} copy-done((bf16[80,12,640]{2,0,1:T(8,128)(2,1)S(1)}, bf16[80,12,640]{2,0,1:T(8,128)(2,1)}, u32[]{:S(2)}) %copy-start.1) | copy-done | bytes 1228824
  1.4 7.8 %shard_map.46 = (bf16[640,960]{1,0:T(8,128)(2,1)S(1)}, f32[512,640]{1,0:T(8,128)S(1)}, bf16[4,960,1280]{2,1,0:T(8,128)(2,1)S(1)}, bf16[3,960,640]{2,1,0:T(8,128)(2,1)}) custom-call(s32[4]{0:T(128)S(1)} %pad_add_fusion.refs_0_.refs_1_, bf16[960,640]{1,0:T(8,128)(2,1)S(1)} %bitcast.10, bf16[960,8,640]{2,1,0:T(8,128)(2,1)} %bitcast.11), custom_call_target="tpu_custom_call" | custom-call | flops 1000 | bytes 1000 | tf_op jit(solution)/shard_map/pallas_call | solution.py:51
  9.2 0.5 collective-permute-start
  9.7 2.1 %shard_map.47 = (f32[512,640]{1,0:T(8,128)S(1)}, f32[512,640]{1,0:T(8,128)S(1)}, bf16[4,960,1280]{2,1,0:T(8,128)(2,1)S(1)}) custom-call(s32[4]{0:T(128)S(1)} %pad_add_fusion.refs_0_.refs_1_, bf16[640,960]{1,0:T(8,128)(2,1)S(1)} %get-tuple-element.35.refs_1_.refs_2_, bf16[4,960,1280]{2,1,0:T(8,128)(2,1)S(1)} %get-tuple-element.36.refs_2_), custom_call_target="tpu_custom_call", output_to_operand_aliasing={{2}: (2, {})} | custom-call | flops 1000 | bytes 1000 | tf_op jit(solution)/shard_map/pallas_call | solution.py:51
  11.8 0.1 collective-permute-start.1
  11.9 0.5 collective-permute-start.2
  12.4 2.2 %shard_map.48 = (f32[512,640]{1,0:T(8,128)S(1)}, f32[512,640]{1,0:T(8,128)S(1)}, bf16[4,960,1280]{2,1,0:T(8,128)(2,1)S(1)}) custom-call(s32[4]{0:T(128)S(1)} %pad_add_fusion.refs_0_.refs_1_, bf16[640,960]{1,0:T(8,128)(2,1)S(1)} %get-tuple-element.35.refs_1_.refs_2_, bf16[4,960,1280]{2,1,0:T(8,128)(2,1)S(1)} %get-tuple-element.37.refs_2_), custom_call_target="tpu_custom_call", output_to_operand_aliasing={{2}: (2, {})} | custom-call | flops 1000 | bytes 1000 | tf_op jit(solution)/shard_map/pallas_call | solution.py:51
  14.6 0.1 collective-permute-start.3
  14.7 0.4 collective-permute-start.4
  15.1 2.9 %shard_map.49 = (f32[512,640]{1,0:T(8,128)S(1)}, f32[512,640]{1,0:T(8,128)S(1)}, f32[512,640]{1,0:T(8,128)S(1)}, bf16[4,960,1280]{2,1,0:T(8,128)(2,1)S(1)}) custom-call(s32[4]{0:T(128)S(1)} %pad_add_fusion.refs_0_.refs_1_, bf16[640,960]{1,0:T(8,128)(2,1)S(1)} %get-tuple-element.35.refs_1_.refs_2_, ...), custom_call_target="tpu_custom_call", output_to_operand_aliasing={{3}: (2, {})} | custom-call | flops 1000 | bytes 1000 | tf_op jit(solution)/shard_map/pallas_call | solution.py:51
  18.1 0.6 shard_map.50.refs_0_
  18.7 2.6 %collective-permute-start.5 = (bf16[520,640]{1,0:T(8,128)(2,1)S(1)}, bf16[520,640]{1,0:T(8,128)(2,1)S(1)}, u32[]{:S(2)}, u32[]{:S(2)}) collective-permute-start(bf16[520,640]{1,0:T(8,128)(2,1)S(1)} %shard_map.50.refs_0_), channel_id=1, source_target_pairs={{0,2},{1,3},{2,0},{3,1},{4,6},{5,7},{6,4},{7,5},{8,10},{9,11},{10,... | collective-permute-start | bytes 1996808 | tf_op jit(solution)/shard_map/ppermute | solution.py:258
  21.3 0.0 collective-permute-done.1.refs_2_
  21.3 0.6 shard_map.51.refs_0_
  21.9 1.6 %collective-permute-start.6 = (bf16[520,640]{1,0:T(8,128)(2,1)S(1)}, bf16[520,640]{1,0:T(8,128)(2,1)S(1)}, u32[]{:S(2)}, u32[]{:S(2)}) collective-permute-start(bf16[520,640]{1,0:T(8,128)(2,1)S(1)} %shard_map.51.refs_0_), channel_id=1, source_target_pairs={{0,4},{4,0},{8,12},{12,8},{16,20},{20,16},{24,28},{28,24},{1,5},{5... | collective-permute-start | bytes 1996808 | tf_op jit(solution)/shard_map/ppermute | solution.py:258
  23.5 0.0 collective-permute-done.2.refs_3_
  23.5 1.0 %shard_map.52 = (f32[128,640]{1,0:T(8,128)S(1)}, bf16[136,640]{1,0:T(8,128)(2,1)S(1)}, bf16[136,640]{1,0:T(8,128)(2,1)S(1)}, bf16[136,640]{1,0:T(8,128)(2,1)S(1)}) custom-call(bf16[520,640]{1,0:T(8,128)(2,1)S(1)} %shard_map.51.refs_0_, s32[4]{0:T(128)S(1)} %pad_add_fusion.refs_0_.refs_1_, f32[512,640]{1,0:T(8,128)S(1)} %get-tuple-element.43.refs_2_, ...), custom_call_target="tpu_custom_call" | custom-call | flops 1000 | bytes 1000 | tf_op jit(solution)/shard_map/pallas_call | solution.py:51
  24.5 2.7 %collective-permute-start.7 = (bf16[136,640]{1,0:T(8,128)(2,1)S(1)}, bf16[136,640]{1,0:T(8,128)(2,1)S(1)}, u32[]{:S(2)}, u32[]{:S(2)}) collective-permute-start(bf16[136,640]{1,0:T(8,128)(2,1)S(1)} %get-tuple-element.52), channel_id=1, source_target_pairs={{0,16},{4,20},{8,24},{12,28},{16,0},{20,4},{24,8},{28,12},{1,17},{... | collective-permute-start | bytes 522248 | tf_op jit(solution)/shard_map/ppermute | solution.py:258
  27.2 0.0 collective-permute-done.3.refs_4_
  27.2 1.3 %collective-permute-start.8 = (bf16[136,640]{1,0:T(8,128)(2,1)S(1)}, bf16[136,640]{1,0:T(8,128)(2,1)S(1)}, u32[]{:S(2)}, u32[]{:S(2)}) collective-permute-start(bf16[136,640]{1,0:T(8,128)(2,1)S(1)} %get-tuple-element.53), channel_id=1, source_target_pairs={{0,24},{4,28},{8,16},{12,20},{16,8},{20,12},{24,0},{28,4},{1,25},{... | collective-permute-start | bytes 522248 | tf_op jit(solution)/shard_map/ppermute | solution.py:258
  28.5 0.3 collective-permute-start.9
  28.8 3.8 %shard_map.53 = (f32[512,640]{1,0:T(8,128)S(1)}, f32[512,640]{1,0:T(8,128)S(1)}) custom-call(f32[128,640]{1,0:T(8,128)S(1)} %get-tuple-element.45.refs_0_.refs_2_, s32[4]{0:T(128)S(1)} %pad_add_fusion.refs_0_.refs_1_, bf16[640,960]{1,0:T(8,128)(2,1)S(1)} %get-tuple-element.35.refs_1_.refs_2_, bf16[3,960,640]{2,1,0:T(8,128)(2,1)S(1)} %copy-done, ...), custom_call_target="tpu_custom_call" | custom-call | flops 1000 | bytes 1000 | tf_op jit(solution)/shard_map/pallas_call | solution.py:51
  32.7 4.2 %collective-permute-done.5.refs_2_.refs_3_ = bf16[520,640]{1,0:T(8,128)(2,1)S(1)} collective-permute-done((bf16[520,640]{1,0:T(8,128)(2,1)S(1)}, bf16[520,640]{1,0:T(8,128)(2,1)S(1)}, u32[]{:S(2)}, u32[]{:S(2)}) %collective-permute-start.5) | collective-permute-done | bytes 665632 | tf_op jit(solution)/shard_map/ppermute | solution.py:258
  36.8 1.1 %shard_map.54.refs_0_ = bf16[264,640]{1,0:T(8,128)(2,1)S(1)} custom-call(s32[4]{0:T(128)S(1)} %pad_add_fusion.refs_0_.refs_1_, f32[512,640]{1,0:T(8,128)S(1)} %get-tuple-element.49.refs_1_.refs_2_, bf16[520,640]{1,0:T(8,128)(2,1)S(1)} %collective-permute-done.5.refs_2_.refs_3_), custom_call_target="tpu_custom_call" | custom-call | flops 1000 | bytes 1000 | tf_op jit(solution)/shard_map/pallas_call | solution.py:51
  37.9 1.9 %collective-permute-start.10 = (bf16[264,640]{1,0:T(8,128)(2,1)S(1)}, bf16[264,640]{1,0:T(8,128)(2,1)S(1)}, u32[]{:S(2)}, u32[]{:S(2)}) collective-permute-start(bf16[264,640]{1,0:T(8,128)(2,1)S(1)} %shard_map.54.refs_0_), channel_id=1, source_target_pairs={{0,4},{4,0},{8,12},{12,8},{16,20},{20,16},{24,28},{28,24},{1,5},{5... | collective-permute-start | bytes 1013768 | tf_op jit(solution)/shard_map/ppermute | solution.py:258
  39.8 1.1 %shard_map.55.refs_0_ = bf16[264,640]{1,0:T(8,128)(2,1)S(1)} custom-call(bf16[264,640]{1,0:T(8,128)(2,1)S(1)} %shard_map.54.refs_0_, s32[4]{0:T(128)S(1)} %pad_add_fusion.refs_0_.refs_1_, f32[512,640]{1,0:T(8,128)S(1)} %get-tuple-element.50.refs_2_.refs_4_, bf16[520,640]{1,0:T(8,128)(2,1)S(1)} %collective-permute-done.6.refs_3_.refs_5_), custom_call_target="tpu_custom_call" | custom-call | flops 1000 | bytes 1000 | tf_op jit(solution)/shard_map/pallas_call | solution.py:51
  40.8 1.5 %collective-permute-start.11 = (bf16[264,640]{1,0:T(8,128)(2,1)S(1)}, bf16[264,640]{1,0:T(8,128)(2,1)S(1)}, u32[]{:S(2)}, u32[]{:S(2)}) collective-permute-start(bf16[264,640]{1,0:T(8,128)(2,1)S(1)} %shard_map.55.refs_0_), channel_id=1, source_target_pairs={{0,2},{1,3},{2,0},{3,1},{4,6},{5,7},{6,4},{7,5},{8,10},{9,11},{10,... | collective-permute-start | bytes 1013768 | tf_op jit(solution)/shard_map/ppermute | solution.py:258
  42.4 0.9 %shard_map.56 = (f32[256,640]{1,0:T(8,128)S(1)}, f32[256,640]{1,0:T(8,128)S(1)}) custom-call(bf16[264,640]{1,0:T(8,128)(2,1)S(1)} %shard_map.55.refs_0_, s32[4]{0:T(128)S(1)} %pad_add_fusion.refs_0_.refs_1_, f32[512,640]{1,0:T(8,128)S(1)} %get-tuple-element.49.refs_1_.refs_2_, bf16[520,640]{1,0:T(8,128)(2,1)S(1)} %collective-permute-done.5.refs_2_.refs_3_, ...), custom_call_target="tpu_custom_call" | custom-call | flops 1000 | bytes 1000 | tf_op jit(solution)/shard_map/pallas_call | solution.py:51
  43.3 0.9 %shard_map.57 = (f32[64,640]{1,0:T(8,128)S(1)}, bf16[72,640]{1,0:T(8,128)(2,1)S(1)}) custom-call(f32[256,640]{1,0:T(8,128)S(1)} %get-tuple-element.51.refs_0_.refs_2_, s32[4]{0:T(128)S(1)} %pad_add_fusion.refs_0_.refs_1_, f32[128,640]{1,0:T(8,128)S(1)} %get-tuple-element.45.refs_0_.refs_2_, bf16[136,640]{1,0:T(8,128)(2,1)S(1)} %collective-permute-done.7.refs_3_, ...), custom_call_target="tpu_custom_call" | custom-call | flops 34359738368 | bytes 1000 | tf_op jit(solution)/shard_map/pallas_call | solution.py:51
  44.3 0.0 copy-start.2
  44.3 0.0 copy-start.3
  44.3 0.6 collective-permute-start.12
  44.8 5.2 %collective-permute-done.11.refs_5_ = bf16[264,640]{1,0:T(8,128)(2,1)S(1)} collective-permute-done((bf16[264,640]{1,0:T(8,128)(2,1)S(1)}, bf16[264,640]{1,0:T(8,128)(2,1)S(1)}, u32[]{:S(2)}, u32[]{:S(2)}) %collective-permute-start.11) | collective-permute-done | bytes 337952 | tf_op jit(solution)/shard_map/ppermute | solution.py:258
  50.1 1.2 %shard_map.58 = (bf16[136,640]{1,0:T(8,128)(2,1)S(1)}, bf16[136,640]{1,0:T(8,128)(2,1)S(1)}, bf16[136,640]{1,0:T(8,128)(2,1)S(1)}) custom-call(bf16[72,640]{1,0:T(8,128)(2,1)S(1)} %get-tuple-element.55.refs_0_, s32[4]{0:T(128)S(1)} %pad_add_fusion.refs_0_.refs_1_, f32[256,640]{1,0:T(8,128)S(1)} %get-tuple-element.51.refs_0_.refs_2_, ...), custom_call_target="tpu_custom_call" | custom-call | flops 1000 | bytes 1000 | tf_op jit(solution)/shard_map/pallas_call | solution.py:51
  51.3 2.6 %collective-permute-start.13 = (bf16[136,640]{1,0:T(8,128)(2,1)S(1)}, bf16[136,640]{1,0:T(8,128)(2,1)S(1)}, u32[]{:S(2)}, u32[]{:S(2)}) collective-permute-start(bf16[136,640]{1,0:T(8,128)(2,1)S(1)} %get-tuple-element.57.refs_0_), channel_id=1, source_target_pairs={{0,16},{4,20},{8,24},{12,28},{16,0},{20,4},{24,8},{28,12},{1,17},{... | collective-permute-start | bytes 522248 | tf_op jit(solution)/shard_map/ppermute | solution.py:258
  54.0 1.4 %collective-permute-start.14 = (bf16[136,640]{1,0:T(8,128)(2,1)S(1)}, bf16[136,640]{1,0:T(8,128)(2,1)S(1)}, u32[]{:S(2)}, u32[]{:S(2)}) collective-permute-start(bf16[136,640]{1,0:T(8,128)(2,1)S(1)} %get-tuple-element.61), channel_id=1, source_target_pairs={{0,24},{4,28},{8,16},{12,20},{16,8},{20,12},{24,0},{28,4},{1,25},{... | collective-permute-start | bytes 522248 | tf_op jit(solution)/shard_map/ppermute | solution.py:258
  55.3 0.2 collective-permute-start.15
  55.6 0.6 shard_map.59
  56.2 1.5 %collective-permute-start.16 = (bf16[40,640]{1,0:T(8,128)(2,1)S(1)}, bf16[40,640]{1,0:T(8,128)(2,1)S(1)}, u32[]{:S(2)}, u32[]{:S(2)}) collective-permute-start(bf16[40,640]{1,0:T(8,128)(2,1)S(1)} %get-tuple-element.64), channel_id=1, source_target_pairs={{0,2},{1,3},{2,0},{3,1},{4,6},{5,7},{6,4},{7,5},{8,10},{9,11},{10,... | collective-permute-start | bytes 153608 | tf_op jit(solution)/shard_map/ppermute | solution.py:258
  57.7 0.1 dynamic-slice_bitcast_fusion
  57.8 0.1 copy.8.refs_6_
  57.9 0.1 dynamic_slice.7.refs_8_
  58.0 0.7 %shard_map.60 = (f32[128,640]{1,0:T(8,128)S(1)}, f32[2,80,640]{2,1,0:T(8,128)S(1)}) custom-call(f32[32,640]{1,0:T(8,128)S(1)} %get-tuple-element.59.refs_0_.refs_1_, s32[4]{0:T(128)S(1)} %pad_add_fusion.refs_0_.refs_1_, f32[256,640]{1,0:T(8,128)S(1)} %get-tuple-element.51.refs_0_.refs_2_, bf16[264,640]{1,0:T(8,128)(2,1)S(1)} %collective-permute-done.10.refs_3_, ...), custom_call_target="tpu_custom_call" | custom-call | flops 1000 | bytes 1000 | tf_op jit(solution)/shard_map/pallas_call | solution.py:51
  58.7 7.0 %collective-permute-done.13.refs_1_ = bf16[136,640]{1,0:T(8,128)(2,1)S(1)} collective-permute-done((bf16[136,640]{1,0:T(8,128)(2,1)S(1)}, bf16[136,640]{1,0:T(8,128)(2,1)S(1)}, u32[]{:S(2)}, u32[]{:S(2)}) %collective-permute-start.13) | collective-permute-done | bytes 174112 | tf_op jit(solution)/shard_map/ppermute | solution.py:258
  65.7 0.2 collective-permute-done.15.refs_3_
  65.9 0.3 shard_map.61.refs_0_
  66.3 0.7 %shard_map.62 = bf16[2,80,640]{2,1,0:T(8,128)(2,1)} custom-call(bf16[128,640]{1,0:T(8,128)(2,1)S(1)} %shard_map.61.refs_0_, f32[32,640]{1,0:T(8,128)S(1)} %get-tuple-element.59.refs_0_.refs_1_, bf16[40,640]{1,0:T(8,128)(2,1)S(1)} %collective-permute-done.16.refs_2_, f32[2,80,640]{2,1,0:T(8,128)S(1)} %get-tuple-element.63.refs_4_.refs_3_), custom_call_target="tpu_custom_call" | custom-call | flops 1000 | bytes 1000 | tf_op jit(solution)/shard_map/pallas_call | solution.py:51
  (16 shorter events, 0.0 us)
Async XLA Ops:
  0.1 1.3 %copy-start.1 = (bf16[80,12,640]{2,0,1:T(8,128)(2,1)S(1)}, bf16[80,12,640]{2,0,1:T(8,128)(2,1)}, u32[]{:S(2)}) copy-start(bf16[80,12,640]{2,0,1:T(8,128)(2,1)} %param.4) | copy-start | bytes 3686404
  9.2 8.9 %collective-permute-start = (f32[512,640]{1,0:T(8,128)S(1)}, f32[512,640]{1,0:T(8,128)S(1)}, u32[]{:S(2)}, u32[]{:S(2)}) collective-permute-start(f32[512,640]{1,0:T(8,128)S(1)} %get-tuple-element.40), channel_id=1, source_target_pairs={{0,1},{1,0},{2,3},{3,2},{4,5},{5,4},{6,7},{7,6},{8,9},{9,8},{10,11... | collective-permute-start | bytes 3932168 | tf_op jit(solution)/shard_map/ppermute | solution.py:258
  11.8 9.5 %collective-permute-start.1 = (f32[512,640]{1,0:T(8,128)S(1)}, f32[512,640]{1,0:T(8,128)S(1)}, u32[]{:S(2)}, u32[]{:S(2)}) collective-permute-start(f32[512,640]{1,0:T(8,128)S(1)} %get-tuple-element.42), channel_id=1, source_target_pairs={{0,1},{1,0},{2,3},{3,2},{4,5},{5,4},{6,7},{7,6},{8,9},{9,8},{10,11... | collective-permute-start | bytes 3932168 | tf_op jit(solution)/shard_map/ppermute | solution.py:258
  11.9 11.6 %collective-permute-start.2 = (f32[512,640]{1,0:T(8,128)S(1)}, f32[512,640]{1,0:T(8,128)S(1)}, u32[]{:S(2)}, u32[]{:S(2)}) collective-permute-start(f32[512,640]{1,0:T(8,128)S(1)} %get-tuple-element.44), channel_id=1, source_target_pairs={{0,1},{1,0},{2,3},{3,2},{4,5},{5,4},{6,7},{7,6},{8,9},{9,8},{10,11... | collective-permute-start | bytes 3932168 | tf_op jit(solution)/shard_map/ppermute | solution.py:258
  14.6 12.6 %collective-permute-start.3 = (f32[512,640]{1,0:T(8,128)S(1)}, f32[512,640]{1,0:T(8,128)S(1)}, u32[]{:S(2)}, u32[]{:S(2)}) collective-permute-start(f32[512,640]{1,0:T(8,128)S(1)} %get-tuple-element.47), channel_id=1, source_target_pairs={{0,1},{1,0},{2,3},{3,2},{4,5},{5,4},{6,7},{7,6},{8,9},{9,8},{10,11... | collective-permute-start | bytes 3932168 | tf_op jit(solution)/shard_map/ppermute | solution.py:258
  14.7 13.8 %collective-permute-start.4 = (f32[512,640]{1,0:T(8,128)S(1)}, f32[512,640]{1,0:T(8,128)S(1)}, u32[]{:S(2)}, u32[]{:S(2)}) collective-permute-start(f32[512,640]{1,0:T(8,128)S(1)} %get-tuple-element.48), channel_id=1, source_target_pairs={{0,1},{1,0},{2,3},{3,2},{4,5},{5,4},{6,7},{7,6},{8,9},{9,8},{10,11... | collective-permute-start | bytes 3932168 | tf_op jit(solution)/shard_map/ppermute | solution.py:258
  18.7 18.2 %collective-permute-start.5 = (bf16[520,640]{1,0:T(8,128)(2,1)S(1)}, bf16[520,640]{1,0:T(8,128)(2,1)S(1)}, u32[]{:S(2)}, u32[]{:S(2)}) collective-permute-start(bf16[520,640]{1,0:T(8,128)(2,1)S(1)} %shard_map.50.refs_0_), channel_id=1, source_target_pairs={{0,2},{1,3},{2,0},{3,1},{4,6},{5,7},{6,4},{7,5},{8,10},{9,11},{10,... | collective-permute-start | bytes 1996808 | tf_op jit(solution)/shard_map/ppermute | solution.py:258
  21.3 7.5 %copy-start = (bf16[3,960,640]{2,1,0:T(8,128)(2,1)S(1)}, bf16[3,960,640]{2,1,0:T(8,128)(2,1)}, u32[]{:S(2)}) copy-start(bf16[3,960,640]{2,1,0:T(8,128)(2,1)} %get-tuple-element.46.refs_3_) | copy-start | bytes 11059204
  21.9 17.9 %collective-permute-start.6 = (bf16[520,640]{1,0:T(8,128)(2,1)S(1)}, bf16[520,640]{1,0:T(8,128)(2,1)S(1)}, u32[]{:S(2)}, u32[]{:S(2)}) collective-permute-start(bf16[520,640]{1,0:T(8,128)(2,1)S(1)} %shard_map.51.refs_0_), channel_id=1, source_target_pairs={{0,4},{4,0},{8,12},{12,8},{16,20},{20,16},{24,28},{28,24},{1,5},{5... | collective-permute-start | bytes 1996808 | tf_op jit(solution)/shard_map/ppermute | solution.py:258
  24.5 18.8 %collective-permute-start.7 = (bf16[136,640]{1,0:T(8,128)(2,1)S(1)}, bf16[136,640]{1,0:T(8,128)(2,1)S(1)}, u32[]{:S(2)}, u32[]{:S(2)}) collective-permute-start(bf16[136,640]{1,0:T(8,128)(2,1)S(1)} %get-tuple-element.52), channel_id=1, source_target_pairs={{0,16},{4,20},{8,24},{12,28},{16,0},{20,4},{24,8},{28,12},{1,17},{... | collective-permute-start | bytes 522248 | tf_op jit(solution)/shard_map/ppermute | solution.py:258
  27.2 16.1 %collective-permute-start.8 = (bf16[136,640]{1,0:T(8,128)(2,1)S(1)}, bf16[136,640]{1,0:T(8,128)(2,1)S(1)}, u32[]{:S(2)}, u32[]{:S(2)}) collective-permute-start(bf16[136,640]{1,0:T(8,128)(2,1)S(1)} %get-tuple-element.53), channel_id=1, source_target_pairs={{0,24},{4,28},{8,16},{12,20},{16,8},{20,12},{24,0},{28,4},{1,25},{... | collective-permute-start | bytes 522248 | tf_op jit(solution)/shard_map/ppermute | solution.py:258
  28.5 14.8 %collective-permute-start.9 = (bf16[136,640]{1,0:T(8,128)(2,1)S(1)}, bf16[136,640]{1,0:T(8,128)(2,1)S(1)}, u32[]{:S(2)}, u32[]{:S(2)}) collective-permute-start(bf16[136,640]{1,0:T(8,128)(2,1)S(1)} %get-tuple-element.54), channel_id=1, source_target_pairs={{0,8},{4,12},{8,0},{12,4},{16,24},{20,28},{24,16},{28,20},{1,9},{5... | collective-permute-start | bytes 522248 | tf_op jit(solution)/shard_map/ppermute | solution.py:258
  37.9 12.2 %collective-permute-start.10 = (bf16[264,640]{1,0:T(8,128)(2,1)S(1)}, bf16[264,640]{1,0:T(8,128)(2,1)S(1)}, u32[]{:S(2)}, u32[]{:S(2)}) collective-permute-start(bf16[264,640]{1,0:T(8,128)(2,1)S(1)} %shard_map.54.refs_0_), channel_id=1, source_target_pairs={{0,4},{4,0},{8,12},{12,8},{16,20},{20,16},{24,28},{28,24},{1,5},{5... | collective-permute-start | bytes 1013768 | tf_op jit(solution)/shard_map/ppermute | solution.py:258
  40.8 9.3 %collective-permute-start.11 = (bf16[264,640]{1,0:T(8,128)(2,1)S(1)}, bf16[264,640]{1,0:T(8,128)(2,1)S(1)}, u32[]{:S(2)}, u32[]{:S(2)}) collective-permute-start(bf16[264,640]{1,0:T(8,128)(2,1)S(1)} %shard_map.55.refs_0_), channel_id=1, source_target_pairs={{0,2},{1,3},{2,0},{3,1},{4,6},{5,7},{6,4},{7,5},{8,10},{9,11},{10,... | collective-permute-start | bytes 1013768 | tf_op jit(solution)/shard_map/ppermute | solution.py:258
  44.3 13.5 %copy-start.2 = (f32[640]{0:T(1024)S(1)}, f32[640]{0:T(1024)}, u32[]{:S(2)}) copy-start(f32[640]{0:T(1024)} %param.6) | copy-start | bytes 7684
  44.3 13.7 %copy-start.3 = (f32[8]{0:T(128)S(1)}, f32[8]{0:T(128)}, u32[]{:S(2)}) copy-start(f32[8]{0:T(128)} %param.7) | copy-start | bytes 100
  44.3 11.3 %collective-permute-start.12 = (bf16[72,640]{1,0:T(8,128)(2,1)S(1)}, bf16[72,640]{1,0:T(8,128)(2,1)S(1)}, u32[]{:S(2)}, u32[]{:S(2)}) collective-permute-start(bf16[72,640]{1,0:T(8,128)(2,1)S(1)} %get-tuple-element.55.refs_0_), channel_id=1, source_target_pairs={{0,4},{4,0},{8,12},{12,8},{16,20},{20,16},{24,28},{28,24},{1,5},{5... | collective-permute-start | bytes 276488 | tf_op jit(solution)/shard_map/ppermute | solution.py:258
  51.3 14.4 %collective-permute-start.13 = (bf16[136,640]{1,0:T(8,128)(2,1)S(1)}, bf16[136,640]{1,0:T(8,128)(2,1)S(1)}, u32[]{:S(2)}, u32[]{:S(2)}) collective-permute-start(bf16[136,640]{1,0:T(8,128)(2,1)S(1)} %get-tuple-element.57.refs_0_), channel_id=1, source_target_pairs={{0,16},{4,20},{8,24},{12,28},{16,0},{20,4},{24,8},{28,12},{1,17},{... | collective-permute-start | bytes 522248 | tf_op jit(solution)/shard_map/ppermute | solution.py:258
  54.0 11.7 %collective-permute-start.14 = (bf16[136,640]{1,0:T(8,128)(2,1)S(1)}, bf16[136,640]{1,0:T(8,128)(2,1)S(1)}, u32[]{:S(2)}, u32[]{:S(2)}) collective-permute-start(bf16[136,640]{1,0:T(8,128)(2,1)S(1)} %get-tuple-element.61), channel_id=1, source_target_pairs={{0,24},{4,28},{8,16},{12,20},{16,8},{20,12},{24,0},{28,4},{1,25},{... | collective-permute-start | bytes 522248 | tf_op jit(solution)/shard_map/ppermute | solution.py:258
  55.3 10.6 %collective-permute-start.15 = (bf16[136,640]{1,0:T(8,128)(2,1)S(1)}, bf16[136,640]{1,0:T(8,128)(2,1)S(1)}, u32[]{:S(2)}, u32[]{:S(2)}) collective-permute-start(bf16[136,640]{1,0:T(8,128)(2,1)S(1)} %get-tuple-element.62), channel_id=1, source_target_pairs={{0,8},{4,12},{8,0},{12,4},{16,24},{20,28},{24,16},{28,20},{1,9},{5... | collective-permute-start | bytes 522248 | tf_op jit(solution)/shard_map/ppermute | solution.py:258
  56.2 10.0 %collective-permute-start.16 = (bf16[40,640]{1,0:T(8,128)(2,1)S(1)}, bf16[40,640]{1,0:T(8,128)(2,1)S(1)}, u32[]{:S(2)}, u32[]{:S(2)}) collective-permute-start(bf16[40,640]{1,0:T(8,128)(2,1)S(1)} %get-tuple-element.64), channel_id=1, source_target_pairs={{0,2},{1,3},{2,0},{3,1},{4,6},{5,7},{6,4},{7,5},{8,10},{9,11},{10,... | collective-permute-start | bytes 153608 | tf_op jit(solution)/shard_map/ppermute | solution.py:258

commit v6 on v5

--- a/solution.py
+++ b/solution.py
@@ -69,7 +69,7 @@
 
 def home_planes(place):
     x, core = place[0], place[1]
-    return (2 * core, x), (2 * core + 1, 0), (2 * core + 1, 1)
+    return (2 * core, x), (2 * core + 1, 0), (2 * core + 1, 1), (2 * core, 1 - x)
 
 
 def front_kernel(place, wide, amp, turned, out, flat, far, held, sem, far_sem, *, block, far_block, unit, own_rows, tiles_y, tiles_z):
@@ -179,6 +179,22 @@
         out_b[here, :] = core_b[here, :] + dot(pl.multiple_of(y * rows, 16), rows, 1 + xx)
 
 
+def edge_kernel(place, turned, far, out, held, sem, *, first, tiles_y, tiles_z):
+    x = place[0]
+    copies = [pltpu.make_async_copy(far.at[slot], held.at[slot], sem.at[slot]) for slot in range(4)]
+    for copy in copies:
+        copy.start()
+    for slot, (xx, i) in enumerate(((x, 0), (0, 1), (1, 1), (1 - x, 0))):
+        copies[slot].wait()
+        got = jnp.dot(
+            turned[pl.ds(first, tiles_y * tiles_z * EDGE), :], held[slot], preferred_element_type=F32
+        )
+        for z in range(tiles_z):
+            for y in range(tiles_y):
+                at = pl.multiple_of((((z * tiles_y + y) * 2 + xx) * 2 + i) * EDGE, EDGE)
+                out[pl.ds(at, EDGE), :] = got[(z * tiles_y + y) * EDGE :][:EDGE]
+
+
 def first_kernel(own, core, out):
     encode(out, own[...] + core[pl.ds(0, own.shape[0]), :])
 
@@ -265,7 +281,7 @@
     depth, virt = k * c, integrals.shape[2]
     own_pairs, own_rows = pairs // ka_size, virt // tile_size
     tiles_y, tiles_z = 2, tile_size // 2
-    hops = [hop for hop in range(2, tiles_z)] + [1]
+    hops = [2, 1] + [hop for hop in range(3, tiles_z)]
     bulk = own_rows - EDGE
     rows = bulk * tiles_z
     edges = EDGE * tiles_y * own_pairs * 2
@@ -284,12 +300,12 @@
         functools.partial(
             front_kernel, block=block, far_block=far_block, unit=32, own_rows=own_rows, tiles_y=tiles_y, tiles_z=tiles_z
         ),
-        [pltpu.VMEM((virt, depth), BF16), full(2 * rows), held, pltpu.HBM((3, depth, cols), BF16)],
+        [pltpu.VMEM((virt, depth), BF16), full(2 * rows), held, pltpu.HBM((4, depth, cols), BF16)],
         place, wide, amplitudes.reshape(depth, pairs, cols), specs=[SCALAR, WHOLE, FAR], room=40, out_specs=[WHOLE] * 3 + [FAR],
         scratch=[
             pltpu.VMEM((depth, pairs, cols), BF16),
             pltpu.SemaphoreType.DMA((depth // block,)),
-            pltpu.SemaphoreType.DMA((3, depth // far_block)),
+            pltpu.SemaphoreType.DMA((4, depth // far_block)),
         ],
     )
 
@@ -307,11 +323,16 @@
     g_b, g_c = swap(c_b, "ka", 1), swap(c_c, "ka", 1)
     c_ah, c_bh, flat = products(flat, [("core", "a_home")], [("core", "b_home")])
     g_ah, g_bh = swap(c_ah, "ka", 1), swap(c_bh, "ka", 1)
-    o_a, o_b, o_c, flat = products(flat, *([("own", part)] for part in ("a_away", "b_away", "c")))
+    o_a, o_b, flat = products(flat, *([("own", part)] for part in ("a_away", "b_away")))
     (send_a,) = call(first_kernel, [coded(2 * rows)], o_a, g_a)
     got_a = swap(send_a, "ka", 2)
     (send_b,) = call(first_kernel, [coded(2 * rows)], o_b, g_b, after=[send_a])
     got_b = swap(send_b, "tile", 1)
+    (o_c,) = call(
+        functools.partial(edge_kernel, first=2 * rows, tiles_y=tiles_y, tiles_z=tiles_z),
+        [full(tiles_z * edges)], place, turned, far, specs=[SCALAR, WHOLE, FAR], after=[send_b], room=16,
+        scratch=[pltpu.VMEM((4, depth, cols), BF16), pltpu.SemaphoreType.DMA((4,))],
+    )
     keep_c, *sends = call(
         functools.partial(spread_kernel, rows=edges, count=tiles_z, base=0),
         [full(edges)] + [coded(edges)] * (tiles_z - 1), place, o_c, g_c,

time: 68.2 us -> 67.5 us (0.990)
  waiting for transfers between devices: 16.6 us -> 12.8 us
  Pallas kernels: 28.6 us -> 31.4 us
    ppermute x17, waiting for transfers between devices: 16.6 us -> 12.8 us  [swap(): lax.ppermute(value, axis, [(i, i ^ bit) for i in range(lax.axis_size(axis...]
    pallas_call x17 -> x18, Pallas kernels: 28.6 us -> 31.4 us  [call(): pl.pallas_call(body, in_specs=[pl.BlockSpec(memory_space=pl.ANY)] * count...]
  transfers between devices with their start and end apart: 17 -> 17, of which waited for: 4 -> 5; matrix products, arithmetic and copies ran while one was open for 0% -> 0% of each run, Pallas kernels for 30% -> 34%
where the time goes in v6:
time: 67.5 us; the launch traced here: 66.3 us
  Pallas kernels  31.4 us (47%)
  starting transfers between devices  20.3 us (30%)
  waiting for transfers between devices  12.8 us (19%)
  local copies, waits for them, and re-layouts  1.56 us (2%)
    pallas_call x18, Pallas kernels, call(): pl.pallas_call(body, in_specs=[pl.BlockSpec(memory_space=pl.ANY)] * count...  31.4 us
    ppermute x17, starting transfers between devices, swap(): lax.ppermute(value, axis, [(i, i ^ bit) for i in range(lax.axis_size(axis...  20.3 us
    ppermute x17, waiting for transfers between devices, swap(): lax.ppermute(value, axis, [(i, i ^ bit) for i in range(lax.axis_size(axis...  12.8 us
  transfers between devices with their start and end apart: 17, of which 5 were waited for; matrix products, arithmetic and copies ran while one was open for 0% of the time, Pallas kernels for 34%

profile of v6, /device:TPU:0, one launch (start us, length us, event | category | flops | bytes accessed | tf_op | source)
XLA Modules:
  0.0 66.3 jit_solution(249447279691851260)
XLA Ops:
  0.0 0.1 pad_add_fusion.refs_0_.refs_1_
  0.1 1.3 %copy-done = bf16[80,12,640]{2,0,1:T(8,128)(2,1)S(1)} copy-done((bf16[80,12,640]{2,0,1:T(8,128)(2,1)S(1)}, bf16[80,12,640]{2,0,1:T(8,128)(2,1)}, u32[]{:S(2)}) %copy-start) | copy-done | bytes 1228824
  1.4 8.0 %shard_map.46 = (bf16[640,960]{1,0:T(8,128)(2,1)S(1)}, f32[512,640]{1,0:T(8,128)S(1)}, bf16[4,960,1280]{2,1,0:T(8,128)(2,1)S(1)}, bf16[4,960,640]{2,1,0:T(8,128)(2,1)}) custom-call(s32[4]{0:T(128)S(1)} %pad_add_fusion.refs_0_.refs_1_, bf16[960,640]{1,0:T(8,128)(2,1)S(1)} %bitcast.12, bf16[960,8,640]{2,1,0:T(8,128)(2,1)} %bitcast.13), custom_call_target="tpu_custom_call" | custom-call | flops 1000 | bytes 1000 | tf_op jit(solution)/shard_map/pallas_call | solution.py:51
  9.3 0.5 collective-permute-start
  9.9 2.1 %shard_map.47 = (f32[512,640]{1,0:T(8,128)S(1)}, f32[512,640]{1,0:T(8,128)S(1)}, bf16[4,960,1280]{2,1,0:T(8,128)(2,1)S(1)}) custom-call(s32[4]{0:T(128)S(1)} %pad_add_fusion.refs_0_.refs_1_, bf16[640,960]{1,0:T(8,128)(2,1)S(1)} %get-tuple-element.34.refs_1_.refs_2_, bf16[4,960,1280]{2,1,0:T(8,128)(2,1)S(1)} %get-tuple-element.35.refs_2_), custom_call_target="tpu_custom_call", output_to_operand_aliasing={{2}: (2, {})} | custom-call | flops 1000 | bytes 1000 | tf_op jit(solution)/shard_map/pallas_call | solution.py:51
  11.9 0.1 collective-permute-start.1
  12.1 0.5 collective-permute-start.2
  12.5 2.2 %shard_map.48 = (f32[512,640]{1,0:T(8,128)S(1)}, f32[512,640]{1,0:T(8,128)S(1)}, bf16[4,960,1280]{2,1,0:T(8,128)(2,1)S(1)}) custom-call(s32[4]{0:T(128)S(1)} %pad_add_fusion.refs_0_.refs_1_, bf16[640,960]{1,0:T(8,128)(2,1)S(1)} %get-tuple-element.34.refs_1_.refs_2_, bf16[4,960,1280]{2,1,0:T(8,128)(2,1)S(1)} %get-tuple-element.36.refs_2_), custom_call_target="tpu_custom_call", output_to_operand_aliasing={{2}: (2, {})} | custom-call | flops 1000 | bytes 1000 | tf_op jit(solution)/shard_map/pallas_call | solution.py:51
  14.7 0.1 collective-permute-start.3
  14.9 0.4 collective-permute-start.4
  15.3 2.2 %shard_map.49 = (f32[512,640]{1,0:T(8,128)S(1)}, f32[512,640]{1,0:T(8,128)S(1)}, bf16[4,960,1280]{2,1,0:T(8,128)(2,1)S(1)}) custom-call(s32[4]{0:T(128)S(1)} %pad_add_fusion.refs_0_.refs_1_, bf16[640,960]{1,0:T(8,128)(2,1)S(1)} %get-tuple-element.34.refs_1_.refs_2_, bf16[4,960,1280]{2,1,0:T(8,128)(2,1)S(1)} %get-tuple-element.37.refs_2_), custom_call_target="tpu_custom_call", output_to_operand_aliasing={{2}: (2, {})} | custom-call | flops 1000 | bytes 1000 | tf_op jit(solution)/shard_map/pallas_call | solution.py:51
  17.5 0.6 shard_map.50.refs_0_
  18.1 2.6 %collective-permute-start.5 = (bf16[520,640]{1,0:T(8,128)(2,1)S(1)}, bf16[520,640]{1,0:T(8,128)(2,1)S(1)}, u32[]{:S(2)}, u32[]{:S(2)}) collective-permute-start(bf16[520,640]{1,0:T(8,128)(2,1)S(1)} %shard_map.50.refs_0_), channel_id=1, source_target_pairs={{0,2},{1,3},{2,0},{3,1},{4,6},{5,7},{6,4},{7,5},{8,10},{9,11},{10,... | collective-permute-start | bytes 1996808 | tf_op jit(solution)/shard_map/ppermute | solution.py:274
  20.8 0.0 collective-permute-done.1.refs_2_
  20.8 0.6 shard_map.51.refs_0_
  21.4 1.6 %collective-permute-start.6 = (bf16[520,640]{1,0:T(8,128)(2,1)S(1)}, bf16[520,640]{1,0:T(8,128)(2,1)S(1)}, u32[]{:S(2)}, u32[]{:S(2)}) collective-permute-start(bf16[520,640]{1,0:T(8,128)(2,1)S(1)} %shard_map.51.refs_0_), channel_id=1, source_target_pairs={{0,4},{4,0},{8,12},{12,8},{16,20},{20,16},{24,28},{28,24},{1,5},{5... | collective-permute-start | bytes 1996808 | tf_op jit(solution)/shard_map/ppermute | solution.py:274
  23.0 3.5 %shard_map.52.refs_2_ = f32[512,640]{1,0:T(8,128)S(1)} custom-call(bf16[520,640]{1,0:T(8,128)(2,1)S(1)} %shard_map.51.refs_0_, s32[4]{0:T(128)S(1)} %pad_add_fusion.refs_0_.refs_1_, bf16[640,960]{1,0:T(8,128)(2,1)S(1)} %get-tuple-element.34.refs_1_.refs_2_, bf16[4,960,640]{2,1,0:T(8,128)(2,1)S(1)} %bitcast.11), custom_call_target="tpu_custom_call" | custom-call | flops 1000 | bytes 1000 | tf_op jit(solution)/shard_map/pallas_call | solution.py:51
  26.5 1.0 %shard_map.53 = (f32[128,640]{1,0:T(8,128)S(1)}, bf16[136,640]{1,0:T(8,128)(2,1)S(1)}, bf16[136,640]{1,0:T(8,128)(2,1)S(1)}, bf16[136,640]{1,0:T(8,128)(2,1)S(1)}) custom-call(bf16[520,640]{1,0:T(8,128)(2,1)S(1)} %shard_map.51.refs_0_, s32[4]{0:T(128)S(1)} %pad_add_fusion.refs_0_.refs_1_, f32[512,640]{1,0:T(8,128)S(1)} %shard_map.52.refs_2_, ...), custom_call_target="tpu_custom_call" | custom-call | flops 1000 | bytes 1000 | tf_op jit(solution)/shard_map/pallas_call | solution.py:51
  27.5 2.7 %collective-permute-start.7 = (bf16[136,640]{1,0:T(8,128)(2,1)S(1)}, bf16[136,640]{1,0:T(8,128)(2,1)S(1)}, u32[]{:S(2)}, u32[]{:S(2)}) collective-permute-start(bf16[136,640]{1,0:T(8,128)(2,1)S(1)} %get-tuple-element.50), channel_id=1, source_target_pairs={{0,16},{4,20},{8,24},{12,28},{16,0},{20,4},{24,8},{28,12},{1,17},{... | collective-permute-start | bytes 522248 | tf_op jit(solution)/shard_map/ppermute | solution.py:274
  30.1 1.6 %collective-permute-start.8 = (bf16[136,640]{1,0:T(8,128)(2,1)S(1)}, bf16[136,640]{1,0:T(8,128)(2,1)S(1)}, u32[]{:S(2)}, u32[]{:S(2)}) collective-permute-start(bf16[136,640]{1,0:T(8,128)(2,1)S(1)} %get-tuple-element.51), channel_id=1, source_target_pairs={{0,8},{4,12},{8,0},{12,4},{16,24},{20,28},{24,16},{28,20},{1,9},{5... | collective-permute-start | bytes 522248 | tf_op jit(solution)/shard_map/ppermute | solution.py:274
  31.7 0.2 collective-permute-start.9
  31.9 3.6 %shard_map.54 = (f32[512,640]{1,0:T(8,128)S(1)}, f32[512,640]{1,0:T(8,128)S(1)}) custom-call(f32[128,640]{1,0:T(8,128)S(1)} %get-tuple-element.44.refs_0_.refs_2_, s32[4]{0:T(128)S(1)} %pad_add_fusion.refs_0_.refs_1_, bf16[640,960]{1,0:T(8,128)(2,1)S(1)} %get-tuple-element.34.refs_1_.refs_2_, bf16[4,960,640]{2,1,0:T(8,128)(2,1)S(1)} %bitcast.11, ...), custom_call_target="tpu_custom_call" | custom-call | flops 1000 | bytes 1000 | tf_op jit(solution)/shard_map/pallas_call | solution.py:51
  35.6 0.7 %collective-permute-done.5.refs_2_.refs_3_ = bf16[520,640]{1,0:T(8,128)(2,1)S(1)} collective-permute-done((bf16[520,640]{1,0:T(8,128)(2,1)S(1)}, bf16[520,640]{1,0:T(8,128)(2,1)S(1)}, u32[]{:S(2)}, u32[]{:S(2)}) %collective-permute-start.5) | collective-permute-done | bytes 665632 | tf_op jit(solution)/shard_map/ppermute | solution.py:274
  36.3 1.1 %shard_map.55.refs_0_ = bf16[264,640]{1,0:T(8,128)(2,1)S(1)} custom-call(s32[4]{0:T(128)S(1)} %pad_add_fusion.refs_0_.refs_1_, f32[512,640]{1,0:T(8,128)S(1)} %get-tuple-element.47.refs_1_.refs_2_, bf16[520,640]{1,0:T(8,128)(2,1)S(1)} %collective-permute-done.5.refs_2_.refs_3_), custom_call_target="tpu_custom_call" | custom-call | flops 1000 | bytes 1000 | tf_op jit(solution)/shard_map/pallas_call | solution.py:51
  37.4 1.9 %collective-permute-start.10 = (bf16[264,640]{1,0:T(8,128)(2,1)S(1)}, bf16[264,640]{1,0:T(8,128)(2,1)S(1)}, u32[]{:S(2)}, u32[]{:S(2)}) collective-permute-start(bf16[264,640]{1,0:T(8,128)(2,1)S(1)} %shard_map.55.refs_0_), channel_id=1, source_target_pairs={{0,4},{4,0},{8,12},{12,8},{16,20},{20,16},{24,28},{28,24},{1,5},{5... | collective-permute-start | bytes 1013768 | tf_op jit(solution)/shard_map/ppermute | solution.py:274
  39.2 1.1 %shard_map.56.refs_0_ = bf16[264,640]{1,0:T(8,128)(2,1)S(1)} custom-call(bf16[264,640]{1,0:T(8,128)(2,1)S(1)} %shard_map.55.refs_0_, s32[4]{0:T(128)S(1)} %pad_add_fusion.refs_0_.refs_1_, f32[512,640]{1,0:T(8,128)S(1)} %get-tuple-element.48.refs_2_.refs_4_, bf16[520,640]{1,0:T(8,128)(2,1)S(1)} %collective-permute-done.6.refs_3_.refs_5_), custom_call_target="tpu_custom_call" | custom-call | flops 1000 | bytes 1000 | tf_op jit(solution)/shard_map/pallas_call | solution.py:51
  40.3 1.5 %collective-permute-start.11 = (bf16[264,640]{1,0:T(8,128)(2,1)S(1)}, bf16[264,640]{1,0:T(8,128)(2,1)S(1)}, u32[]{:S(2)}, u32[]{:S(2)}) collective-permute-start(bf16[264,640]{1,0:T(8,128)(2,1)S(1)} %shard_map.56.refs_0_), channel_id=1, source_target_pairs={{0,2},{1,3},{2,0},{3,1},{4,6},{5,7},{6,4},{7,5},{8,10},{9,11},{10,... | collective-permute-start | bytes 1013768 | tf_op jit(solution)/shard_map/ppermute | solution.py:274
  41.8 0.9 %shard_map.57 = (f32[256,640]{1,0:T(8,128)S(1)}, f32[256,640]{1,0:T(8,128)S(1)}) custom-call(bf16[264,640]{1,0:T(8,128)(2,1)S(1)} %shard_map.56.refs_0_, s32[4]{0:T(128)S(1)} %pad_add_fusion.refs_0_.refs_1_, f32[512,640]{1,0:T(8,128)S(1)} %get-tuple-element.47.refs_1_.refs_2_, bf16[520,640]{1,0:T(8,128)(2,1)S(1)} %collective-permute-done.5.refs_2_.refs_3_, ...), custom_call_target="tpu_custom_call" | custom-call | flops 1000 | bytes 1000 | tf_op jit(solution)/shard_map/pallas_call | solution.py:51
  42.8 0.5 collective-permute-done.9.refs_5_
  43.2 0.9 %shard_map.58 = (f32[64,640]{1,0:T(8,128)S(1)}, bf16[72,640]{1,0:T(8,128)(2,1)S(1)}) custom-call(f32[256,640]{1,0:T(8,128)S(1)} %get-tuple-element.49.refs_0_.refs_2_, s32[4]{0:T(128)S(1)} %pad_add_fusion.refs_0_.refs_1_, f32[128,640]{1,0:T(8,128)S(1)} %get-tuple-element.44.refs_0_.refs_2_, bf16[136,640]{1,0:T(8,128)(2,1)S(1)} %collective-permute-done.7.refs_3_, ...), custom_call_target="tpu_custom_call" | custom-call | flops 34359738368 | bytes 1000 | tf_op jit(solution)/shard_map/pallas_call | solution.py:51
  44.2 0.0 copy-start.1
  44.2 0.0 copy-start.2
  44.2 0.6 collective-permute-start.12
  44.8 4.8 %collective-permute-done.11.refs_5_ = bf16[264,640]{1,0:T(8,128)(2,1)S(1)} collective-permute-done((bf16[264,640]{1,0:T(8,128)(2,1)S(1)}, bf16[264,640]{1,0:T(8,128)(2,1)S(1)}, u32[]{:S(2)}, u32[]{:S(2)}) %collective-permute-start.11) | collective-permute-done | bytes 337952 | tf_op jit(solution)/shard_map/ppermute | solution.py:274
  49.6 1.2 %shard_map.59 = (bf16[136,640]{1,0:T(8,128)(2,1)S(1)}, bf16[136,640]{1,0:T(8,128)(2,1)S(1)}, bf16[136,640]{1,0:T(8,128)(2,1)S(1)}) custom-call(bf16[72,640]{1,0:T(8,128)(2,1)S(1)} %get-tuple-element.53.refs_0_, s32[4]{0:T(128)S(1)} %pad_add_fusion.refs_0_.refs_1_, f32[256,640]{1,0:T(8,128)S(1)} %get-tuple-element.49.refs_0_.refs_2_, ...), custom_call_target="tpu_custom_call" | custom-call | flops 1000 | bytes 1000 | tf_op jit(solution)/shard_map/pallas_call | solution.py:51
  50.8 2.7 %collective-permute-start.13 = (bf16[136,640]{1,0:T(8,128)(2,1)S(1)}, bf16[136,640]{1,0:T(8,128)(2,1)S(1)}, u32[]{:S(2)}, u32[]{:S(2)}) collective-permute-start(bf16[136,640]{1,0:T(8,128)(2,1)S(1)} %get-tuple-element.55.refs_0_), channel_id=1, source_target_pairs={{0,16},{4,20},{8,24},{12,28},{16,0},{20,4},{24,8},{28,12},{1,17},{... | collective-permute-start | bytes 522248 | tf_op jit(solution)/shard_map/ppermute | solution.py:274
  53.4 1.6 %collective-permute-start.14 = (bf16[136,640]{1,0:T(8,128)(2,1)S(1)}, bf16[136,640]{1,0:T(8,128)(2,1)S(1)}, u32[]{:S(2)}, u32[]{:S(2)}) collective-permute-start(bf16[136,640]{1,0:T(8,128)(2,1)S(1)} %get-tuple-element.59), channel_id=1, source_target_pairs={{0,8},{4,12},{8,0},{12,4},{16,24},{20,28},{24,16},{28,20},{1,9},{5... | collective-permute-start | bytes 522248 | tf_op jit(solution)/shard_map/ppermute | solution.py:274
  55.0 0.2 collective-permute-start.15
  55.2 0.6 shard_map.60
  55.9 1.5 %collective-permute-start.16 = (bf16[40,640]{1,0:T(8,128)(2,1)S(1)}, bf16[40,640]{1,0:T(8,128)(2,1)S(1)}, u32[]{:S(2)}, u32[]{:S(2)}) collective-permute-start(bf16[40,640]{1,0:T(8,128)(2,1)S(1)} %get-tuple-element.62), channel_id=1, source_target_pairs={{0,2},{1,3},{2,0},{3,1},{4,6},{5,7},{6,4},{7,5},{8,10},{9,11},{10,... | collective-permute-start | bytes 153608 | tf_op jit(solution)/shard_map/ppermute | solution.py:274
  57.4 0.1 dynamic-slice_bitcast_fusion
  57.5 0.1 copy.8.refs_6_
  57.6 0.1 dynamic_slice.7.refs_8_
  57.7 0.7 %shard_map.61 = (f32[128,640]{1,0:T(8,128)S(1)}, f32[2,80,640]{2,1,0:T(8,128)S(1)}) custom-call(f32[32,640]{1,0:T(8,128)S(1)} %get-tuple-element.57.refs_0_.refs_1_, s32[4]{0:T(128)S(1)} %pad_add_fusion.refs_0_.refs_1_, f32[256,640]{1,0:T(8,128)S(1)} %get-tuple-element.49.refs_0_.refs_2_, bf16[264,640]{1,0:T(8,128)(2,1)S(1)} %collective-permute-done.10.refs_3_, ...), custom_call_target="tpu_custom_call" | custom-call | flops 1000 | bytes 1000 | tf_op jit(solution)/shard_map/pallas_call | solution.py:51
  58.4 4.9 %collective-permute-done.13.refs_1_ = bf16[136,640]{1,0:T(8,128)(2,1)S(1)} collective-permute-done((bf16[136,640]{1,0:T(8,128)(2,1)S(1)}, bf16[136,640]{1,0:T(8,128)(2,1)S(1)}, u32[]{:S(2)}, u32[]{:S(2)}) %collective-permute-start.13) | collective-permute-done | bytes 174112 | tf_op jit(solution)/shard_map/ppermute | solution.py:274
  63.3 1.9 %collective-permute-done.15.refs_3_ = bf16[136,640]{1,0:T(8,128)(2,1)S(1)} collective-permute-done((bf16[136,640]{1,0:T(8,128)(2,1)S(1)}, bf16[136,640]{1,0:T(8,128)(2,1)S(1)}, u32[]{:S(2)}, u32[]{:S(2)}) %collective-permute-start.15) | collective-permute-done | bytes 174112 | tf_op jit(solution)/shard_map/ppermute | solution.py:274
  65.2 0.3 shard_map.62.refs_0_
  65.6 0.7 %shard_map.63 = bf16[2,80,640]{2,1,0:T(8,128)(2,1)} custom-call(bf16[128,640]{1,0:T(8,128)(2,1)S(1)} %shard_map.62.refs_0_, f32[32,640]{1,0:T(8,128)S(1)} %get-tuple-element.57.refs_0_.refs_1_, bf16[40,640]{1,0:T(8,128)(2,1)S(1)} %collective-permute-done.16.refs_2_, f32[2,80,640]{2,1,0:T(8,128)S(1)} %get-tuple-element.61.refs_4_.refs_3_), custom_call_target="tpu_custom_call" | custom-call | flops 1000 | bytes 1000 | tf_op jit(solution)/shard_map/pallas_call | solution.py:51
  (20 shorter events, 0.0 us)
Async XLA Ops:
  0.1 1.3 %copy-start = (bf16[80,12,640]{2,0,1:T(8,128)(2,1)S(1)}, bf16[80,12,640]{2,0,1:T(8,128)(2,1)}, u32[]{:S(2)}) copy-start(bf16[80,12,640]{2,0,1:T(8,128)(2,1)} %param.4) | copy-start | bytes 3686404
  9.3 8.2 %collective-permute-start = (f32[512,640]{1,0:T(8,128)S(1)}, f32[512,640]{1,0:T(8,128)S(1)}, u32[]{:S(2)}, u32[]{:S(2)}) collective-permute-start(f32[512,640]{1,0:T(8,128)S(1)} %get-tuple-element.39), channel_id=1, source_target_pairs={{0,1},{1,0},{2,3},{3,2},{4,5},{5,4},{6,7},{7,6},{8,9},{9,8},{10,11... | collective-permute-start | bytes 3932168 | tf_op jit(solution)/shard_map/ppermute | solution.py:274
  11.9 8.8 %collective-permute-start.1 = (f32[512,640]{1,0:T(8,128)S(1)}, f32[512,640]{1,0:T(8,128)S(1)}, u32[]{:S(2)}, u32[]{:S(2)}) collective-permute-start(f32[512,640]{1,0:T(8,128)S(1)} %get-tuple-element.41), channel_id=1, source_target_pairs={{0,1},{1,0},{2,3},{3,2},{4,5},{5,4},{6,7},{7,6},{8,9},{9,8},{10,11... | collective-permute-start | bytes 3932168 | tf_op jit(solution)/shard_map/ppermute | solution.py:274
  12.1 14.4 %collective-permute-start.2 = (f32[512,640]{1,0:T(8,128)S(1)}, f32[512,640]{1,0:T(8,128)S(1)}, u32[]{:S(2)}, u32[]{:S(2)}) collective-permute-start(f32[512,640]{1,0:T(8,128)S(1)} %get-tuple-element.43), channel_id=1, source_target_pairs={{0,1},{1,0},{2,3},{3,2},{4,5},{5,4},{6,7},{7,6},{8,9},{9,8},{10,11... | collective-permute-start | bytes 3932168 | tf_op jit(solution)/shard_map/ppermute | solution.py:274
  12.5 10.4 %slice-start = ((s8[4915200]{0:T(1024)(128)(4,1)}), s8[4194304]{0:T(1024)(128)(4,1)S(1)}, s32[]{:S(2)}) async-start(s8[4915200]{0:T(1024)(128)(4,1)} %bitcast.10), calls=%async_computation | async-start | bytes 8388608
  14.7 15.4 %collective-permute-start.3 = (f32[512,640]{1,0:T(8,128)S(1)}, f32[512,640]{1,0:T(8,128)S(1)}, u32[]{:S(2)}, u32[]{:S(2)}) collective-permute-start(f32[512,640]{1,0:T(8,128)S(1)} %get-tuple-element.45), channel_id=1, source_target_pairs={{0,1},{1,0},{2,3},{3,2},{4,5},{5,4},{6,7},{7,6},{8,9},{9,8},{10,11... | collective-permute-start | bytes 3932168 | tf_op jit(solution)/shard_map/ppermute | solution.py:274
  14.9 16.8 %collective-permute-start.4 = (f32[512,640]{1,0:T(8,128)S(1)}, f32[512,640]{1,0:T(8,128)S(1)}, u32[]{:S(2)}, u32[]{:S(2)}) collective-permute-start(f32[512,640]{1,0:T(8,128)S(1)} %get-tuple-element.46), channel_id=1, source_target_pairs={{0,1},{1,0},{2,3},{3,2},{4,5},{5,4},{6,7},{7,6},{8,9},{9,8},{10,11... | collective-permute-start | bytes 3932168 | tf_op jit(solution)/shard_map/ppermute | solution.py:274
  15.3 7.6 %slice-start.1 = ((s8[4915200]{0:T(1024)(128)(4,1)}), s8[720896]{0:T(1024)(128)(4,1)S(1)}, s32[]{:S(2)}) async-start(s8[4915200]{0:T(1024)(128)(4,1)} %bitcast.10), calls=%async_computation.1 | async-start | bytes 1441792
  18.1 18.2 %collective-permute-start.5 = (bf16[520,640]{1,0:T(8,128)(2,1)S(1)}, bf16[520,640]{1,0:T(8,128)(2,1)S(1)}, u32[]{:S(2)}, u32[]{:S(2)}) collective-permute-start(bf16[520,640]{1,0:T(8,128)(2,1)S(1)} %shard_map.50.refs_0_), channel_id=1, source_target_pairs={{0,2},{1,3},{2,0},{3,1},{4,6},{5,7},{6,4},{7,5},{8,10},{9,11},{10,... | collective-permute-start | bytes 1996808 | tf_op jit(solution)/shard_map/ppermute | solution.py:274
  21.4 17.9 %collective-permute-start.6 = (bf16[520,640]{1,0:T(8,128)(2,1)S(1)}, bf16[520,640]{1,0:T(8,128)(2,1)S(1)}, u32[]{:S(2)}, u32[]{:S(2)}) collective-permute-start(bf16[520,640]{1,0:T(8,128)(2,1)S(1)} %shard_map.51.refs_0_), channel_id=1, source_target_pairs={{0,4},{4,0},{8,12},{12,8},{16,20},{20,16},{24,28},{28,24},{1,5},{5... | collective-permute-start | bytes 1996808 | tf_op jit(solution)/shard_map/ppermute | solution.py:274
  27.5 15.3 %collective-permute-start.7 = (bf16[136,640]{1,0:T(8,128)(2,1)S(1)}, bf16[136,640]{1,0:T(8,128)(2,1)S(1)}, u32[]{:S(2)}, u32[]{:S(2)}) collective-permute-start(bf16[136,640]{1,0:T(8,128)(2,1)S(1)} %get-tuple-element.50), channel_id=1, source_target_pairs={{0,16},{4,20},{8,24},{12,28},{16,0},{20,4},{24,8},{28,12},{1,17},{... | collective-permute-start | bytes 522248 | tf_op jit(solution)/shard_map/ppermute | solution.py:274
  30.1 12.7 %collective-permute-start.8 = (bf16[136,640]{1,0:T(8,128)(2,1)S(1)}, bf16[136,640]{1,0:T(8,128)(2,1)S(1)}, u32[]{:S(2)}, u32[]{:S(2)}) collective-permute-start(bf16[136,640]{1,0:T(8,128)(2,1)S(1)} %get-tuple-element.51), channel_id=1, source_target_pairs={{0,8},{4,12},{8,0},{12,4},{16,24},{20,28},{24,16},{28,20},{1,9},{5... | collective-permute-start | bytes 522248 | tf_op jit(solution)/shard_map/ppermute | solution.py:274
  31.7 11.5 %collective-permute-start.9 = (bf16[136,640]{1,0:T(8,128)(2,1)S(1)}, bf16[136,640]{1,0:T(8,128)(2,1)S(1)}, u32[]{:S(2)}, u32[]{:S(2)}) collective-permute-start(bf16[136,640]{1,0:T(8,128)(2,1)S(1)} %get-tuple-element.52), channel_id=1, source_target_pairs={{0,24},{4,28},{8,16},{12,20},{16,8},{20,12},{24,0},{28,4},{1,25},{... | collective-permute-start | bytes 522248 | tf_op jit(solution)/shard_map/ppermute | solution.py:274
  37.4 12.2 %collective-permute-start.10 = (bf16[264,640]{1,0:T(8,128)(2,1)S(1)}, bf16[264,640]{1,0:T(8,128)(2,1)S(1)}, u32[]{:S(2)}, u32[]{:S(2)}) collective-permute-start(bf16[264,640]{1,0:T(8,128)(2,1)S(1)} %shard_map.55.refs_0_), channel_id=1, source_target_pairs={{0,4},{4,0},{8,12},{12,8},{16,20},{20,16},{24,28},{28,24},{1,5},{5... | collective-permute-start | bytes 1013768 | tf_op jit(solution)/shard_map/ppermute | solution.py:274
  40.3 9.3 %collective-permute-start.11 = (bf16[264,640]{1,0:T(8,128)(2,1)S(1)}, bf16[264,640]{1,0:T(8,128)(2,1)S(1)}, u32[]{:S(2)}, u32[]{:S(2)}) collective-permute-start(bf16[264,640]{1,0:T(8,128)(2,1)S(1)} %shard_map.56.refs_0_), channel_id=1, source_target_pairs={{0,2},{1,3},{2,0},{3,1},{4,6},{5,7},{6,4},{7,5},{8,10},{9,11},{10,... | collective-permute-start | bytes 1013768 | tf_op jit(solution)/shard_map/ppermute | solution.py:274
  44.2 13.3 %copy-start.1 = (f32[640]{0:T(1024)S(1)}, f32[640]{0:T(1024)}, u32[]{:S(2)}) copy-start(f32[640]{0:T(1024)} %param.6) | copy-start | bytes 7684
  44.2 13.4 %copy-start.2 = (f32[8]{0:T(128)S(1)}, f32[8]{0:T(128)}, u32[]{:S(2)}) copy-start(f32[8]{0:T(128)} %param.7) | copy-start | bytes 100
  44.2 11.1 %collective-permute-start.12 = (bf16[72,640]{1,0:T(8,128)(2,1)S(1)}, bf16[72,640]{1,0:T(8,128)(2,1)S(1)}, u32[]{:S(2)}, u32[]{:S(2)}) collective-permute-start(bf16[72,640]{1,0:T(8,128)(2,1)S(1)} %get-tuple-element.53.refs_0_), channel_id=1, source_target_pairs={{0,4},{4,0},{8,12},{12,8},{16,20},{20,16},{24,28},{28,24},{1,5},{5... | collective-permute-start | bytes 276488 | tf_op jit(solution)/shard_map/ppermute | solution.py:274
  50.8 12.5 %collective-permute-start.13 = (bf16[136,640]{1,0:T(8,128)(2,1)S(1)}, bf16[136,640]{1,0:T(8,128)(2,1)S(1)}, u32[]{:S(2)}, u32[]{:S(2)}) collective-permute-start(bf16[136,640]{1,0:T(8,128)(2,1)S(1)} %get-tuple-element.55.refs_0_), channel_id=1, source_target_pairs={{0,16},{4,20},{8,24},{12,28},{16,0},{20,4},{24,8},{28,12},{1,17},{... | collective-permute-start | bytes 522248 | tf_op jit(solution)/shard_map/ppermute | solution.py:274
  53.4 9.9 %collective-permute-start.14 = (bf16[136,640]{1,0:T(8,128)(2,1)S(1)}, bf16[136,640]{1,0:T(8,128)(2,1)S(1)}, u32[]{:S(2)}, u32[]{:S(2)}) collective-permute-start(bf16[136,640]{1,0:T(8,128)(2,1)S(1)} %get-tuple-element.59), channel_id=1, source_target_pairs={{0,8},{4,12},{8,0},{12,4},{16,24},{20,28},{24,16},{28,20},{1,9},{5... | collective-permute-start | bytes 522248 | tf_op jit(solution)/shard_map/ppermute | solution.py:274
  55.0 10.2 %collective-permute-start.15 = (bf16[136,640]{1,0:T(8,128)(2,1)S(1)}, bf16[136,640]{1,0:T(8,128)(2,1)S(1)}, u32[]{:S(2)}, u32[]{:S(2)}) collective-permute-start(bf16[136,640]{1,0:T(8,128)(2,1)S(1)} %get-tuple-element.60), channel_id=1, source_target_pairs={{0,24},{4,28},{8,16},{12,20},{16,8},{20,12},{24,0},{28,4},{1,25},{... | collective-permute-start | bytes 522248 | tf_op jit(solution)/shard_map/ppermute | solution.py:274
  55.9 9.7 %collective-permute-start.16 = (bf16[40,640]{1,0:T(8,128)(2,1)S(1)}, bf16[40,640]{1,0:T(8,128)(2,1)S(1)}, u32[]{:S(2)}, u32[]{:S(2)}) collective-permute-start(bf16[40,640]{1,0:T(8,128)(2,1)S(1)} %get-tuple-element.62), channel_id=1, source_target_pairs={{0,2},{1,3},{2,0},{3,1},{4,6},{5,7},{6,4},{7,5},{8,10},{9,11},{10,... | collective-permute-start | bytes 153608 | tf_op jit(solution)/shard_map/ppermute | solution.py:274

commit v7 on v6

--- a/solution.py
+++ b/solution.py
@@ -294,7 +294,7 @@
     def coded(height):
         return shape((height + PAD, cols), BF16)
 
-    block, far_block = 320, 320
+    block, far_block = 320, 160
     held = pltpu.VMEM((pairs // 2, depth, 2 * cols), BF16)
     turned, c_a, flat, far = call(
         functools.partial(

time: 67.5 us -> 67.1 us (level)
  no operation moved by 1% of the time
where the time goes in v7:
time: 67.1 us; the launch traced here: 65.9 us
  Pallas kernels  31 us (46%)
  starting transfers between devices  20.3 us (30%)
  waiting for transfers between devices  12.8 us (19%)
  local copies, waits for them, and re-layouts  1.56 us (2%)
    pallas_call x18, Pallas kernels, call(): pl.pallas_call(body, in_specs=[pl.BlockSpec(memory_space=pl.ANY)] * count...  31 us
    ppermute x17, starting transfers between devices, swap(): lax.ppermute(value, axis, [(i, i ^ bit) for i in range(lax.axis_size(axis...  20.3 us
    ppermute x17, waiting for transfers between devices, swap(): lax.ppermute(value, axis, [(i, i ^ bit) for i in range(lax.axis_size(axis...  12.8 us
  transfers between devices with their start and end apart: 17, of which 5 were waited for; matrix products, arithmetic and copies ran while one was open for 0% of the time, Pallas kernels for 34%

profile of v7, /device:TPU:0, one launch (start us, length us, event | category | flops | bytes accessed | tf_op | source)
XLA Modules:
  0.0 65.9 jit_solution(6548471053443886289)
XLA Ops:
  0.0 0.1 pad_add_fusion.refs_0_.refs_1_
  0.1 1.3 %copy-done = bf16[80,12,640]{2,0,1:T(8,128)(2,1)S(1)} copy-done((bf16[80,12,640]{2,0,1:T(8,128)(2,1)S(1)}, bf16[80,12,640]{2,0,1:T(8,128)(2,1)}, u32[]{:S(2)}) %copy-start) | copy-done | bytes 1228824
  1.4 7.6 %shard_map.46 = (bf16[640,960]{1,0:T(8,128)(2,1)S(1)}, f32[512,640]{1,0:T(8,128)S(1)}, bf16[4,960,1280]{2,1,0:T(8,128)(2,1)S(1)}, bf16[4,960,640]{2,1,0:T(8,128)(2,1)}) custom-call(s32[4]{0:T(128)S(1)} %pad_add_fusion.refs_0_.refs_1_, bf16[960,640]{1,0:T(8,128)(2,1)S(1)} %bitcast.12, bf16[960,8,640]{2,1,0:T(8,128)(2,1)} %bitcast.13), custom_call_target="tpu_custom_call" | custom-call | flops 1000 | bytes 1000 | tf_op jit(solution)/shard_map/pallas_call | solution.py:51
  9.0 0.5 collective-permute-start
  9.5 2.1 %shard_map.47 = (f32[512,640]{1,0:T(8,128)S(1)}, f32[512,640]{1,0:T(8,128)S(1)}, bf16[4,960,1280]{2,1,0:T(8,128)(2,1)S(1)}) custom-call(s32[4]{0:T(128)S(1)} %pad_add_fusion.refs_0_.refs_1_, bf16[640,960]{1,0:T(8,128)(2,1)S(1)} %get-tuple-element.34.refs_1_.refs_2_, bf16[4,960,1280]{2,1,0:T(8,128)(2,1)S(1)} %get-tuple-element.35.refs_2_), custom_call_target="tpu_custom_call", output_to_operand_aliasing={{2}: (2, {})} | custom-call | flops 1000 | bytes 1000 | tf_op jit(solution)/shard_map/pallas_call | solution.py:51
  11.6 0.1 collective-permute-start.1
  11.7 0.5 collective-permute-start.2
  12.2 2.2 %shard_map.48 = (f32[512,640]{1,0:T(8,128)S(1)}, f32[512,640]{1,0:T(8,128)S(1)}, bf16[4,960,1280]{2,1,0:T(8,128)(2,1)S(1)}) custom-call(s32[4]{0:T(128)S(1)} %pad_add_fusion.refs_0_.refs_1_, bf16[640,960]{1,0:T(8,128)(2,1)S(1)} %get-tuple-element.34.refs_1_.refs_2_, bf16[4,960,1280]{2,1,0:T(8,128)(2,1)S(1)} %get-tuple-element.36.refs_2_), custom_call_target="tpu_custom_call", output_to_operand_aliasing={{2}: (2, {})} | custom-call | flops 1000 | bytes 1000 | tf_op jit(solution)/shard_map/pallas_call | solution.py:51
  14.4 0.1 collective-permute-start.3
  14.5 0.4 collective-permute-start.4
  14.9 2.2 %shard_map.49 = (f32[512,640]{1,0:T(8,128)S(1)}, f32[512,640]{1,0:T(8,128)S(1)}, bf16[4,960,1280]{2,1,0:T(8,128)(2,1)S(1)}) custom-call(s32[4]{0:T(128)S(1)} %pad_add_fusion.refs_0_.refs_1_, bf16[640,960]{1,0:T(8,128)(2,1)S(1)} %get-tuple-element.34.refs_1_.refs_2_, bf16[4,960,1280]{2,1,0:T(8,128)(2,1)S(1)} %get-tuple-element.37.refs_2_), custom_call_target="tpu_custom_call", output_to_operand_aliasing={{2}: (2, {})} | custom-call | flops 1000 | bytes 1000 | tf_op jit(solution)/shard_map/pallas_call | solution.py:51
  17.2 0.6 shard_map.50.refs_0_
  17.8 2.6 %collective-permute-start.5 = (bf16[520,640]{1,0:T(8,128)(2,1)S(1)}, bf16[520,640]{1,0:T(8,128)(2,1)S(1)}, u32[]{:S(2)}, u32[]{:S(2)}) collective-permute-start(bf16[520,640]{1,0:T(8,128)(2,1)S(1)} %shard_map.50.refs_0_), channel_id=1, source_target_pairs={{0,2},{1,3},{2,0},{3,1},{4,6},{5,7},{6,4},{7,5},{8,10},{9,11},{10,... | collective-permute-start | bytes 1996808 | tf_op jit(solution)/shard_map/ppermute | solution.py:274
  20.4 0.6 shard_map.51.refs_0_
  21.0 1.6 %collective-permute-start.6 = (bf16[520,640]{1,0:T(8,128)(2,1)S(1)}, bf16[520,640]{1,0:T(8,128)(2,1)S(1)}, u32[]{:S(2)}, u32[]{:S(2)}) collective-permute-start(bf16[520,640]{1,0:T(8,128)(2,1)S(1)} %shard_map.51.refs_0_), channel_id=1, source_target_pairs={{0,4},{4,0},{8,12},{12,8},{16,20},{20,16},{24,28},{28,24},{1,5},{5... | collective-permute-start | bytes 1996808 | tf_op jit(solution)/shard_map/ppermute | solution.py:274
  22.6 3.5 %shard_map.52.refs_2_ = f32[512,640]{1,0:T(8,128)S(1)} custom-call(bf16[520,640]{1,0:T(8,128)(2,1)S(1)} %shard_map.51.refs_0_, s32[4]{0:T(128)S(1)} %pad_add_fusion.refs_0_.refs_1_, bf16[640,960]{1,0:T(8,128)(2,1)S(1)} %get-tuple-element.34.refs_1_.refs_2_, bf16[4,960,640]{2,1,0:T(8,128)(2,1)S(1)} %bitcast.11), custom_call_target="tpu_custom_call" | custom-call | flops 1000 | bytes 1000 | tf_op jit(solution)/shard_map/pallas_call | solution.py:51
  26.1 0.0 collective-permute-done.2.refs_3_
  26.1 1.0 %shard_map.53 = (f32[128,640]{1,0:T(8,128)S(1)}, bf16[136,640]{1,0:T(8,128)(2,1)S(1)}, bf16[136,640]{1,0:T(8,128)(2,1)S(1)}, bf16[136,640]{1,0:T(8,128)(2,1)S(1)}) custom-call(bf16[520,640]{1,0:T(8,128)(2,1)S(1)} %shard_map.51.refs_0_, s32[4]{0:T(128)S(1)} %pad_add_fusion.refs_0_.refs_1_, f32[512,640]{1,0:T(8,128)S(1)} %shard_map.52.refs_2_, ...), custom_call_target="tpu_custom_call" | custom-call | flops 1000 | bytes 1000 | tf_op jit(solution)/shard_map/pallas_call | solution.py:51
  27.1 2.6 %collective-permute-start.7 = (bf16[136,640]{1,0:T(8,128)(2,1)S(1)}, bf16[136,640]{1,0:T(8,128)(2,1)S(1)}, u32[]{:S(2)}, u32[]{:S(2)}) collective-permute-start(bf16[136,640]{1,0:T(8,128)(2,1)S(1)} %get-tuple-element.50), channel_id=1, source_target_pairs={{0,16},{4,20},{8,24},{12,28},{16,0},{20,4},{24,8},{28,12},{1,17},{... | collective-permute-start | bytes 522248 | tf_op jit(solution)/shard_map/ppermute | solution.py:274
  29.7 1.6 %collective-permute-start.8 = (bf16[136,640]{1,0:T(8,128)(2,1)S(1)}, bf16[136,640]{1,0:T(8,128)(2,1)S(1)}, u32[]{:S(2)}, u32[]{:S(2)}) collective-permute-start(bf16[136,640]{1,0:T(8,128)(2,1)S(1)} %get-tuple-element.51), channel_id=1, source_target_pairs={{0,8},{4,12},{8,0},{12,4},{16,24},{20,28},{24,16},{28,20},{1,9},{5... | collective-permute-start | bytes 522248 | tf_op jit(solution)/shard_map/ppermute | solution.py:274
  31.3 0.2 collective-permute-start.9
  31.6 3.6 %shard_map.54 = (f32[512,640]{1,0:T(8,128)S(1)}, f32[512,640]{1,0:T(8,128)S(1)}) custom-call(f32[128,640]{1,0:T(8,128)S(1)} %get-tuple-element.44.refs_0_.refs_2_, s32[4]{0:T(128)S(1)} %pad_add_fusion.refs_0_.refs_1_, bf16[640,960]{1,0:T(8,128)(2,1)S(1)} %get-tuple-element.34.refs_1_.refs_2_, bf16[4,960,640]{2,1,0:T(8,128)(2,1)S(1)} %bitcast.11, ...), custom_call_target="tpu_custom_call" | custom-call | flops 1000 | bytes 1000 | tf_op jit(solution)/shard_map/pallas_call | solution.py:51
  35.2 0.7 %collective-permute-done.5.refs_2_.refs_3_ = bf16[520,640]{1,0:T(8,128)(2,1)S(1)} collective-permute-done((bf16[520,640]{1,0:T(8,128)(2,1)S(1)}, bf16[520,640]{1,0:T(8,128)(2,1)S(1)}, u32[]{:S(2)}, u32[]{:S(2)}) %collective-permute-start.5) | collective-permute-done | bytes 665632 | tf_op jit(solution)/shard_map/ppermute | solution.py:274
  35.9 1.1 %shard_map.55.refs_0_ = bf16[264,640]{1,0:T(8,128)(2,1)S(1)} custom-call(s32[4]{0:T(128)S(1)} %pad_add_fusion.refs_0_.refs_1_, f32[512,640]{1,0:T(8,128)S(1)} %get-tuple-element.47.refs_1_.refs_2_, bf16[520,640]{1,0:T(8,128)(2,1)S(1)} %collective-permute-done.5.refs_2_.refs_3_), custom_call_target="tpu_custom_call" | custom-call | flops 1000 | bytes 1000 | tf_op jit(solution)/shard_map/pallas_call | solution.py:51
  37.0 1.9 %collective-permute-start.10 = (bf16[264,640]{1,0:T(8,128)(2,1)S(1)}, bf16[264,640]{1,0:T(8,128)(2,1)S(1)}, u32[]{:S(2)}, u32[]{:S(2)}) collective-permute-start(bf16[264,640]{1,0:T(8,128)(2,1)S(1)} %shard_map.55.refs_0_), channel_id=1, source_target_pairs={{0,4},{4,0},{8,12},{12,8},{16,20},{20,16},{24,28},{28,24},{1,5},{5... | collective-permute-start | bytes 1013768 | tf_op jit(solution)/shard_map/ppermute | solution.py:274
  38.9 1.1 %shard_map.56.refs_0_ = bf16[264,640]{1,0:T(8,128)(2,1)S(1)} custom-call(bf16[264,640]{1,0:T(8,128)(2,1)S(1)} %shard_map.55.refs_0_, s32[4]{0:T(128)S(1)} %pad_add_fusion.refs_0_.refs_1_, f32[512,640]{1,0:T(8,128)S(1)} %get-tuple-element.48.refs_2_.refs_4_, bf16[520,640]{1,0:T(8,128)(2,1)S(1)} %collective-permute-done.6.refs_3_.refs_5_), custom_call_target="tpu_custom_call" | custom-call | flops 1000 | bytes 1000 | tf_op jit(solution)/shard_map/pallas_call | solution.py:51
  39.9 1.5 %collective-permute-start.11 = (bf16[264,640]{1,0:T(8,128)(2,1)S(1)}, bf16[264,640]{1,0:T(8,128)(2,1)S(1)}, u32[]{:S(2)}, u32[]{:S(2)}) collective-permute-start(bf16[264,640]{1,0:T(8,128)(2,1)S(1)} %shard_map.56.refs_0_), channel_id=1, source_target_pairs={{0,2},{1,3},{2,0},{3,1},{4,6},{5,7},{6,4},{7,5},{8,10},{9,11},{10,... | collective-permute-start | bytes 1013768 | tf_op jit(solution)/shard_map/ppermute | solution.py:274
  41.5 0.9 %shard_map.57 = (f32[256,640]{1,0:T(8,128)S(1)}, f32[256,640]{1,0:T(8,128)S(1)}) custom-call(bf16[264,640]{1,0:T(8,128)(2,1)S(1)} %shard_map.56.refs_0_, s32[4]{0:T(128)S(1)} %pad_add_fusion.refs_0_.refs_1_, f32[512,640]{1,0:T(8,128)S(1)} %get-tuple-element.47.refs_1_.refs_2_, bf16[520,640]{1,0:T(8,128)(2,1)S(1)} %collective-permute-done.5.refs_2_.refs_3_, ...), custom_call_target="tpu_custom_call" | custom-call | flops 1000 | bytes 1000 | tf_op jit(solution)/shard_map/pallas_call | solution.py:51
  42.4 0.5 collective-permute-done.9.refs_5_
  42.9 0.9 %shard_map.58 = (f32[64,640]{1,0:T(8,128)S(1)}, bf16[72,640]{1,0:T(8,128)(2,1)S(1)}) custom-call(f32[256,640]{1,0:T(8,128)S(1)} %get-tuple-element.49.refs_0_.refs_2_, s32[4]{0:T(128)S(1)} %pad_add_fusion.refs_0_.refs_1_, f32[128,640]{1,0:T(8,128)S(1)} %get-tuple-element.44.refs_0_.refs_2_, bf16[136,640]{1,0:T(8,128)(2,1)S(1)} %collective-permute-done.7.refs_3_, ...), custom_call_target="tpu_custom_call" | custom-call | flops 34359738368 | bytes 1000 | tf_op jit(solution)/shard_map/pallas_call | solution.py:51
  43.8 0.0 copy-start.1
  43.8 0.0 copy-start.2
  43.8 0.5 collective-permute-start.12
  44.4 4.8 %collective-permute-done.11.refs_5_ = bf16[264,640]{1,0:T(8,128)(2,1)S(1)} collective-permute-done((bf16[264,640]{1,0:T(8,128)(2,1)S(1)}, bf16[264,640]{1,0:T(8,128)(2,1)S(1)}, u32[]{:S(2)}, u32[]{:S(2)}) %collective-permute-start.11) | collective-permute-done | bytes 337952 | tf_op jit(solution)/shard_map/ppermute | solution.py:274
  49.2 1.2 %shard_map.59 = (bf16[136,640]{1,0:T(8,128)(2,1)S(1)}, bf16[136,640]{1,0:T(8,128)(2,1)S(1)}, bf16[136,640]{1,0:T(8,128)(2,1)S(1)}) custom-call(bf16[72,640]{1,0:T(8,128)(2,1)S(1)} %get-tuple-element.53.refs_0_, s32[4]{0:T(128)S(1)} %pad_add_fusion.refs_0_.refs_1_, f32[256,640]{1,0:T(8,128)S(1)} %get-tuple-element.49.refs_0_.refs_2_, ...), custom_call_target="tpu_custom_call" | custom-call | flops 1000 | bytes 1000 | tf_op jit(solution)/shard_map/pallas_call | solution.py:51
  50.4 2.7 %collective-permute-start.13 = (bf16[136,640]{1,0:T(8,128)(2,1)S(1)}, bf16[136,640]{1,0:T(8,128)(2,1)S(1)}, u32[]{:S(2)}, u32[]{:S(2)}) collective-permute-start(bf16[136,640]{1,0:T(8,128)(2,1)S(1)} %get-tuple-element.55.refs_0_), channel_id=1, source_target_pairs={{0,16},{4,20},{8,24},{12,28},{16,0},{20,4},{24,8},{28,12},{1,17},{... | collective-permute-start | bytes 522248 | tf_op jit(solution)/shard_map/ppermute | solution.py:274
  53.1 1.6 %collective-permute-start.14 = (bf16[136,640]{1,0:T(8,128)(2,1)S(1)}, bf16[136,640]{1,0:T(8,128)(2,1)S(1)}, u32[]{:S(2)}, u32[]{:S(2)}) collective-permute-start(bf16[136,640]{1,0:T(8,128)(2,1)S(1)} %get-tuple-element.59), channel_id=1, source_target_pairs={{0,8},{4,12},{8,0},{12,4},{16,24},{20,28},{24,16},{28,20},{1,9},{5... | collective-permute-start | bytes 522248 | tf_op jit(solution)/shard_map/ppermute | solution.py:274
  54.7 0.2 collective-permute-start.15
  54.9 0.6 shard_map.60
  55.5 1.5 %collective-permute-start.16 = (bf16[40,640]{1,0:T(8,128)(2,1)S(1)}, bf16[40,640]{1,0:T(8,128)(2,1)S(1)}, u32[]{:S(2)}, u32[]{:S(2)}) collective-permute-start(bf16[40,640]{1,0:T(8,128)(2,1)S(1)} %get-tuple-element.62), channel_id=1, source_target_pairs={{0,2},{1,3},{2,0},{3,1},{4,6},{5,7},{6,4},{7,5},{8,10},{9,11},{10,... | collective-permute-start | bytes 153608 | tf_op jit(solution)/shard_map/ppermute | solution.py:274
  57.1 0.1 dynamic-slice_bitcast_fusion
  57.1 0.1 copy.8.refs_6_
  57.2 0.1 dynamic_slice.7.refs_8_
  57.3 0.7 %shard_map.61 = (f32[128,640]{1,0:T(8,128)S(1)}, f32[2,80,640]{2,1,0:T(8,128)S(1)}) custom-call(f32[32,640]{1,0:T(8,128)S(1)} %get-tuple-element.57.refs_0_.refs_1_, s32[4]{0:T(128)S(1)} %pad_add_fusion.refs_0_.refs_1_, f32[256,640]{1,0:T(8,128)S(1)} %get-tuple-element.49.refs_0_.refs_2_, bf16[264,640]{1,0:T(8,128)(2,1)S(1)} %collective-permute-done.10.refs_3_, ...), custom_call_target="tpu_custom_call" | custom-call | flops 1000 | bytes 1000 | tf_op jit(solution)/shard_map/pallas_call | solution.py:51
  58.1 4.9 %collective-permute-done.13.refs_1_ = bf16[136,640]{1,0:T(8,128)(2,1)S(1)} collective-permute-done((bf16[136,640]{1,0:T(8,128)(2,1)S(1)}, bf16[136,640]{1,0:T(8,128)(2,1)S(1)}, u32[]{:S(2)}, u32[]{:S(2)}) %collective-permute-start.13) | collective-permute-done | bytes 174112 | tf_op jit(solution)/shard_map/ppermute | solution.py:274
  63.0 1.9 %collective-permute-done.15.refs_3_ = bf16[136,640]{1,0:T(8,128)(2,1)S(1)} collective-permute-done((bf16[136,640]{1,0:T(8,128)(2,1)S(1)}, bf16[136,640]{1,0:T(8,128)(2,1)S(1)}, u32[]{:S(2)}, u32[]{:S(2)}) %collective-permute-start.15) | collective-permute-done | bytes 174112 | tf_op jit(solution)/shard_map/ppermute | solution.py:274
  64.8 0.3 shard_map.62.refs_0_
  65.2 0.7 %shard_map.63 = bf16[2,80,640]{2,1,0:T(8,128)(2,1)} custom-call(bf16[128,640]{1,0:T(8,128)(2,1)S(1)} %shard_map.62.refs_0_, f32[32,640]{1,0:T(8,128)S(1)} %get-tuple-element.57.refs_0_.refs_1_, bf16[40,640]{1,0:T(8,128)(2,1)S(1)} %collective-permute-done.16.refs_2_, f32[2,80,640]{2,1,0:T(8,128)S(1)} %get-tuple-element.61.refs_4_.refs_3_), custom_call_target="tpu_custom_call" | custom-call | flops 1000 | bytes 1000 | tf_op jit(solution)/shard_map/pallas_call | solution.py:51
  (20 shorter events, 0.0 us)
Async XLA Ops:
  0.1 1.3 %copy-start = (bf16[80,12,640]{2,0,1:T(8,128)(2,1)S(1)}, bf16[80,12,640]{2,0,1:T(8,128)(2,1)}, u32[]{:S(2)}) copy-start(bf16[80,12,640]{2,0,1:T(8,128)(2,1)} %param.4) | copy-start | bytes 3686404
  9.0 8.2 %collective-permute-start = (f32[512,640]{1,0:T(8,128)S(1)}, f32[512,640]{1,0:T(8,128)S(1)}, u32[]{:S(2)}, u32[]{:S(2)}) collective-permute-start(f32[512,640]{1,0:T(8,128)S(1)} %get-tuple-element.39), channel_id=1, source_target_pairs={{0,1},{1,0},{2,3},{3,2},{4,5},{5,4},{6,7},{7,6},{8,9},{9,8},{10,11... | collective-permute-start | bytes 3932168 | tf_op jit(solution)/shard_map/ppermute | solution.py:274
  11.6 8.8 %collective-permute-start.1 = (f32[512,640]{1,0:T(8,128)S(1)}, f32[512,640]{1,0:T(8,128)S(1)}, u32[]{:S(2)}, u32[]{:S(2)}) collective-permute-start(f32[512,640]{1,0:T(8,128)S(1)} %get-tuple-element.41), channel_id=1, source_target_pairs={{0,1},{1,0},{2,3},{3,2},{4,5},{5,4},{6,7},{7,6},{8,9},{9,8},{10,11... | collective-permute-start | bytes 3932168 | tf_op jit(solution)/shard_map/ppermute | solution.py:274
  11.7 14.4 %collective-permute-start.2 = (f32[512,640]{1,0:T(8,128)S(1)}, f32[512,640]{1,0:T(8,128)S(1)}, u32[]{:S(2)}, u32[]{:S(2)}) collective-permute-start(f32[512,640]{1,0:T(8,128)S(1)} %get-tuple-element.43), channel_id=1, source_target_pairs={{0,1},{1,0},{2,3},{3,2},{4,5},{5,4},{6,7},{7,6},{8,9},{9,8},{10,11... | collective-permute-start | bytes 3932168 | tf_op jit(solution)/shard_map/ppermute | solution.py:274
  12.2 10.4 %slice-start = ((s8[4915200]{0:T(1024)(128)(4,1)}), s8[4194304]{0:T(1024)(128)(4,1)S(1)}, s32[]{:S(2)}) async-start(s8[4915200]{0:T(1024)(128)(4,1)} %bitcast.10), calls=%async_computation | async-start | bytes 8388608
  14.4 15.4 %collective-permute-start.3 = (f32[512,640]{1,0:T(8,128)S(1)}, f32[512,640]{1,0:T(8,128)S(1)}, u32[]{:S(2)}, u32[]{:S(2)}) collective-permute-start(f32[512,640]{1,0:T(8,128)S(1)} %get-tuple-element.45), channel_id=1, source_target_pairs={{0,1},{1,0},{2,3},{3,2},{4,5},{5,4},{6,7},{7,6},{8,9},{9,8},{10,11... | collective-permute-start | bytes 3932168 | tf_op jit(solution)/shard_map/ppermute | solution.py:274
  14.5 16.8 %collective-permute-start.4 = (f32[512,640]{1,0:T(8,128)S(1)}, f32[512,640]{1,0:T(8,128)S(1)}, u32[]{:S(2)}, u32[]{:S(2)}) collective-permute-start(f32[512,640]{1,0:T(8,128)S(1)} %get-tuple-element.46), channel_id=1, source_target_pairs={{0,1},{1,0},{2,3},{3,2},{4,5},{5,4},{6,7},{7,6},{8,9},{9,8},{10,11... | collective-permute-start | bytes 3932168 | tf_op jit(solution)/shard_map/ppermute | solution.py:274
  14.9 7.7 %slice-start.1 = ((s8[4915200]{0:T(1024)(128)(4,1)}), s8[720896]{0:T(1024)(128)(4,1)S(1)}, s32[]{:S(2)}) async-start(s8[4915200]{0:T(1024)(128)(4,1)} %bitcast.10), calls=%async_computation.1 | async-start | bytes 1441792
  17.8 18.2 %collective-permute-start.5 = (bf16[520,640]{1,0:T(8,128)(2,1)S(1)}, bf16[520,640]{1,0:T(8,128)(2,1)S(1)}, u32[]{:S(2)}, u32[]{:S(2)}) collective-permute-start(bf16[520,640]{1,0:T(8,128)(2,1)S(1)} %shard_map.50.refs_0_), channel_id=1, source_target_pairs={{0,2},{1,3},{2,0},{3,1},{4,6},{5,7},{6,4},{7,5},{8,10},{9,11},{10,... | collective-permute-start | bytes 1996808 | tf_op jit(solution)/shard_map/ppermute | solution.py:274
  21.0 17.9 %collective-permute-start.6 = (bf16[520,640]{1,0:T(8,128)(2,1)S(1)}, bf16[520,640]{1,0:T(8,128)(2,1)S(1)}, u32[]{:S(2)}, u32[]{:S(2)}) collective-permute-start(bf16[520,640]{1,0:T(8,128)(2,1)S(1)} %shard_map.51.refs_0_), channel_id=1, source_target_pairs={{0,4},{4,0},{8,12},{12,8},{16,20},{20,16},{24,28},{28,24},{1,5},{5... | collective-permute-start | bytes 1996808 | tf_op jit(solution)/shard_map/ppermute | solution.py:274
  27.1 15.3 %collective-permute-start.7 = (bf16[136,640]{1,0:T(8,128)(2,1)S(1)}, bf16[136,640]{1,0:T(8,128)(2,1)S(1)}, u32[]{:S(2)}, u32[]{:S(2)}) collective-permute-start(bf16[136,640]{1,0:T(8,128)(2,1)S(1)} %get-tuple-element.50), channel_id=1, source_target_pairs={{0,16},{4,20},{8,24},{12,28},{16,0},{20,4},{24,8},{28,12},{1,17},{... | collective-permute-start | bytes 522248 | tf_op jit(solution)/shard_map/ppermute | solution.py:274
  29.7 12.7 %collective-permute-start.8 = (bf16[136,640]{1,0:T(8,128)(2,1)S(1)}, bf16[136,640]{1,0:T(8,128)(2,1)S(1)}, u32[]{:S(2)}, u32[]{:S(2)}) collective-permute-start(bf16[136,640]{1,0:T(8,128)(2,1)S(1)} %get-tuple-element.51), channel_id=1, source_target_pairs={{0,8},{4,12},{8,0},{12,4},{16,24},{20,28},{24,16},{28,20},{1,9},{5... | collective-permute-start | bytes 522248 | tf_op jit(solution)/shard_map/ppermute | solution.py:274
  31.3 11.6 %collective-permute-start.9 = (bf16[136,640]{1,0:T(8,128)(2,1)S(1)}, bf16[136,640]{1,0:T(8,128)(2,1)S(1)}, u32[]{:S(2)}, u32[]{:S(2)}) collective-permute-start(bf16[136,640]{1,0:T(8,128)(2,1)S(1)} %get-tuple-element.52), channel_id=1, source_target_pairs={{0,24},{4,28},{8,16},{12,20},{16,8},{20,12},{24,0},{28,4},{1,25},{... | collective-permute-start | bytes 522248 | tf_op jit(solution)/shard_map/ppermute | solution.py:274
  37.0 12.2 %collective-permute-start.10 = (bf16[264,640]{1,0:T(8,128)(2,1)S(1)}, bf16[264,640]{1,0:T(8,128)(2,1)S(1)}, u32[]{:S(2)}, u32[]{:S(2)}) collective-permute-start(bf16[264,640]{1,0:T(8,128)(2,1)S(1)} %shard_map.55.refs_0_), channel_id=1, source_target_pairs={{0,4},{4,0},{8,12},{12,8},{16,20},{20,16},{24,28},{28,24},{1,5},{5... | collective-permute-start | bytes 1013768 | tf_op jit(solution)/shard_map/ppermute | solution.py:274
  39.9 9.3 %collective-permute-start.11 = (bf16[264,640]{1,0:T(8,128)(2,1)S(1)}, bf16[264,640]{1,0:T(8,128)(2,1)S(1)}, u32[]{:S(2)}, u32[]{:S(2)}) collective-permute-start(bf16[264,640]{1,0:T(8,128)(2,1)S(1)} %shard_map.56.refs_0_), channel_id=1, source_target_pairs={{0,2},{1,3},{2,0},{3,1},{4,6},{5,7},{6,4},{7,5},{8,10},{9,11},{10,... | collective-permute-start | bytes 1013768 | tf_op jit(solution)/shard_map/ppermute | solution.py:274
  43.8 13.2 %copy-start.1 = (f32[640]{0:T(1024)S(1)}, f32[640]{0:T(1024)}, u32[]{:S(2)}) copy-start(f32[640]{0:T(1024)} %param.6) | copy-start | bytes 7684
  43.8 13.4 %copy-start.2 = (f32[8]{0:T(128)S(1)}, f32[8]{0:T(128)}, u32[]{:S(2)}) copy-start(f32[8]{0:T(128)} %param.7) | copy-start | bytes 100
  43.8 11.0 %collective-permute-start.12 = (bf16[72,640]{1,0:T(8,128)(2,1)S(1)}, bf16[72,640]{1,0:T(8,128)(2,1)S(1)}, u32[]{:S(2)}, u32[]{:S(2)}) collective-permute-start(bf16[72,640]{1,0:T(8,128)(2,1)S(1)} %get-tuple-element.53.refs_0_), channel_id=1, source_target_pairs={{0,4},{4,0},{8,12},{12,8},{16,20},{20,16},{24,28},{28,24},{1,5},{5... | collective-permute-start | bytes 276488 | tf_op jit(solution)/shard_map/ppermute | solution.py:274
  50.4 12.5 %collective-permute-start.13 = (bf16[136,640]{1,0:T(8,128)(2,1)S(1)}, bf16[136,640]{1,0:T(8,128)(2,1)S(1)}, u32[]{:S(2)}, u32[]{:S(2)}) collective-permute-start(bf16[136,640]{1,0:T(8,128)(2,1)S(1)} %get-tuple-element.55.refs_0_), channel_id=1, source_target_pairs={{0,16},{4,20},{8,24},{12,28},{16,0},{20,4},{24,8},{28,12},{1,17},{... | collective-permute-start | bytes 522248 | tf_op jit(solution)/shard_map/ppermute | solution.py:274
  53.1 9.9 %collective-permute-start.14 = (bf16[136,640]{1,0:T(8,128)(2,1)S(1)}, bf16[136,640]{1,0:T(8,128)(2,1)S(1)}, u32[]{:S(2)}, u32[]{:S(2)}) collective-permute-start(bf16[136,640]{1,0:T(8,128)(2,1)S(1)} %get-tuple-element.59), channel_id=1, source_target_pairs={{0,8},{4,12},{8,0},{12,4},{16,24},{20,28},{24,16},{28,20},{1,9},{5... | collective-permute-start | bytes 522248 | tf_op jit(solution)/shard_map/ppermute | solution.py:274
  54.7 10.2 %collective-permute-start.15 = (bf16[136,640]{1,0:T(8,128)(2,1)S(1)}, bf16[136,640]{1,0:T(8,128)(2,1)S(1)}, u32[]{:S(2)}, u32[]{:S(2)}) collective-permute-start(bf16[136,640]{1,0:T(8,128)(2,1)S(1)} %get-tuple-element.60), channel_id=1, source_target_pairs={{0,24},{4,28},{8,16},{12,20},{16,8},{20,12},{24,0},{28,4},{1,25},{... | collective-permute-start | bytes 522248 | tf_op jit(solution)/shard_map/ppermute | solution.py:274
  55.5 9.7 %collective-permute-start.16 = (bf16[40,640]{1,0:T(8,128)(2,1)S(1)}, bf16[40,640]{1,0:T(8,128)(2,1)S(1)}, u32[]{:S(2)}, u32[]{:S(2)}) collective-permute-start(bf16[40,640]{1,0:T(8,128)(2,1)S(1)} %get-tuple-element.62), channel_id=1, source_target_pairs={{0,2},{1,3},{2,0},{3,1},{4,6},{5,7},{6,4},{7,5},{8,10},{9,11},{10,... | collective-permute-start | bytes 153608 | tf_op jit(solution)/shard_map/ppermute | solution.py:274
